TPU v7x, 256 devices: a whole 4x4x8 slice. The times are simulated.
256 devices in a mesh: row: 16 (over x, y_hi, core), col: 16 (over z, y_lo).
Axes of the slice: x: 4, y: 4 (y_hi: 2, y_lo: 2; y = y_hi * 2 + y_lo), z: 8, core: 2. Of those that a mesh axis runs over, the one named last changes fastest.
Arguments:
- object_field: float32 [2, 6144, 6144], P(None, 'row', 'col'), may hold values from -6 to 6
- probe: float32 [2, 128, 128], replicated, may hold values from -6 to 6
- amplitudes: float32 [16, 16, 12, 128, 128], P('row', 'col'), may hold values from 0.2 to 4
- offsets: int32 [16, 16, 12, 2], P('row', 'col'), may hold values from -64 to 319
- counts: int32 [16, 16], P('row', 'col'), may hold values from 1 to 12, as said below
Outputs:
- updated_object: float32 [2, 6144, 6144], P(None, 'row', 'col')
Inputs may be any that keep to these rules, and one draw needn't show every extreme that they name: `counts`: some tile has exactly 12 live positions in every draw.
All inputs are finite; a program needn't handle non-finite values.
Results may differ from a plain program's by a relative error of at most 0.0001.
Values sent between devices are 32-bit elements; how exact they have to be, the bound alone decides.
A program may use at most 64 MiB of HBM per device.

v0:
```python
import math

import jax
import jax.numpy as jnp
from jax import lax
from jax.sharding import PartitionSpec as P

ITERS = 2


def passed_along(value, axis, steps):
    count = lax.axis_size(axis)
    leading, last = (max(0, -steps), min(count, count - steps))
    return lax.ppermute(value, axis, [(source, source + steps) for source in range(leading, last)])


def with_halo(block, sides, width):
    for axis, dim in sides:
        count = lax.axis_size(axis)
        forward = [(i, i + 1) for i in range(count - 1)]
        backward = [(target, source) for source, target in forward]
        low = lax.ppermute(
            lax.slice_in_dim(block, block.shape[dim] - width, None, axis=dim), axis, forward
        )
        high = lax.ppermute(lax.slice_in_dim(block, 0, width, axis=dim), axis, backward)
        block = jnp.concatenate([low, block, high], axis=dim)
    return block


def dft_tables(length):
    index = jnp.arange(length, dtype=jnp.int32)
    phase = index[:, None] * index[None, :] % length
    angle = phase.astype(jnp.float32) * (2.0 * math.pi / length)
    scale = 1.0 / math.sqrt(length)
    return (jnp.cos(angle) * scale, jnp.sin(angle) * scale)


def left_mul(table, batch):
    return jnp.einsum("km,pmn->pkn", table, batch, precision=lax.Precision.HIGHEST)


def right_mul(batch, table):
    return jnp.einsum("pkn,nl->pkl", batch, table, precision=lax.Precision.HIGHEST)


def transform(real, imag, cosine, sine_signed):
    mid_r = left_mul(cosine, real) - left_mul(sine_signed, imag)
    mid_i = left_mul(cosine, imag) + left_mul(sine_signed, real)
    out_r = right_mul(mid_r, cosine) - right_mul(mid_i, sine_signed)
    out_i = right_mul(mid_r, sine_signed) + right_mul(mid_i, cosine)
    return (out_r, out_i)


def fold_back(stacked, half, tile):
    tops = stacked[:, :half, :]
    bottoms = stacked[:, half + tile :, :]
    from_below = passed_along(tops, "row", -1)
    from_above = passed_along(bottoms, "row", 1)
    middle = stacked[:, half : half + tile, :]
    middle = middle.at[:, :half, :].add(from_above)
    middle = middle.at[:, tile - half :, :].add(from_below)
    lefts = middle[:, :, :half]
    rights = middle[:, :, half + tile :]
    from_right = passed_along(lefts, "col", -1)
    from_left = passed_along(rights, "col", 1)
    inner = middle[:, :, half : half + tile]
    inner = inner.at[:, :, :half].add(from_left)
    inner = inner.at[:, :, tile - half :].add(from_right)
    return inner


def column_picks(start_cols, length, extent):
    across = jnp.arange(extent, dtype=jnp.int32)
    within = jnp.arange(length, dtype=jnp.int32)
    target = start_cols[:, None, None] + within[None, :, None]
    return (across[None, None, :] == target).astype(jnp.float32)


def place_all(pieces, picks, start_rows, total):
    zero_i = jnp.int32(0)
    spread = jnp.einsum("pcrk,pkx->pcrx", pieces, picks, precision=lax.Precision.HIGHEST)

    def place(slot, acc):
        srow = start_rows[slot]
        old = lax.dynamic_slice(acc, (zero_i, srow, zero_i), spread.shape[1:])
        return lax.dynamic_update_slice(acc, old + spread[slot], (zero_i, srow, zero_i))

    return lax.fori_loop(0, pieces.shape[0], place, total)


def shards(object_field, probe, amplitudes, offsets, counts):
    length = probe.shape[-1]
    half = length // 2
    tile = object_field.shape[1]
    npos = offsets.shape[2]
    extent = tile + 2 * half
    start_rows = offsets[0, 0, :, 0] + half
    start_cols = offsets[0, 0, :, 1] + half
    live = (jnp.arange(npos, dtype=jnp.int32) < counts[0, 0]).astype(jnp.float32)
    measured = amplitudes[0, 0]
    cosine, sine = dft_tables(length)
    picks = column_picks(start_cols, length, extent)
    probe_r = probe[0]
    probe_i = probe[1]
    power = probe_r * probe_r + probe_i * probe_i
    light_pieces = power[None, None] * live[:, None, None, None]
    light_full = place_all(
        light_pieces, picks, start_rows, jnp.zeros((1, extent, extent), jnp.float32)
    )
    light = fold_back(light_full, half, tile)
    zero_i = jnp.int32(0)
    field = object_field
    for step in range(ITERS):
        padded = with_halo(field, (("row", 1), ("col", 2)), half)

        def strip(srow):
            return lax.dynamic_slice(padded, (zero_i, srow, zero_i), (2, length, extent))

        strips = jax.vmap(strip)(start_rows)
        wins = jnp.einsum("pcrx,pkx->pcrk", strips, picks, precision=lax.Precision.HIGHEST)
        exit_r = probe_r[None] * wins[:, 0] - probe_i[None] * wins[:, 1]
        exit_i = probe_r[None] * wins[:, 1] + probe_i[None] * wins[:, 0]
        far_r, far_i = transform(exit_r, exit_i, cosine, -sine)
        ratio = measured / jnp.sqrt(far_r * far_r + far_i * far_i + 0.25) - 1.0
        back_r, back_i = transform(far_r * ratio, far_i * ratio, cosine, sine)
        grad_r = (probe_r[None] * back_r + probe_i[None] * back_i) * live[:, None, None]
        grad_i = (probe_r[None] * back_i - probe_i[None] * back_r) * live[:, None, None]
        grads = jnp.stack([grad_r, grad_i], axis=1)
        update_full = place_all(
            grads, picks, start_rows, jnp.zeros((2, extent, extent), jnp.float32)
        )
        update = fold_back(update_full, half, tile)
        field = field + update / (light + 1.0)
    return field


def solution(mesh):
    placed = (
        P(None, "row", "col"),
        P(),
        P("row", "col", None, None, None),
        P("row", "col", None, None),
        P("row", "col"),
    )
    return jax.shard_map(
        shards, mesh=mesh, in_specs=placed, out_specs=P(None, "row", "col"), check_vma=False
    )
```

profile of v0, /device:TPU:141, one launch (start us, length us, event | category | flops | bytes accessed | tf_op | source)
XLA Modules:
  0.0 593.3 jit_solution(14598793153559826457)
XLA Ops:
  2.4 3.4 fusion.13
  5.9 44.5 %while.52 = (s32[]{:T(128)}, f32[1,512,512]{2,1,0:T(8,128)S(1)}, s32[12]{0:T(128)S(1)}, f32[12,1,128,512]{3,2,1,0:T(8,128)}, s32[]{:T(128)}, /*index=5*/s32[]{:T(128)}, s32[]{:T(128)}) while((s32[]{:T(128)}, f32[1,512,512]{2,1,0:T(8,128)S(1)}, s32[12]{0:T(128)S(1)}, f32[12,1,128,512]{3,2,1,0:T(8,128)}, s32[]{:T(128)}, /*index=5*/s32[]{:T(128)}, ...), condition=%wide.region_3.4_spmd, body=%wide.region_2.3_spmd.sunk | while | flops 65541 | bytes 1310855 | solution.py:88
  51.1 4.5 collective-permute-start.8
  57.9 5.1 collective-permute-start
  72.5 3.2 collective-permute-start.2
  79.0 4.2 collective-permute-start.10
  83.2 2.9 collective-permute-start.11
  86.2 17.1 %collective-permute-done.2 = f32[2,512,64]{2,0,1:T(2,128)S(1)} collective-permute-done((f32[2,512,64]{2,0,1:T(2,128)S(1)}, f32[2,512,64]{2,0,1:T(2,128)S(1)}, u32[]{:S(2)}, u32[]{:S(2)}) %collective-permute-start.2) | collective-permute-done | bytes 262176 | tf_op jit(solution)/shard_map/ppermute | solution.py:22
  104.5 3.7 pad_maximum_fusion
  108.1 8.5 %gather_fusion = f32[12,2,128,512]{3,1,2,0:T(2,128)} fusion(f32[2,512,512]{2,0,1:T(2,128)S(1)} %pad_maximum_fusion, s32[12]{0:T(128)S(1)} %shift-left_bitcast_fusion), kind=kCustom, calls=%fused_computation | custom fusion | bytes 12583056 | tf_op jit(solution)/shard_map/vmap()/gather | solution.py:117
  116.7 7.2 %fusion.2 = f32[12,2,128,128]{3,2,1,0:T(8,128)S(1)} fusion(f32[12,2,128,512]{3,1,2,0:T(2,128)} %gather_fusion, s32[12,128]{1,0:T(8,128)S(1)} %iota_add_fusion), kind=kOutput, calls=%fused_computation.11 | convolution fusion | flops 2416705536 | bytes 7870464 | tf_op jit(solution)/shard_map/pcrx,pkx->pcrk/dot_general | solution.py:120
  150.1 4.7 fusion.9
  155.4 52.3 %while.51 = (s32[]{:T(128)}, f32[2,512,512]{2,0,1:T(2,128)S(1)}, s32[12]{0:T(128)S(1)}, f32[12,2,128,512]{3,2,1,0:T(8,128)}, s32[]{:T(128)}, /*index=5*/s32[]{:T(128)}, s32[]{:T(128)}) while((s32[]{:T(128)}, f32[2,512,512]{2,0,1:T(2,128)S(1)}, s32[12]{0:T(128)S(1)}, f32[12,2,128,512]{3,2,1,0:T(8,128)}, s32[]{:T(128)}, /*index=5*/s32[]{:T(128)}, ...), condition=%wide.region_1.2_spmd, body=%wide.region_0.1_spmd.sunk | while | flops 131077 | bytes 3670151 | solution.py:88
  225.9 4.0 collective-permute-start.6
  234.9 13.0 %collective-permute-done.6 = f32[2,384,64]{2,0,1:T(2,128)S(1)} collective-permute-done((f32[2,384,64]{2,0,1:T(2,128)S(1)}, f32[2,384,64]{2,0,1:T(2,128)S(1)}, u32[]{:S(2)}, u32[]{:S(2)}) %collective-permute-start.6) | collective-permute-done | bytes 196640 | tf_op jit(solution)/shard_map/ppermute | solution.py:14
  248.4 13.5 %scatter-add.44 = f32[2,384,384]{2,0,1:T(2,128)} dynamic-update-slice(f32[2,384,384]{2,0,1:T(2,128)} %slice.459, f32[2,384,64]{2,0,1:T(2,128)S(1)} %slice_add_fusion.3, s32[]{:T(128)} %constant.375.clone.1, s32[]{:T(128)} %constant.375.clone.1, s32[]{:T(128)} %constant.375.clone.1) | dynamic-update-slice | bytes 393220 | tf_op jit(solution)/shard_map/scatter-add | solution.py:67
  263.5 64.5 %scatter-add.45 = f32[2,384,384]{2,0,1:T(2,128)} dynamic-update-slice(f32[2,384,384]{2,0,1:T(2,128)} %scatter-add.44, f32[2,384,64]{2,0,1:T(2,128)S(1)} %slice_add_fusion.2, s32[]{:T(128)} %constant.375.clone.1, s32[]{:T(128)} %constant.375.clone.1, s32[]{:T(128)} %constant.385.clone.1) | dynamic-update-slice | bytes 393220 | tf_op jit(solution)/shard_map/scatter-add | solution.py:68
  332.8 3.1 collective-permute-start.13
  335.9 7.0 %collective-permute-done.13 = f32[2,64,384]{2,0,1:T(2,128)S(1)} collective-permute-done((f32[2,64,384]{2,0,1:T(2,128)S(1)}, f32[2,64,384]{2,0,1:T(2,128)S(1)}, u32[]{:S(2)}, u32[]{:S(2)}) %collective-permute-start.13) | collective-permute-done | bytes 196640 | tf_op jit(solution)/shard_map/ppermute | solution.py:25
  345.5 3.4 collective-permute-start.15
  348.9 21.0 %collective-permute-done.14 = f32[2,512,64]{2,0,1:T(2,128)S(1)} collective-permute-done((f32[2,512,64]{2,0,1:T(2,128)S(1)}, f32[2,512,64]{2,0,1:T(2,128)S(1)}, u32[]{:S(2)}, u32[]{:S(2)}) %collective-permute-start.14) | collective-permute-done | bytes 262176 | tf_op jit(solution)/shard_map/ppermute | solution.py:22
  370.7 8.3 %pad_maximum_fusion.1 = f32[2,512,512]{2,0,1:T(2,128)S(1)} fusion(f32[2,512,64]{2,0,1:T(2,128)} %collective-permute-done.15, f32[2,64,384]{2,0,1:T(2,128)S(1)} %collective-permute-done.13, f32[2,384,384]{2,0,1:T(2,128)} %copy-done.1, f32[2,64,384]{2,0,1:T(2,128)S(1)} %collective-permute-done.12, f32[2,512,64]{2,0,1:T(2,128)} %copy-done.10), kind=kLoop, calls=%fused_computation.20 | loop fusion | flops 2097152 | bytes 4194304 | tf_op jit(solution)/shard_map/concatenate | solution.py:26
  379.0 8.5 %gather_fusion.1 = f32[12,2,128,512]{3,1,2,0:T(2,128)} fusion(f32[2,512,512]{2,0,1:T(2,128)S(1)} %pad_maximum_fusion.1, s32[12]{0:T(128)S(1)} %shift-left_bitcast_fusion), kind=kCustom, calls=%fused_computation.1 | custom fusion | bytes 12583056 | tf_op jit(solution)/shard_map/vmap()/gather | solution.py:117
  387.5 6.8 %fusion = f32[12,2,128,128]{3,2,0,1:T(8,128)S(1)} fusion(f32[12,2,128,512]{3,1,2,0:T(2,128)} %gather_fusion.1, s32[12,128]{1,0:T(8,128)S(1)} %iota_add_fusion), kind=kOutput, calls=%fused_computation.9 | convolution fusion | flops 2416705536 | bytes 7870464 | tf_op jit(solution)/shard_map/pcrx,pkx->pcrk/dot_general | solution.py:120
  420.8 4.7 fusion.7
  426.0 49.5 %while.53 = (s32[]{:T(128)}, f32[2,512,512]{2,0,1:T(2,128)S(1)}, s32[12]{0:T(128)S(1)}, f32[12,2,128,512]{3,2,1,0:T(8,128)}, s32[]{:T(128)}, /*index=5*/s32[]{:T(128)}, s32[]{:T(128)}) while((s32[]{:T(128)}, f32[2,512,512]{2,0,1:T(2,128)S(1)}, s32[12]{0:T(128)S(1)}, f32[12,2,128,512]{3,2,1,0:T(8,128)}, s32[]{:T(128)}, /*index=5*/s32[]{:T(128)}, ...), condition=%wide.region_5.6_spmd, body=%wide.region_4.5_spmd.sunk | while | flops 131077 | bytes 3670151 | solution.py:88
  477.6 3.1 collective-permute-start.17
  481.4 7.6 %collective-permute-done.17 = f32[2,64,512]{2,0,1:T(2,128)S(1)} collective-permute-done((f32[2,64,512]{2,0,1:T(2,128)S(1)}, f32[2,64,512]{2,0,1:T(2,128)S(1)}, u32[]{:S(2)}, u32[]{:S(2)}) %collective-permute-start.17) | collective-permute-done | bytes 262176 | tf_op jit(solution)/shard_map/ppermute | solution.py:14
  493.8 3.2 collective-permute-start.19
  497.0 14.8 %collective-permute-done.18 = f32[2,384,64]{2,0,1:T(2,128)S(1)} collective-permute-done((f32[2,384,64]{2,0,1:T(2,128)S(1)}, f32[2,384,64]{2,0,1:T(2,128)S(1)}, u32[]{:S(2)}, u32[]{:S(2)}) %collective-permute-start.18) | collective-permute-done | bytes 196640 | tf_op jit(solution)/shard_map/ppermute | solution.py:14
  512.3 13.2 %scatter-add.56 = f32[2,384,384]{2,0,1:T(2,128)S(1)} dynamic-update-slice(f32[2,384,384]{2,0,1:T(2,128)S(1)} %slice.475, f32[2,384,64]{2,0,1:T(2,128)S(1)} %slice_add_fusion.1, s32[]{:T(128)} %constant.375.clone.1, s32[]{:T(128)} %constant.375.clone.1, s32[]{:T(128)} %constant.375.clone.1) | dynamic-update-slice | bytes 393220 | tf_op jit(solution)/shard_map/scatter-add | solution.py:67
  527.0 64.2 %scatter-add.59 = f32[2,384,384]{2,0,1:T(2,128)S(1)} dynamic-update-slice(f32[2,384,384]{2,0,1:T(2,128)S(1)} %scatter-add.56, f32[2,384,64]{2,0,1:T(2,128)S(1)} %slice_add_fusion, s32[]{:T(128)} %constant.375.clone.1, s32[]{:T(128)} %constant.375.clone.1, s32[]{:T(128)} %constant.385.clone.1) | dynamic-update-slice | bytes 393220 | tf_op jit(solution)/shard_map/scatter-add | solution.py:68
  (266 shorter events, 195.9 us)
Async XLA Ops:
  5.9 51.8 %copy-start.3 = (f32[2,384,384]{2,1,0:T(8,128)S(1)}, f32[2,384,384]{2,1,0:T(8,128)}, u32[]{:S(2)}) copy-start(f32[2,384,384]{2,1,0:T(8,128)} %param.35) | copy-start | bytes 3538948
  50.3 5.3 copy-start.13
  51.1 15.1 %collective-permute-start.8 = (f32[1,64,512]{2,1,0:T(8,128)}, f32[1,64,512]{2,1,0:T(8,128)}, u32[]{:S(2)}, u32[]{:S(2)}) collective-permute-start(f32[1,64,512]{2,1,0:T(8,128)} %get-tuple-element.438), channel_id=1, source_target_pairs={{0,16},{16,32},{32,48},{48,64},{64,80},{80,96},{96,112},{112,128},... | collective-permute-start | bytes 393224 | tf_op jit(solution)/shard_map/ppermute | solution.py:14
  55.6 10.5 %copy-start.11 = (f32[2,128,128]{2,1,0:T(8,128)S(1)}, f32[2,128,128]{2,1,0:T(8,128)}, u32[]{:S(2)}) copy-start(f32[2,128,128]{2,1,0:T(8,128)} %param.36) | copy-start | bytes 393220
  55.6 10.5 %copy-start.12 = (s32[1,1,12,2]{2,3,1,0:T(2,128)S(1)}, s32[1,1,12,2]{2,3,1,0:T(2,128)}, u32[]{:S(2)}) copy-start(s32[1,1,12,2]{2,3,1,0:T(2,128)} %param.38) | copy-start | bytes 292
  55.6 22.2 %collective-permute-start.9 = (f32[1,64,512]{2,1,0:T(8,128)}, f32[1,64,512]{2,1,0:T(8,128)S(1)}, u32[]{:S(2)}, u32[]{:S(2)}) collective-permute-start(f32[1,64,512]{2,1,0:T(8,128)} %get-tuple-element.437), channel_id=1, source_target_pairs={{16,0},{32,16},{48,32},{64,48},{80,64},{96,80},{112,96},{128,112},... | collective-permute-start | bytes 393224 | tf_op jit(solution)/shard_map/ppermute | solution.py:14
  57.9 9.8 %collective-permute-start = (f32[2,64,384]{2,0,1:T(2,128)S(1)}, f32[2,64,384]{2,0,1:T(2,128)S(1)}, u32[]{:S(2)}, u32[]{:S(2)}) collective-permute-start(f32[2,64,384]{2,0,1:T(2,128)S(1)} %copy.116), channel_id=1, source_target_pairs={{0,16},{16,32},{32,48},{48,64},{64,80},{80,96},{96,112},{112,128},... | collective-permute-start | bytes 589832 | tf_op jit(solution)/shard_map/ppermute | solution.py:22
  63.2 8.5 %collective-permute-start.1 = (f32[2,64,384]{2,0,1:T(2,128)S(1)}, f32[2,64,384]{2,0,1:T(2,128)S(1)}, u32[]{:S(2)}, u32[]{:S(2)}) collective-permute-start(f32[2,64,384]{2,0,1:T(2,128)S(1)} %copy.117), channel_id=1, source_target_pairs={{16,0},{32,16},{48,32},{64,48},{80,64},{96,80},{112,96},{128,112},... | collective-permute-start | bytes 589832 | tf_op jit(solution)/shard_map/ppermute | solution.py:25
  68.8 9.0 %copy-start.5 = (f32[1,384,512]{2,1,0:T(8,128)S(1)}, f32[1,384,512]{2,1,0:T(8,128)}, u32[]{:S(2)}) copy-start(f32[1,384,512]{2,1,0:T(8,128)} %add_dynamic-update-slice_fusion.2) | copy-start | bytes 2359300
  72.5 30.7 %collective-permute-start.2 = (f32[2,512,64]{2,0,1:T(2,128)S(1)}, f32[2,512,64]{2,0,1:T(2,128)S(1)}, u32[]{:S(2)}, u32[]{:S(2)}) collective-permute-start(f32[2,512,64]{2,0,1:T(2,128)S(1)} %get-tuple-element.431), channel_id=1, source_target_pairs={{0,1},{1,2},{2,3},{3,4},{4,5},{5,6},{6,7},{7,8},{8,9},{9,10},{10,1... | collective-permute-start | bytes 786440 | tf_op jit(solution)/shard_map/ppermute | solution.py:22
  75.8 28.7 %collective-permute-start.3 = (f32[2,512,64]{2,0,1:T(2,128)S(1)}, f32[2,512,64]{2,0,1:T(2,128)S(1)}, u32[]{:S(2)}, u32[]{:S(2)}) collective-permute-start(f32[2,512,64]{2,0,1:T(2,128)S(1)} %get-tuple-element.432), channel_id=1, source_target_pairs={{1,0},{2,1},{3,2},{4,3},{5,4},{6,5},{7,6},{8,7},{9,8},{10,9},{11,1... | collective-permute-start | bytes 786440 | tf_op jit(solution)/shard_map/ppermute | solution.py:25
  77.9 25.4 %copy-start.6 = (f32[1,384,512]{2,1,0:T(8,128)}, f32[1,384,512]{2,1,0:T(8,128)S(1)}, u32[]{:S(2)}) copy-start(f32[1,384,512]{2,1,0:T(8,128)S(1)} %fusion.40) | copy-start | bytes 2359300
  79.0 132.0 %collective-permute-start.10 = (f32[1,384,64]{2,1,0:T(8,128)S(1)}, f32[1,384,64]{2,1,0:T(8,128)}, u32[]{:S(2)}, u32[]{:S(2)}) collective-permute-start(f32[1,384,64]{2,1,0:T(8,128)S(1)} %get-tuple-element.440), channel_id=1, source_target_pairs={{0,1},{1,2},{2,3},{3,4},{4,5},{5,6},{6,7},{7,8},{8,9},{9,10},{10,1... | collective-permute-start | bytes 294920 | tf_op jit(solution)/shard_map/ppermute | solution.py:14
  83.2 132.7 %collective-permute-start.11 = (f32[1,384,64]{2,1,0:T(8,128)S(1)}, f32[1,384,64]{2,1,0:T(8,128)}, u32[]{:S(2)}, u32[]{:S(2)}) collective-permute-start(f32[1,384,64]{2,1,0:T(8,128)S(1)} %get-tuple-element.439), channel_id=1, source_target_pairs={{1,0},{2,1},{3,2},{4,3},{5,4},{6,5},{7,6},{8,7},{9,8},{10,9},{11,1... | collective-permute-start | bytes 294920 | tf_op jit(solution)/shard_map/ppermute | solution.py:14
  208.6 10.9 %collective-permute-start.4 = (f32[2,64,512]{2,0,1:T(2,128)}, f32[2,64,512]{2,0,1:T(2,128)}, u32[]{:S(2)}, u32[]{:S(2)}) collective-permute-start(f32[2,64,512]{2,0,1:T(2,128)} %get-tuple-element.420), channel_id=1, source_target_pairs={{0,16},{16,32},{32,48},{48,64},{64,80},{80,96},{96,112},{112,128},... | collective-permute-start | bytes 786440 | tf_op jit(solution)/shard_map/ppermute | solution.py:14
  214.0 9.5 %collective-permute-start.5 = (f32[2,64,512]{2,0,1:T(2,128)}, f32[2,64,512]{2,0,1:T(2,128)}, u32[]{:S(2)}, u32[]{:S(2)}) collective-permute-start(f32[2,64,512]{2,0,1:T(2,128)} %get-tuple-element.419), channel_id=1, source_target_pairs={{16,0},{32,16},{48,32},{64,48},{80,64},{96,80},{112,96},{128,112},... | collective-permute-start | bytes 786440 | tf_op jit(solution)/shard_map/ppermute | solution.py:14
  219.4 10.5 %copy-start.9 = (f32[1,384,384]{2,1,0:T(8,128)S(1)}, f32[1,384,384]{2,1,0:T(8,128)}, u32[]{:S(2)}) copy-start(f32[1,384,384]{2,1,0:T(8,128)} %scatter-add.51) | copy-start | bytes 1769476
  225.9 22.0 %collective-permute-start.6 = (f32[2,384,64]{2,0,1:T(2,128)S(1)}, f32[2,384,64]{2,0,1:T(2,128)S(1)}, u32[]{:S(2)}, u32[]{:S(2)}) collective-permute-start(f32[2,384,64]{2,0,1:T(2,128)S(1)} %get-tuple-element.430), channel_id=1, source_target_pairs={{0,1},{1,2},{2,3},{3,4},{4,5},{5,6},{6,7},{7,8},{8,9},{9,10},{10,1... | collective-permute-start | bytes 589832 | tf_op jit(solution)/shard_map/ppermute | solution.py:14
  229.9 98.1 %copy-start.7 = (f32[384,384]{1,0:T(8,128)}, f32[384,384]{1,0:T(8,128)S(1)}, u32[]{:S(2)}) copy-start(f32[384,384]{1,0:T(8,128)S(1)} %add_bitcast_fusion) | copy-start | bytes 1769476
  232.3 29.7 %collective-permute-start.7 = (f32[2,384,64]{2,0,1:T(2,128)}, f32[2,384,64]{2,0,1:T(2,128)}, u32[]{:S(2)}, u32[]{:S(2)}) collective-permute-start(f32[2,384,64]{2,0,1:T(2,128)} %get-tuple-element.429), channel_id=1, source_target_pairs={{1,0},{2,1},{3,2},{4,3},{5,4},{6,5},{7,6},{8,7},{9,8},{10,9},{11,1... | collective-permute-start | bytes 589832 | tf_op jit(solution)/shard_map/ppermute | solution.py:14
  248.4 79.6 %copy-start.4 = (f32[2,384,384]{2,1,0:T(8,128)S(1)}, f32[2,384,384]{2,1,0:T(8,128)}, u32[]{:S(2)}) copy-start(f32[2,384,384]{2,1,0:T(8,128)} %param.35) | copy-start | bytes 3538948
  330.7 12.9 %copy-start.1 = (f32[2,384,384]{2,0,1:T(2,128)}, f32[2,384,384]{2,0,1:T(2,128)S(1)}, u32[]{:S(2)}) copy-start(f32[2,384,384]{2,0,1:T(2,128)S(1)} %divide_add_fusion.1) | copy-start | bytes 3538948
  330.8 5.0 collective-permute-start.12
  332.8 10.1 %collective-permute-start.13 = (f32[2,64,384]{2,0,1:T(2,128)S(1)}, f32[2,64,384]{2,0,1:T(2,128)S(1)}, u32[]{:S(2)}, u32[]{:S(2)}) collective-permute-start(f32[2,64,384]{2,0,1:T(2,128)S(1)} %get-tuple-element.434), channel_id=1, source_target_pairs={{16,0},{32,16},{48,32},{64,48},{80,64},{96,80},{112,96},{128,112},... | collective-permute-start | bytes 589832 | tf_op jit(solution)/shard_map/ppermute | solution.py:25
  343.6 26.3 %collective-permute-start.14 = (f32[2,512,64]{2,0,1:T(2,128)S(1)}, f32[2,512,64]{2,0,1:T(2,128)S(1)}, u32[]{:S(2)}, u32[]{:S(2)}) collective-permute-start(f32[2,512,64]{2,0,1:T(2,128)S(1)} %get-tuple-element.427), channel_id=1, source_target_pairs={{0,1},{1,2},{2,3},{3,4},{4,5},{5,6},{6,7},{7,8},{8,9},{9,10},{10,1... | collective-permute-start | bytes 786440 | tf_op jit(solution)/shard_map/ppermute | solution.py:22
  345.5 25.2 %collective-permute-start.15 = (f32[2,512,64]{2,0,1:T(2,128)S(1)}, f32[2,512,64]{2,0,1:T(2,128)}, u32[]{:S(2)}, u32[]{:S(2)}) collective-permute-start(f32[2,512,64]{2,0,1:T(2,128)S(1)} %get-tuple-element.428), channel_id=1, source_target_pairs={{1,0},{2,1},{3,2},{4,3},{5,4},{6,5},{7,6},{8,7},{9,8},{10,9},{11,1... | collective-permute-start | bytes 786440 | tf_op jit(solution)/shard_map/ppermute | solution.py:25
  475.6 5.6 collective-permute-start.16
  477.6 11.5 %collective-permute-start.17 = (f32[2,64,512]{2,0,1:T(2,128)S(1)}, f32[2,64,512]{2,0,1:T(2,128)S(1)}, u32[]{:S(2)}, u32[]{:S(2)}) collective-permute-start(f32[2,64,512]{2,0,1:T(2,128)S(1)} %get-tuple-element.417), channel_id=1, source_target_pairs={{16,0},{32,16},{48,32},{64,48},{80,64},{96,80},{112,96},{128,112},... | collective-permute-start | bytes 786440 | tf_op jit(solution)/shard_map/ppermute | solution.py:14
  490.5 21.3 %collective-permute-start.18 = (f32[2,384,64]{2,0,1:T(2,128)S(1)}, f32[2,384,64]{2,0,1:T(2,128)S(1)}, u32[]{:S(2)}, u32[]{:S(2)}) collective-permute-start(f32[2,384,64]{2,0,1:T(2,128)S(1)} %get-tuple-element.426), channel_id=1, source_target_pairs={{0,1},{1,2},{2,3},{3,4},{4,5},{5,6},{6,7},{7,8},{8,9},{9,10},{10,1... | collective-permute-start | bytes 589832 | tf_op jit(solution)/shard_map/ppermute | solution.py:14
  493.8 31.7 %collective-permute-start.19 = (f32[2,384,64]{2,0,1:T(2,128)}, f32[2,384,64]{2,0,1:T(2,128)}, u32[]{:S(2)}, u32[]{:S(2)}) collective-permute-start(f32[2,384,64]{2,0,1:T(2,128)} %get-tuple-element.425), channel_id=1, source_target_pairs={{1,0},{2,1},{3,2},{4,3},{5,4},{6,5},{7,6},{8,7},{9,8},{10,9},{11,1... | collective-permute-start | bytes 589832 | tf_op jit(solution)/shard_map/ppermute | solution.py:14
  512.3 78.9 %copy-start.2 = (f32[2,384,384]{2,0,1:T(2,128)S(1)}, f32[2,384,384]{2,0,1:T(2,128)}, u32[]{:S(2)}) copy-start(f32[2,384,384]{2,0,1:T(2,128)} %copy-done.1) | copy-start | bytes 3538948
  512.3 78.9 %copy-start.8 = (f32[384,384]{1,0:T(8,128)S(1)}, f32[384,384]{1,0:T(8,128)}, u32[]{:S(2)}) copy-start(f32[384,384]{1,0:T(8,128)} %copy-done.7) | copy-start | bytes 1769476
  (3 other events, 3.2 us)
where the time goes:
time: 601 us; the launch traced here: 593 us
  local copies, waits for them, and re-layouts  231 us (38%)
  waiting for transfers between devices  87.5 us (15%)
  matrix products  79.1 us (13%)
  other arithmetic  68.6 us (11%)
  loops' own time  67.3 us (11%)
  starting transfers between devices  57.6 us (10%)
    scatter-add x3, local copies, waits for them, and re-layouts, fold_back(): inner = inner.at[:, :, tile - half:].add(from_right)  130 us
    another operation x3, loops' own time, place_all(): return lax.fori_loop(0, pieces.shape[0], place, total)  67.3 us
    add x36, other arithmetic, place(): old + spread[slot]  40.2 us
    ppermute x12, waiting for transfers between devices, passed_along(): lax.ppermute(value, axis, [(source, source + steps) for source in range(l...  38.4 us
    ppermute x4, waiting for transfers between devices, with_halo(): lax.ppermute(lax.slice_in_dim(block, block.shape[dim] - width, None, axis...  38 us
    ppermute x12, starting transfers between devices, passed_along(): lax.ppermute(value, axis, [(source, source + steps) for source in range(l...  35 us
    scatter-add x3, local copies, waits for them, and re-layouts, fold_back(): inner = inner.at[:, :, :half].add(from_left)  28.5 us
    dot_general x16, matrix products, left_mul(): jnp.einsum('km,pmn->pkn', table, batch, precision=lax.Precision.HIGHEST)  26.8 us
  transfers between devices with their start and end apart: 20, of which 9 were waited for; matrix products, arithmetic and copies ran while one was open for 21% of the time, Pallas kernels for 0%

commit v1 on v0

v1 whole, which is shorter than its diff:
```python
import math

import jax
import jax.numpy as jnp
import numpy as np
from jax import lax
from jax.experimental import pallas as pl
from jax.experimental.pallas import tpu as pltpu
from jax.sharding import PartitionSpec as P

ITERS = 2
NEIGHBOURS = ((-1, 0), (1, 0), (0, -1), (0, 1), (-1, -1), (-1, 1), (1, -1), (1, 1))
OPPOSITE = (1, 0, 3, 2, 7, 6, 5, 4)
MESH = pl.DeviceIdType.MESH
VMEM = pl.BlockSpec(memory_space=pltpu.VMEM)
SMEM = pl.BlockSpec(memory_space=pltpu.SMEM)
LIMIT = 24 << 20


def dft_tables(length):
    index = np.arange(length)
    angle = (np.outer(index, index) % length) * (2.0 * math.pi / length)
    cosine, sine = np.cos(angle) / math.sqrt(length), np.sin(angle) / math.sqrt(length)
    table = np.block([[cosine, -sine], [sine, cosine]])
    high = table.astype(jnp.bfloat16)
    low = (table - high.astype(np.float64)).astype(jnp.bfloat16)
    return np.stack([high, low, high.T, low.T])


def there(d, grid):
    row, col = lax.axis_index("row"), lax.axis_index("col")
    ok = None
    if d[0]:
        ok = row > 0 if d[0] < 0 else row < grid[0] - 1
    if d[1]:
        side = col > 0 if d[1] < 0 else col < grid[1] - 1
        ok = side if ok is None else jnp.logical_and(ok, side)
    return ok


def target(d):
    return {"row": lax.axis_index("row") + d[0], "col": lax.axis_index("col") + d[1]}


def enter(grid):
    barrier = pltpu.get_barrier_semaphore()
    for d in NEIGHBOURS:

        @pl.when(there(d, grid))
        def _():
            pl.semaphore_signal(barrier, inc=1, device_id=target(d), device_id_type=MESH)

    up_down, left_right = 1, 1
    for d in NEIGHBOURS[:2]:
        up_down += jnp.where(there(d, grid), 1, 0)
    for d in NEIGHBOURS[2:4]:
        left_right += jnp.where(there(d, grid), 1, 0)
    pl.semaphore_wait(barrier, up_down * left_right - 1)


def start_all(copies, grid):
    for d, copy in zip(NEIGHBOURS, copies):

        @pl.when(there(d, grid))
        def _():
            copy.start()


def wait_all(copies, grid):
    for i, copy in enumerate(copies):

        @pl.when(there(NEIGHBOURS[i], grid))
        def _():
            copy.wait_send()

        @pl.when(there(NEIGHBOURS[OPPOSITE[i]], grid))
        def _():
            copy.wait_recv()


def swap(x):
    return pltpu.roll(x, 64, x.ndim - 1)


def lower(rows):
    return lax.broadcasted_iota(jnp.int32, (rows, 128), 1) < 64


def pack(x, keep_low):
    rows = x.shape[0] // 2
    keep = lower(rows) if keep_low else ~lower(rows)
    return jnp.where(keep, x[:rows], swap(x[rows:]))


def unpack(x):
    return jnp.concatenate([x, swap(x)], axis=0)


def remote(src, dst, sems, i):
    return pltpu.make_async_remote_copy(
        src, dst, sems.at[0, i], sems.at[1, i], device_id=target(NEIGHBOURS[i]), device_id_type=MESH
    )


def halo_copies(tile, ext, side, corner, side_in, corner_in, sems):
    half, edge = 64, tile.shape[1]
    first = edge - 384
    ends = [
        remote(
            tile.at[:, first // 2 : first // 2 + half, 0:384],
            ext.at[:, 448:512, 0:384],
            sems,
            0,
        ),
        remote(
            tile.at[:, first // 2 + 320 : first // 2 + 384, 0:384],
            ext.at[:, 0:half, 0:384],
            sems,
            1,
        ),
    ]
    ends += [remote(side.at[k], side_in.at[k], sems, 2 + k) for k in range(2)]
    ends += [remote(corner.at[k], corner_in.at[k], sems, 4 + k) for k in range(4)]
    return ends


def halo_pack(tile, base, side, corner):
    for p in range(2):
        for k, lane in enumerate((0, 256)):
            side[k, p] = pack(tile[p, base : base + 384, lane : lane + 128], k == 0)
        for k, (row, lane) in enumerate(((0, 0), (0, 256), (320, 0), (320, 256))):
            corner[k, p] = pack(tile[p, base + row : base + row + 64, lane : lane + 128], lane == 0)


def halo_unpack(ext, side_in, corner_in):
    for p in range(2):
        ext[p, 64:448, 384:512] = jnp.concatenate(
            [
                jnp.where(lower(192), side_in[0, p], side_in[1, p]),
                jnp.where(lower(192), swap(side_in[0, p]), swap(side_in[1, p])),
            ],
            axis=0,
        )
        for row, k in ((448, 0), (0, 2)):
            a, b = corner_in[k, p], corner_in[k + 1, p]
            ext[p, row : row + 64, 384:512] = jnp.concatenate(
                [jnp.where(lower(32), a, b), jnp.where(lower(32), swap(a), swap(b))], axis=0
            )


def halo_clear(ext, side_in, corner_in, grid):
    for i, d in enumerate(NEIGHBOURS):

        @pl.when(jnp.logical_not(there(d, grid)))
        def _():
            if i == 0:
                ext[:, 0:64, 0:384] = jnp.zeros((2, 64, 384), jnp.float32)
            elif i == 1:
                ext[:, 448:512, 0:384] = jnp.zeros((2, 64, 384), jnp.float32)
            elif i < 4:
                side_in[OPPOSITE[i] - 2] = jnp.zeros((2, 192, 128), jnp.float32)
            else:
                corner_in[OPPOSITE[i] - 4] = jnp.zeros((2, 32, 128), jnp.float32)


def fold_pack(update, side, corner):
    for p in range(2):
        for k in range(2):
            side[k, p] = pack(update[p, 64:448, 384:512], k == 1)
        for k, row in enumerate((0, 0, 448, 448)):
            corner[k, p] = pack(update[p, row : row + 64, 384:512], k % 2 == 1)


def fold_copies(update, ends_in, side, corner, side_in, corner_in, sems):
    ends = [
        remote(update.at[:, 0:64, 0:384], ends_in.at[0], sems, 0),
        remote(update.at[:, 448:512, 0:384], ends_in.at[1], sems, 1),
    ]
    ends += [remote(side.at[k], side_in.at[k], sems, 2 + k) for k in range(2)]
    ends += [remote(corner.at[k], corner_in.at[k], sems, 4 + k) for k in range(4)]
    return ends


def fold_add(dest, base, inverse, ends_in, side_in, corner_in, grid):
    def add(p, row, lane, value):
        rows, lanes = pl.ds(base + row, value.shape[0]), pl.ds(lane, value.shape[1])
        dest[p, rows, lanes] += value * inverse[pl.ds(row, value.shape[0]), lanes]

    for i, d in enumerate(NEIGHBOURS):

        @pl.when(there(NEIGHBOURS[OPPOSITE[i]], grid))
        def _():
            for p in range(2):
                if i < 2:
                    add(p, 320 if i == 0 else 0, 0, ends_in[i, p])
                elif i < 4:
                    x = unpack(side_in[i - 2, p])
                    keep = lower(384) if i == 3 else ~lower(384)
                    add(p, 0, 0 if i == 3 else 256, jnp.where(keep, x, 0.0))
                else:
                    x = unpack(corner_in[i - 4, p])
                    keep = lower(64) if d[1] == 1 else ~lower(64)
                    row, lane = (320 if d[0] == -1 else 0), (0 if d[1] == 1 else 256)
                    add(p, row, lane, jnp.where(keep, x, 0.0))


def spread_kernel(grid):
    def kernel(field, offsets, counts, ext, around, mine, side, corner, side_in, corner_in, sems, small):
        mine[...] = jnp.zeros_like(mine)
        mine[0:12, 0:2] = offsets[...]
        mine[12:13, 0:1] = counts[...]
        for i, d in enumerate(NEIGHBOURS):

            @pl.when(jnp.logical_not(there(d, grid)))
            def _():
                around[OPPOSITE[i]] = jnp.zeros((16, 128), jnp.int32)

        halo_clear(ext, side_in, corner_in, grid)
        halo_pack(field, 0, side, corner)
        enter(grid)
        copies = halo_copies(field, ext, side, corner, side_in, corner_in, sems)
        notes = [remote(mine, around.at[i], small, i) for i in range(8)]
        start_all(notes, grid)
        start_all(copies, grid)
        ext[:, 64:448, 0:384] = field[...]
        wait_all(copies, grid)
        wait_all(notes, grid)
        halo_unpack(ext, side_in, corner_in)

    return kernel


def split(x):
    high = x.astype(jnp.bfloat16)
    return high, (x - high.astype(jnp.float32)).astype(jnp.bfloat16)


def dot(a, b):
    return jnp.dot(a, b, preferred_element_type=jnp.float32)


def right_mul(x, high, low):
    xh, xl = split(x)
    return dot(xh, high) + dot(xl, high) + dot(xh, low)


def left_mul(high, low, x):
    xh, xl = split(x)
    return dot(high, xh) + dot(high, xl) + dot(low, xh)


def cross(x):
    return jnp.concatenate(
        [
            jnp.concatenate([x[:128, :128], x[128:, :128]], axis=1),
            jnp.concatenate([x[:128, 128:], x[128:, 128:]], axis=1),
        ],
        axis=0,
    )


def gradient_kernel(with_light):
    def kernel(*refs):
        if with_light:
            offsets, counts, around, ext, probe, measured, tables, update, inverse, tall, light, power = refs
        else:
            offsets, counts, ext, probe, measured, tables, update, tall = refs
        count = counts[0, 0]
        update[...] = jnp.zeros_like(update)
        for p in range(2):
            tall[p, 0:8] = probe[p, 120:128]
            tall[p, 8:136] = probe[p]
        if with_light:
            light[...] = jnp.zeros_like(light)
            power[...] = tall[0] * tall[0] + tall[1] * tall[1]
        lane = lax.broadcasted_iota(jnp.int32, (128, 128), 1)
        sub = lax.broadcasted_iota(jnp.int32, (8, 128), 0)

        def turned(source, shift_rows, shift_lanes):
            return pltpu.roll(source[pl.ds(8 - shift_rows, 128), :], shift_lanes, 1)

        def scatter(dest, first, lanes, shift_rows, shift_lanes, value):
            head = jnp.where(sub >= shift_rows, value[:8], 0.0)
            main = jnp.concatenate([head, value[8:]], axis=0)
            tail = jnp.where(sub < shift_rows, value[:8], 0.0)
            for which, at in enumerate(lanes):
                keep = lane >= shift_lanes if which == 0 else lane < shift_lanes
                dest[pl.ds(first, 128), at] += jnp.where(keep, main, 0.0)
                dest[pl.ds(first + 128, 8), at] += jnp.where(keep[:8], tail, 0.0)

        def tiles_of(col, base, wrap):
            tile = lax.shift_right_arithmetic(col, 7) + base
            first = lax.rem(tile + wrap, wrap)
            second = lax.rem(tile + wrap + 1, wrap)
            return [pl.ds(pl.multiple_of(t * 128, 128), 128) for t in (first, second)]

        def brighten(row, col):
            low_row, low_col = jnp.bitwise_and(row, 7), jnp.bitwise_and(col, 127)
            first = pl.multiple_of(row - low_row + 128, 8)
            scatter(light, first, tiles_of(col, 1, 5), low_row, low_col, turned(power, low_row, low_col))

        def pair(step, carry):
            places, waves, beams = [], [], []
            for which in range(2):
                slot = step * 2 + which
                row, col = offsets[slot, 0], offsets[slot, 1]
                low_row, low_col = jnp.bitwise_and(row, 7), jnp.bitwise_and(col, 127)
                first = pl.multiple_of(row - low_row + 64, 8)
                lanes = tiles_of(col, 0, 4)
                beam = [turned(tall.at[p], low_row, low_col) for p in range(2)]
                window = []
                for p in range(2):
                    main = jnp.where(
                        lane >= low_col, ext[p, pl.ds(first, 128), lanes[0]], ext[p, pl.ds(first, 128), lanes[1]]
                    )
                    tail = jnp.where(
                        lane[:8] >= low_col,
                        ext[p, pl.ds(first + 128, 8), lanes[0]],
                        ext[p, pl.ds(first + 128, 8), lanes[1]],
                    )
                    window.append(
                        jnp.concatenate([jnp.where(sub >= low_row, main[:8], tail), main[8:]], axis=0)
                    )
                real = beam[0] * window[0] - beam[1] * window[1]
                imag = beam[0] * window[1] + beam[1] * window[0]
                waves.append(jnp.concatenate([real, imag], axis=1))
                beams.append(beam)
                places.append((first, lanes, low_row, low_col, (slot < count).astype(jnp.float32), row, col))
            half = cross(right_mul(jnp.concatenate(waves, axis=0), tables[0], tables[1]))
            far = left_mul(tables[2], tables[3], half)
            real, imag = far[:128], far[128:]
            known = jnp.concatenate([measured[step * 2], measured[step * 2 + 1]], axis=1)
            ratio = known * lax.rsqrt(real * real + imag * imag + 0.25) - 1.0
            change = jnp.concatenate([real * ratio, imag * ratio], axis=0)
            half = cross(left_mul(tables[0], tables[1], change))
            back = right_mul(half, tables[2], tables[3])
            for which in range(2):
                first, lanes, low_row, low_col, live, row, col = places[which]
                beam = [b * live for b in beams[which]]
                real, imag = back[which * 128 : which * 128 + 128, :128], back[which * 128 : which * 128 + 128, 128:]
                scatter(update.at[0], first, lanes, low_row, low_col, beam[0] * real + beam[1] * imag)
                scatter(update.at[1], first, lanes, low_row, low_col, beam[0] * imag - beam[1] * real)
            return carry

        lax.fori_loop(0, lax.shift_right_logical(count + 1, 1), pair, 0)
        if with_light:

            def own(slot, carry):
                brighten(offsets[slot, 0], offsets[slot, 1])
                return carry

            lax.fori_loop(0, count, own, 0)
            for i, d in enumerate(NEIGHBOURS):

                def other(slot, carry):
                    row = around[i, slot, 0] - d[0] * 384
                    col = around[i, slot, 1] - d[1] * 384
                    touches = (row > -128) & (row < 384) & (col > -128) & (col < 384)

                    @pl.when(touches)
                    def _():
                        brighten(row, col)

                    return carry

                lax.fori_loop(0, around[i, 12, 0], other, 0)
            inverse[...] = 1.0 / (light[128:512, 128:512] + 1.0)

    return kernel


def between_kernel(grid):
    def kernel(update, inverse, field, ext, side, corner, side_in, corner_in, ends_in, sems, out_side, out_corner, halo_side, halo_corner, more):
        halo_clear(ext, halo_side, halo_corner, grid)
        fold_pack(update, side, corner)
        enter(grid)
        copies = fold_copies(update, ends_in, side, corner, side_in, corner_in, sems)
        start_all(copies, grid)
        for p in range(2):
            ext[p, 64:448, 0:384] = field[p] + update[p, 64:448, 0:384] * inverse[...]
        wait_all(copies, grid)
        fold_add(ext, 64, inverse, ends_in, side_in, corner_in, grid)
        halo_pack(ext, 64, out_side, out_corner)
        copies = halo_copies(ext, ext, out_side, out_corner, halo_side, halo_corner, more)
        start_all(copies, grid)
        wait_all(copies, grid)
        halo_unpack(ext, halo_side, halo_corner)

    return kernel


def last_kernel(grid):
    def kernel(update, inverse, ext, out, side, corner, side_in, corner_in, ends_in, sems):
        fold_pack(update, side, corner)
        enter(grid)
        copies = fold_copies(update, ends_in, side, corner, side_in, corner_in, sems)
        start_all(copies, grid)
        for p in range(2):
            out[p] = ext[p, 64:448, 0:384] + update[p, 64:448, 0:384] * inverse[...]
        wait_all(copies, grid)
        fold_add(out, 0, inverse, ends_in, side_in, corner_in, grid)

    return kernel


def params(collective_id=None):
    if collective_id is None:
        return pltpu.CompilerParams(vmem_limit_bytes=LIMIT)
    return pltpu.CompilerParams(collective_id=collective_id, has_side_effects=True, vmem_limit_bytes=LIMIT)


def shards(grid, tables, object_field, probe, amplitudes, offsets, counts):
    f32 = jnp.float32
    offsets, measured = offsets[0, 0], amplitudes[0, 0]
    ext_shape = jax.ShapeDtypeStruct((2, 512, 512), f32)
    packs = [pltpu.VMEM((2, 2, 192, 128), f32), pltpu.VMEM((4, 2, 32, 128), f32)]
    ends = pltpu.VMEM((2, 2, 64, 384), f32)
    sems = pltpu.SemaphoreType.DMA((2, 8))
    ext, around = pl.pallas_call(
        spread_kernel(grid),
        name="spread",
        out_shape=(ext_shape, jax.ShapeDtypeStruct((8, 16, 128), jnp.int32)),
        in_specs=[VMEM] * 3,
        out_specs=(VMEM, VMEM),
        scratch_shapes=[pltpu.VMEM((16, 128), jnp.int32)] + packs + packs + [sems, sems],
        compiler_params=params(0),
    )(object_field, offsets, counts)
    tall = pltpu.VMEM((2, 136, 128), f32)
    update, inverse = pl.pallas_call(
        gradient_kernel(True),
        name="gradient_light",
        out_shape=(ext_shape, jax.ShapeDtypeStruct((384, 384), f32)),
        in_specs=[SMEM] * 3 + [VMEM] * 4,
        out_specs=(VMEM, VMEM),
        scratch_shapes=[tall, pltpu.VMEM((648, 640), f32), pltpu.VMEM((136, 128), f32)],
        compiler_params=params(),
    )(offsets, counts, around, ext, probe, measured, tables)
    ext = pl.pallas_call(
        between_kernel(grid),
        name="between",
        out_shape=ext_shape,
        in_specs=[VMEM] * 3,
        out_specs=VMEM,
        scratch_shapes=packs + packs + [ends, sems] + packs + packs + [sems],
        compiler_params=params(1),
    )(update, inverse, object_field)
    update = pl.pallas_call(
        gradient_kernel(False),
        name="gradient",
        out_shape=ext_shape,
        in_specs=[SMEM] * 2 + [VMEM] * 4,
        out_specs=VMEM,
        scratch_shapes=[tall],
        compiler_params=params(),
    )(offsets, counts, ext, probe, measured, tables)
    return pl.pallas_call(
        last_kernel(grid),
        name="last",
        out_shape=jax.ShapeDtypeStruct((2, 384, 384), f32),
        in_specs=[VMEM] * 3,
        out_specs=VMEM,
        scratch_shapes=packs + packs + [ends, sems],
        compiler_params=params(2),
    )(update, inverse, ext)


def solution(mesh):
    grid = (mesh.shape["row"], mesh.shape["col"])
    tables = dft_tables(128)
    placed = (
        P(None, "row", "col"),
        P(),
        P("row", "col", None, None, None),
        P("row", "col", None, None),
        P("row", "col"),
    )

    def body(*args):
        return shards(grid, jnp.asarray(tables), *args)

    return jax.shard_map(body, mesh=mesh, in_specs=placed, out_specs=P(None, "row", "col"), check_vma=False)
```

time: 601 us -> 104 us (0.17)
  the two profiles are of different devices: /device:TPU:141 before, /device:TPU:202 now
where the time goes in v1:
time: 104 us; the launch traced here: 103 us
  Pallas kernels  95.9 us (92%)
  local copies, waits for them, and re-layouts  6.25 us (6%)
    pallas_call x1, Pallas kernels, shards(): pl.pallas_call(between_kernel(grid), name='between', out_shape=ext_shape,...  34.2 us
    pallas_call x1, Pallas kernels, shards(): pl.pallas_call(spread_kernel(grid), name='spread', out_shape=(ext_shape,...  20.6 us
    pallas_call x1, Pallas kernels, shards(): pl.pallas_call(last_kernel(grid), name='last', out_shape=jax.ShapeDtypeSt...  18 us
    pallas_call x1, Pallas kernels, shards(): pl.pallas_call(gradient_kernel(True), name='gradient_light', out_shape=(e...  13.3 us
    pallas_call x1, Pallas kernels, shards(): pl.pallas_call(gradient_kernel(False), name='gradient', out_shape=ext_sha...  9.85 us
    unnamed x17, local copies, waits for them, and re-layouts  5.48 us

profile of v1, /device:TPU:202, one launch (start us, length us, event | category | flops | bytes accessed | tf_op | source)
XLA Modules:
  0.0 102.9 jit_solution(14206427581229602639)
XLA Ops:
  0.7 0.8 copy.9.offsets.refs_0_
  1.4 0.0 copy-start
  1.4 1.3 %copy-done = f32[2,384,384]{2,1,0:T(8,128)S(1)} copy-done((f32[2,384,384]{2,1,0:T(8,128)S(1)}, f32[2,384,384]{2,1,0:T(8,128)}, u32[]{:S(2)}) %copy-start) | copy-done | bytes 1179672
  2.7 20.6 %spread.1 = (f32[2,512,512]{2,1,0:T(8,128)S(1)}, s32[8,16,128]{2,1,0:T(8,128)S(1)}) custom-call(f32[2,384,384]{2,1,0:T(8,128)S(1)} %copy-done, s32[12,2]{1,0:T(8,128)S(1)} %copy.9.offsets.refs_0_, s32[1,1]{1,0:T(1,128)S(6)} %copy.11.counts.refs_1_), custom_call_target="tpu_custom_call" | custom-call | tf_op jit(solution)/shard_map/spread/pallas_call | solution.py:419
  23.3 0.0 copy-start.1
  23.3 0.0 copy-start.2
  23.3 1.2 %copy-done.2 = f32[1,1,12,128,128]{4,3,2,1,0:T(8,128)S(1)} copy-done((f32[1,1,12,128,128]{4,3,2,1,0:T(8,128)S(1)}, f32[1,1,12,128,128]{4,3,2,1,0:T(8,128)}, u32[]{:S(2)}) %copy-start.2) | copy-done | bytes 786456
  24.5 0.0 copy-start.4
  24.5 1.0 %copy-done.4 = bf16[4,256,256]{2,1,0:T(8,128)(2,1)S(1)} copy-done((bf16[4,256,256]{2,1,0:T(8,128)(2,1)S(1)}, bf16[4,256,256]{2,1,0:T(8,128)(2,1)}, u32[]{:S(2)}) %copy-start.4) | copy-done | bytes 524312
  25.6 0.0 copy-start.6
  25.6 0.9 copy-done.6
  26.5 13.3 %gradient_light.1 = (f32[2,512,512]{2,1,0:T(8,128)S(1)}, f32[384,384]{1,0:T(8,128)S(1)}) custom-call(s32[12,2]{1,0:T(8,128)S(1)} %copy.9.offsets.refs_0_, s32[1,1]{1,0:T(1,128)S(6)} %copy.11.counts.refs_1_, s32[8,16,128]{2,1,0:T(8,128)S(1)} %get-tuple-element.9.refs_2_, f32[2,512,512]{2,1,0:T(8,128)S(1)} %get-tuple-element.10.refs_3_, ...), custom_call_target="tpu_custom_call" | custom-call | tf_op jit(solution)/shard_map/gradient_light/pallas_call | solution.py:429
  39.8 0.0 copy-done.1
  39.8 0.0 copy-start.3
  39.8 0.0 copy-start.5
  39.8 0.0 copy-start.7
  39.8 34.2 %between.1.refs_2_.ext = f32[2,512,512]{2,1,0:T(8,128)S(1)} custom-call(f32[2,512,512]{2,1,0:T(8,128)S(1)} %get-tuple-element.11.update, f32[384,384]{1,0:T(8,128)S(1)} %get-tuple-element.12.inverse, f32[2,384,384]{2,1,0:T(8,128)S(1)} %copy-done.1), custom_call_target="tpu_custom_call" | custom-call | tf_op jit(solution)/shard_map/between/pallas_call | solution.py:438
  74.0 0.0 copy-done.3
  74.0 0.0 copy-done.5
  74.1 0.0 copy-done.7
  74.1 9.8 %gradient.1.update = f32[2,512,512]{2,1,0:T(8,128)S(1)} custom-call(s32[12,2]{1,0:T(8,128)S(1)} %copy.9.offsets.refs_0_, s32[1,1]{1,0:T(1,128)S(6)} %copy.11.counts.refs_1_, f32[2,512,512]{2,1,0:T(8,128)S(1)} %between.1.refs_2_.ext, f32[2,128,128]{2,1,0:T(8,128)S(1)} %copy-done.7, f32[12,128,128]{2,1,0:T(8,128)S(1)} %bitcast.3, ...), custom_call_target="tpu_custom_call" | custom-call | tf_op jit(solution)/shard_map/gradient/pallas_call | solution.py:447
  83.9 18.0 %last.1 = f32[2,384,384]{2,1,0:T(8,128)S(1)} custom-call(f32[2,512,512]{2,1,0:T(8,128)S(1)} %gradient.1.update, f32[384,384]{1,0:T(8,128)S(1)} %get-tuple-element.12.inverse, f32[2,512,512]{2,1,0:T(8,128)S(1)} %between.1.refs_2_.ext), custom_call_target="tpu_custom_call" | custom-call | tf_op jit(solution)/shard_map/last/pallas_call | solution.py:456
  101.9 1.0 copy.12
Async XLA Ops:
  1.4 1.3 %copy-start = (f32[2,384,384]{2,1,0:T(8,128)S(1)}, f32[2,384,384]{2,1,0:T(8,128)}, u32[]{:S(2)}) copy-start(f32[2,384,384]{2,1,0:T(8,128)} %field.3) | copy-start | bytes 3538948
  23.3 16.5 %copy-start.1 = (f32[2,384,384]{2,1,0:T(8,128)S(1)}, f32[2,384,384]{2,1,0:T(8,128)}, u32[]{:S(2)}) copy-start(f32[2,384,384]{2,1,0:T(8,128)} %field.3) | copy-start | bytes 3538948
  23.3 1.2 %copy-start.2 = (f32[1,1,12,128,128]{4,3,2,1,0:T(8,128)S(1)}, f32[1,1,12,128,128]{4,3,2,1,0:T(8,128)}, u32[]{:S(2)}) copy-start(f32[1,1,12,128,128]{4,3,2,1,0:T(8,128)} %param.8) | copy-start | bytes 2359300
  24.5 1.0 %copy-start.4 = (bf16[4,256,256]{2,1,0:T(8,128)(2,1)S(1)}, bf16[4,256,256]{2,1,0:T(8,128)(2,1)}, u32[]{:S(2)}) copy-start(bf16[4,256,256]{2,1,0:T(8,128)(2,1)} %constant.2.clone.refs_6_.refs_5_) | copy-start | bytes 1572868
  25.6 0.9 copy-start.6
  39.8 34.3 %copy-start.3 = (f32[1,1,12,128,128]{4,3,2,1,0:T(8,128)S(1)}, f32[1,1,12,128,128]{4,3,2,1,0:T(8,128)}, u32[]{:S(2)}) copy-start(f32[1,1,12,128,128]{4,3,2,1,0:T(8,128)} %param.8) | copy-start | bytes 2359300
  39.8 34.3 %copy-start.5 = (bf16[4,256,256]{2,1,0:T(8,128)(2,1)S(1)}, bf16[4,256,256]{2,1,0:T(8,128)(2,1)}, u32[]{:S(2)}) copy-start(bf16[4,256,256]{2,1,0:T(8,128)(2,1)} %constant.2.clone.refs_6_.refs_5_) | copy-start | bytes 1572868
  39.8 34.3 %copy-start.7 = (f32[2,128,128]{2,1,0:T(8,128)S(1)}, f32[2,128,128]{2,1,0:T(8,128)}, u32[]{:S(2)}) copy-start(f32[2,128,128]{2,1,0:T(8,128)} %refs_3_.1) | copy-start | bytes 393220

commit v2 on v0

v2 whole, which is shorter than its diff:
```python
import math

import jax
import jax.numpy as jnp
import numpy as np
from jax import lax
from jax.experimental import pallas as pl
from jax.experimental.pallas import tpu as pltpu
from jax.sharding import PartitionSpec as P

AROUND = ((-1, 0), (1, 0), (0, -1), (0, 1), (-1, -1), (-1, 1), (1, -1), (1, 1))
MESH = pl.DeviceIdType.MESH
VMEM = pl.BlockSpec(memory_space=pltpu.VMEM)
SMEM = pl.BlockSpec(memory_space=pltpu.SMEM)
HBM = pl.BlockSpec(memory_space=pltpu.MemorySpace.HBM)
LIMIT = 24 << 20
NEAR, FAR, LEFT, RIGHT, FAR_LEFT, FAR_RIGHT, LEFT_NEXT, RIGHT_NEXT, RELAY = range(9)


def dft_tables(length):
    index = np.arange(length)
    angle = (np.outer(index, index) % length) * (2.0 * math.pi / length)
    cosine, sine = np.cos(angle) / math.sqrt(length), np.sin(angle) / math.sqrt(length)
    table = np.block([[cosine, -sine], [sine, cosine]])
    high = table.astype(jnp.bfloat16)
    low = (table - high.astype(np.float64)).astype(jnp.bfloat16)
    return np.stack([high, low, high.T, low.T])


def swap(x):
    return pltpu.roll(x, 64, x.ndim - 1)


def lower(rows):
    return lax.broadcasted_iota(jnp.int32, (rows, 128), 1) < 64


def pack(x, keep_low):
    rows = x.shape[0] // 2
    keep = lower(rows) if keep_low else ~lower(rows)
    return jnp.where(keep, x[:rows], swap(x[rows:]))


def unpack(x):
    return jnp.concatenate([x, swap(x)], axis=0)


def merge(a, b):
    keep = lower(a.shape[0])
    return jnp.concatenate([jnp.where(keep, a, b), jnp.where(keep, swap(a), swap(b))], axis=0)


class Place:
    def __init__(self, grid):
        self.row, self.col = lax.axis_index("row"), lax.axis_index("col")
        self.odd = lax.rem(self.row, 2)
        self.near_row = self.row + 1 - 2 * self.odd
        self.far_row = self.row - 1 + 2 * self.odd
        self.grid = grid
        far = (self.far_row >= 0) & (self.far_row < grid[0])
        left, right = self.col > 0, self.col < grid[1] - 1
        self.far, self.left, self.right = far, left, right
        both = (None, far, left, right, far & left, far & right, left, right, None)
        self.sends = both
        self.gets = tuple(both[i] for i in (NEAR, FAR, RIGHT, LEFT, FAR_RIGHT, FAR_LEFT, RIGHT_NEXT, LEFT_NEXT, RELAY))
        self.near_border = self.pick(320, 0)
        self.far_border = self.pick(0, 320)
        self.near_halo = self.pick(448, 0)
        self.far_halo = self.pick(0, 448)
        self.first = self.pick(256, 0)
        self.rest = self.pick(0, 128)

    def pick(self, even, odd):
        return pl.multiple_of(even + self.odd * (odd - even), 64)

    def target(self, which):
        row = {NEAR: self.near_row, RELAY: self.near_row, FAR: self.far_row, FAR_LEFT: self.far_row, FAR_RIGHT: self.far_row}
        side = {LEFT: -1, FAR_LEFT: -1, LEFT_NEXT: -1, RIGHT: 1, FAR_RIGHT: 1, RIGHT_NEXT: 1}
        return {"row": row.get(which, self.row), "col": self.col + side.get(which, 0)}


def when(condition, body):
    if condition is None:
        body()
    else:
        pl.when(condition)(body)


def greet(place):
    barrier = pltpu.get_barrier_semaphore()
    for which in (NEAR, FAR, LEFT, RIGHT, FAR_LEFT, FAR_RIGHT):
        when(
            place.sends[which],
            lambda: pl.semaphore_signal(
                barrier, inc=1, device_id=place.target(which), device_id_type=MESH
            ),
        )


def greeted(place):
    far, left, right = (jnp.where(x, 1, 0) for x in (place.far, place.left, place.right))
    pl.semaphore_wait(pltpu.get_barrier_semaphore(), 1 + far + (left + right) * (1 + far))


def greet_all(place):
    barrier = pltpu.get_barrier_semaphore()
    count = 0
    for d in AROUND:
        count += jnp.where(beside(place, d), 1, 0)

        @pl.when(beside(place, d))
        def _():
            pl.semaphore_signal(
                barrier, inc=1, device_id={"row": place.row + d[0], "col": place.col + d[1]}, device_id_type=MESH
            )

    return count


def beside(place, d):
    row, col = place.row + d[0], place.col + d[1]
    return (row >= 0) & (row < place.grid[0]) & (col >= 0) & (col < place.grid[1])


def remote(place, which, src, dst, sems, p):
    return pltpu.make_async_remote_copy(
        src, dst, sems.at[0, p, which], sems.at[1, p, which], device_id=place.target(which), device_id_type=MESH
    )


def start(place, copies, *which):
    for i in which:
        when(place.sends[i], copies[i].start)


def wait_recv(place, copies, *which):
    for i in which:
        when(place.gets[i], copies[i].wait_recv)


def wait_send(place, copies):
    for i, copy in enumerate(copies):
        when(place.sends[i], copy.wait_send)


def strips(side, side_in, corner, corner_in, p):
    return {
        FAR_LEFT: (corner.at[0, p], corner_in.at[0, p]),
        FAR_RIGHT: (corner.at[1, p], corner_in.at[1, p]),
        LEFT: (side.at[0, p, 0:64], side_in.at[0, p, 0:64]),
        RIGHT: (side.at[1, p, 0:64], side_in.at[1, p, 0:64]),
        LEFT_NEXT: (side.at[0, p, 64:192], side_in.at[0, p, 64:192]),
        RIGHT_NEXT: (side.at[1, p, 64:192], side_in.at[1, p, 64:192]),
    }


class Halo:
    def __init__(self, place, ext, side, corner, side_in, corner_in, sems):
        self.place, self.ext = place, ext
        self.side, self.corner, self.side_in, self.corner_in = side, corner, side_in, corner_in
        self.copies = []
        for p in range(2):
            ends = strips(side, side_in, corner, corner_in, p)
            rows = lambda first: pl.ds(first, 64)
            inner = lambda first: pl.ds(pl.multiple_of(first + 64, 64), 64)
            ends[NEAR] = (ext.at[p, inner(place.near_border), 0:384], ext.at[p, rows(place.far_halo), 0:384])
            ends[FAR] = (ext.at[p, inner(place.far_border), 0:384], ext.at[p, rows(place.near_halo), 0:384])
            ends[RELAY] = (ext.at[p, inner(place.near_border), 384:512], ext.at[p, rows(place.far_halo), 384:512])
            self.copies.append([remote(place, i, *ends[i], sems, p) for i in range(9)])

    def clear(self):
        place, ext = self.place, self.ext

        @pl.when(jnp.logical_not(place.far))
        def _():
            for p in range(2):
                ext[p, pl.ds(place.far_halo, 64), 0:384] = jnp.zeros((64, 384), jnp.float32)

        for k, side in enumerate((place.right, place.left)):

            @pl.when(jnp.logical_not(side))
            def _():
                self.side_in[k] = jnp.zeros((2, 192, 128), jnp.float32)

            @pl.when(jnp.logical_not(side & place.far))
            def _():
                self.corner_in[k] = jnp.zeros((2, 32, 128), jnp.float32)

    def pack(self, p):
        place, ext = self.place, self.ext
        for k, lane in enumerate((0, 256)):
            take = lambda first, rows: ext[p, pl.ds(pl.multiple_of(first + 64, 64), rows), lane : lane + 128]
            self.side[k, p, 0:64] = pack(take(place.first, 128), k == 0)
            self.side[k, p, 64:192] = pack(take(place.rest, 256), k == 0)
            self.corner[k, p] = pack(take(place.far_border, 64), k == 0)

    def start(self, p):
        start(self.place, self.copies[p], LEFT, RIGHT, FAR, NEAR, FAR_LEFT, FAR_RIGHT, LEFT_NEXT, RIGHT_NEXT)

    def finish(self):
        place, ext = self.place, self.ext
        for p in range(2):
            wait_recv(place, self.copies[p], LEFT, RIGHT)
            rows = pl.ds(pl.multiple_of(place.first + 64, 64), 128)
            ext[p, rows, 384:512] = merge(self.side_in[0, p, 0:64], self.side_in[1, p, 0:64])
            start(place, self.copies[p], RELAY)
            wait_recv(place, self.copies[p], FAR_LEFT, FAR_RIGHT, LEFT_NEXT, RIGHT_NEXT)
            ext[p, pl.ds(place.far_halo, 64), 384:512] = merge(self.corner_in[0, p], self.corner_in[1, p])
            rows = pl.ds(pl.multiple_of(place.rest + 64, 64), 256)
            ext[p, rows, 384:512] = merge(self.side_in[0, p, 64:192], self.side_in[1, p, 64:192])
        for p in range(2):
            wait_recv(place, self.copies[p], FAR, NEAR, RELAY)
            wait_send(place, self.copies[p])


class Fold:
    def __init__(self, place, update, ends_in, near_in, side, corner, side_in, corner_in, sems):
        self.place, self.update, self.ends_in, self.near_in = place, update, ends_in, near_in
        self.side, self.corner, self.side_in, self.corner_in = side, corner, side_in, corner_in
        self.copies = []
        for p in range(2):
            ends = strips(side, side_in, corner, corner_in, p)
            ends[NEAR] = (update.at[p, pl.ds(place.near_halo, 64), 0:384], ends_in.at[0, p])
            ends[FAR] = (update.at[p, pl.ds(place.far_halo, 64), 0:384], ends_in.at[1, p])
            ends[RELAY] = (update.at[p, pl.ds(place.near_halo, 64), 384:512], near_in.at[p])
            self.copies.append([remote(place, i, *ends[i], sems, p) for i in range(9)])

    def take(self, p, first, rows):
        return self.update[p, pl.ds(pl.multiple_of(first + 64, 64), rows), 384:512]

    def pack(self):
        place = self.place
        for p in range(2):
            for k in range(2):
                self.side[k, p, 64:192] = pack(self.take(p, place.rest, 256), k == 1)
                self.corner[k, p] = pack(self.update[p, pl.ds(place.far_halo, 64), 384:512], k == 1)

    def start(self):
        place = self.place
        odd = place.odd.astype(jnp.float32)
        for p in range(2):
            start(place, self.copies[p], RELAY)
        for p in range(2):
            start(place, self.copies[p], FAR, NEAR, FAR_LEFT, FAR_RIGHT, LEFT_NEXT, RIGHT_NEXT)
            wait_recv(place, self.copies[p], RELAY)
            part = self.take(p, place.first, 128)
            near = self.near_in[p]
            part = jnp.concatenate([part[:64] + near * odd, part[64:] + near * (1.0 - odd)], axis=0)
            for k in range(2):
                self.side[k, p, 0:64] = pack(part, k == 1)
            start(place, self.copies[p], LEFT, RIGHT)

    def finish(self, p, dest, base, inverse):
        place = self.place

        def add(first, lane, value):
            lanes, rows = pl.ds(lane, value.shape[1]), value.shape[0]
            at = pl.ds(pl.multiple_of(first + base, 64), rows)
            dest[p, at, lanes] += value * inverse[pl.ds(pl.multiple_of(first, 64), rows), lanes]

        def side(k, value):
            keep = ~lower(value.shape[0]) if k == 0 else lower(value.shape[0])
            return 256 if k == 0 else 0, jnp.where(keep, value, 0.0)

        for i in (FAR, NEAR, FAR_LEFT, FAR_RIGHT, LEFT_NEXT, RIGHT_NEXT, LEFT, RIGHT):

            def body():
                self.copies[p][i].wait_recv()
                k = i % 2
                if i == NEAR:
                    add(place.near_border, 0, self.ends_in[0, p])
                elif i == FAR:
                    add(place.far_border, 0, self.ends_in[1, p])
                elif i in (FAR_LEFT, FAR_RIGHT):
                    add(place.far_border, *side(k, unpack(self.corner_in[k, p])))
                elif i in (LEFT, RIGHT):
                    add(place.first, *side(k, unpack(self.side_in[k, p, 0:64])))
                else:
                    add(place.rest, *side(k, unpack(self.side_in[k, p, 64:192])))

            when(place.gets[i], body)

    def close(self):
        for p in range(2):
            wait_send(self.place, self.copies[p])


def spread_kernel(grid):
    def kernel(
        field, offsets, counts, measured, tables, probe,
        ext, around, measured_here, tables_here, probe_here, update, light,
        mine, offsets_here, side, corner, side_in, corner_in, sems, notes, local,
    ):
        place = Place(grid)
        peers = greet_all(place)
        pulls = [pltpu.make_async_copy(offsets, offsets_here, local.at[0])]
        pulls += [pltpu.make_async_copy(field.at[p], ext.at[p, 64:448, 0:384], local.at[1 + p]) for p in range(2)]
        later = [
            pltpu.make_async_copy(measured, measured_here, local.at[3]),
            pltpu.make_async_copy(tables, tables_here, local.at[4]),
            pltpu.make_async_copy(probe, probe_here, local.at[5]),
        ]
        for pull in pulls:
            pull.start()
        halo = Halo(place, ext, side, corner, side_in, corner_in, sems)
        halo.clear()
        for i, d in enumerate(AROUND):

            @pl.when(jnp.logical_not(beside(place, d)))
            def _():
                around[i] = jnp.zeros((8, 128), jnp.int32)

        pulls[0].wait()
        mine[0:2, 0:12] = offsets_here[0, 0]
        mine[2:3, 0:1] = jnp.full((1, 1), counts[0, 0], jnp.int32)
        around[8] = mine[...]
        pulls[1].wait()
        halo.pack(0)
        pl.semaphore_wait(pltpu.get_barrier_semaphore(), peers)
        halo.start(0)
        pulls[2].wait()
        halo.pack(1)
        halo.start(1)
        letters = []
        for i, d in enumerate(AROUND):
            letter = pltpu.make_async_remote_copy(
                mine,
                around.at[AROUND.index((-d[0], -d[1]))],
                notes.at[0, i],
                notes.at[1, i],
                device_id={"row": place.row + d[0], "col": place.col + d[1]},
                device_id_type=MESH,
            )
            letters.append(letter)
            pl.when(beside(place, d))(letter.start)
        for pull in later:
            pull.start()
        update[...] = jnp.zeros_like(update)
        light[...] = jnp.zeros_like(light)
        halo.finish()
        for i, d in enumerate(AROUND):
            pl.when(beside(place, d))(letters[i].wait_send)
            pl.when(beside(place, (-d[0], -d[1])))(letters[i].wait_recv)
        for pull in later:
            pull.wait()

    return kernel


def split(x):
    high = x.astype(jnp.bfloat16)
    return high, (x - high.astype(jnp.float32)).astype(jnp.bfloat16)


def dot(a, b):
    return jnp.dot(a, b, preferred_element_type=jnp.float32)


def right_mul(x, high, low):
    xh, xl = split(x)
    return dot(xh, high) + dot(xl, high) + dot(xh, low)


def left_mul(high, low, x):
    xh, xl = split(x)
    return dot(high, xh) + dot(high, xl) + dot(low, xh)


def cross(x):
    return jnp.concatenate(
        [
            jnp.concatenate([x[:128, :128], x[128:, :128]], axis=1),
            jnp.concatenate([x[:128, 128:], x[128:, 128:]], axis=1),
        ],
        axis=0,
    )


def gradient_kernel(with_light):
    def kernel(*refs):
        if with_light:
            around, ext, probe, measured, tables, _, _, update, inverse, light, tall, power = refs
        else:
            around, ext, probe, measured, tables, _, update, tall = refs
        count = around[8, 2, 0]
        for p in range(2):
            tall[p, 0:8] = probe[p, 120:128]
            tall[p, 8:136] = probe[p]
        lane = lax.broadcasted_iota(jnp.int32, (128, 128), 1)
        sub = lax.broadcasted_iota(jnp.int32, (8, 128), 0)

        def turned(source, shift_rows, shift_lanes):
            return pltpu.roll(source[pl.ds(8 - shift_rows, 128), :], shift_lanes, 1)

        def scatter(dest, first, lanes, shift_rows, shift_lanes, value):
            head = jnp.where(sub >= shift_rows, value[:8], 0.0)
            main = jnp.concatenate([head, value[8:]], axis=0)
            tail = jnp.where(sub < shift_rows, value[:8], 0.0)
            for which, at in enumerate(lanes):
                keep = lane >= shift_lanes if which == 0 else lane < shift_lanes
                dest[pl.ds(first, 128), at] += jnp.where(keep, main, 0.0)
                dest[pl.ds(first + 128, 8), at] += jnp.where(keep[:8], tail, 0.0)

        def tiles_of(col, base, wrap):
            tile = lax.shift_right_arithmetic(col, 7) + base
            first = lax.rem(tile + wrap, wrap)
            second = lax.rem(tile + wrap + 1, wrap)
            return [pl.ds(pl.multiple_of(t * 128, 128), 128) for t in (first, second)]

        def brighten(row, col, value):
            low_row, low_col = jnp.bitwise_and(row, 7), jnp.bitwise_and(col, 127)
            first = pl.multiple_of(row - low_row + 128, 8)
            scatter(light, first, tiles_of(col, 1, 5), low_row, low_col, value)

        def gather(slot):
            row, col = around[8, 0, slot], around[8, 1, slot]
            low_row, low_col = jnp.bitwise_and(row, 7), jnp.bitwise_and(col, 127)
            first = pl.multiple_of(row - low_row + 64, 8)
            lanes = tiles_of(col, 0, 4)
            beam = [turned(tall.at[p], low_row, low_col) for p in range(2)]
            window = []
            for p in range(2):
                main = jnp.where(
                    lane >= low_col, ext[p, pl.ds(first, 128), lanes[0]], ext[p, pl.ds(first, 128), lanes[1]]
                )
                tail = jnp.where(
                    lane[:8] >= low_col,
                    ext[p, pl.ds(first + 128, 8), lanes[0]],
                    ext[p, pl.ds(first + 128, 8), lanes[1]],
                )
                window.append(jnp.concatenate([jnp.where(sub >= low_row, main[:8], tail), main[8:]], axis=0))
            real = beam[0] * window[0] - beam[1] * window[1]
            imag = beam[0] * window[1] + beam[1] * window[0]
            live = (slot < count).astype(jnp.float32)
            return jnp.concatenate([real, imag], axis=1), (first, lanes, low_row, low_col, live, row, col)

        def put(back, at):
            first, lanes, low_row, low_col, live, row, col = at
            beam = [turned(tall.at[p], low_row, low_col) * live for p in range(2)]
            real, imag = back[:, :128], back[:, 128:]
            scatter(update.at[0], first, lanes, low_row, low_col, beam[0] * real + beam[1] * imag)
            scatter(update.at[1], first, lanes, low_row, low_col, beam[0] * imag - beam[1] * real)
            if with_light:
                brighten(row, col, beam[0] * beam[0] + beam[1] * beam[1])

        def quad(step, carry):
            slots = [step * 4 + k for k in range(4)]
            pairs = ((0, 1), (2, 3))
            gathered = [gather(slot) for slot in slots]
            waves = [jnp.concatenate([gathered[a][0], gathered[b][0]], axis=0) for a, b in pairs]
            half = [cross(right_mul(wave, tables[0], tables[1])) for wave in waves]
            far = [left_mul(tables[2], tables[3], x) for x in half]
            change = []
            for x, (a, b) in zip(far, pairs):
                real, imag = x[:128], x[128:]
                known = jnp.concatenate([measured[0, 0, slots[a]], measured[0, 0, slots[b]]], axis=1)
                ratio = known * lax.rsqrt(real * real + imag * imag + 0.25) - 1.0
                change.append(jnp.concatenate([real * ratio, imag * ratio], axis=0))
            half = [cross(left_mul(tables[0], tables[1], x)) for x in change]
            back = [right_mul(x, tables[2], tables[3]) for x in half]
            for x, (a, b) in zip(back, pairs):
                put(x[:128], gathered[a][1])
                put(x[128:], gathered[b][1])
            return carry

        lax.fori_loop(0, lax.shift_right_logical(count + 3, 2), quad, 0)
        if with_light:
            power[...] = tall[0] * tall[0] + tall[1] * tall[1]
            for i, d in enumerate(AROUND):

                def other(slot, carry):
                    row = around[i, 0, slot] + d[0] * 384
                    col = around[i, 1, slot] + d[1] * 384
                    touches = (row > -128) & (row < 384) & (col > -128) & (col < 384)

                    @pl.when(touches)
                    def _():
                        low_row, low_col = jnp.bitwise_and(row, 7), jnp.bitwise_and(col, 127)
                        brighten(row, col, turned(power, low_row, low_col))

                    return carry

                lax.fori_loop(0, around[i, 2, 0], other, 0)
            inverse[...] = 1.0 / (light[128:512, 128:512] + 1.0)

    return kernel


def between_kernel(grid):
    def kernel(
        update, inverse, field,
        ext, cleared,
        ends_in, near_in, side, corner, side_in, corner_in, sems,
        halo_side, halo_corner, halo_side_in, halo_corner_in, more,
    ):
        place = Place(grid)
        greet(place)
        fold = Fold(place, update, ends_in, near_in, side, corner, side_in, corner_in, sems)
        halo = Halo(place, ext, halo_side, halo_corner, halo_side_in, halo_corner_in, more)
        fold.pack()
        greeted(place)
        fold.start()
        halo.clear()
        for p in range(2):
            ext[p, 64:448, 0:384] = field[p, 64:448, 0:384] + update[p, 64:448, 0:384] * inverse[...]
        cleared[...] = jnp.zeros_like(cleared)
        for p in range(2):
            fold.finish(p, ext, 64, inverse)
            halo.pack(p)
            halo.start(p)
        halo.finish()
        fold.close()

    return kernel


def last_kernel(grid):
    def kernel(update, inverse, ext, out, ends_in, near_in, side, corner, side_in, corner_in, sems):
        place = Place(grid)
        greet(place)
        fold = Fold(place, update, ends_in, near_in, side, corner, side_in, corner_in, sems)
        fold.pack()
        greeted(place)
        fold.start()
        for p in range(2):
            out[p] = ext[p, 64:448, 0:384] + update[p, 64:448, 0:384] * inverse[...]
        for p in range(2):
            fold.finish(p, out, 0, inverse)
        fold.close()

    return kernel


def hold(x):
    return pltpu.with_memory_space_constraint(x, pltpu.MemorySpace.HBM)


def params(collective_id=None):
    if collective_id is None:
        return pltpu.CompilerParams(vmem_limit_bytes=LIMIT)
    return pltpu.CompilerParams(collective_id=collective_id, has_side_effects=True, vmem_limit_bytes=LIMIT)


def shards(grid, tables, object_field, probe, amplitudes, offsets, counts):
    f32, i32 = jnp.float32, jnp.int32
    shape = jax.ShapeDtypeStruct
    ext_shape = shape((2, 512, 512), f32)
    packs = [pltpu.VMEM((2, 2, 192, 128), f32), pltpu.VMEM((2, 2, 32, 128), f32)]
    folds = [pltpu.VMEM((2, 2, 64, 384), f32), pltpu.VMEM((2, 64, 128), f32)] + packs + packs
    sems = pltpu.SemaphoreType.DMA((2, 2, 9))
    ext, around, measured, tables, probe, update, light = pl.pallas_call(
        spread_kernel(grid),
        name="spread",
        out_shape=(
            ext_shape,
            shape((9, 8, 128), i32),
            shape(amplitudes.shape, f32),
            shape(tables.shape, tables.dtype),
            shape(probe.shape, f32),
            ext_shape,
            shape((648, 640), f32),
        ),
        in_specs=[HBM, HBM, SMEM, HBM, HBM, HBM],
        out_specs=(VMEM,) * 7,
        scratch_shapes=[pltpu.VMEM((8, 128), i32), pltpu.VMEM((1, 1, 2, 12), i32)]
        + packs
        + packs
        + [sems, pltpu.SemaphoreType.DMA((2, 8)), pltpu.SemaphoreType.DMA((6,))],
        compiler_params=params(0),
    )(*(hold(x) for x in (object_field, jnp.swapaxes(offsets, 2, 3))), counts, *(hold(x) for x in (amplitudes, tables, probe)))
    tall = pltpu.VMEM((2, 136, 128), f32)
    update, inverse, _ = pl.pallas_call(
        gradient_kernel(True),
        name="gradient_light",
        out_shape=(ext_shape, shape((384, 384), f32), shape((648, 640), f32)),
        in_specs=[SMEM] + [VMEM] * 6,
        out_specs=(VMEM,) * 3,
        scratch_shapes=[tall, pltpu.VMEM((136, 128), f32)],
        input_output_aliases={5: 0, 6: 2},
        compiler_params=params(),
    )(around, ext, probe, measured, tables, update, light)
    ext, cleared = pl.pallas_call(
        between_kernel(grid),
        name="between",
        out_shape=(ext_shape, ext_shape),
        in_specs=[VMEM] * 3,
        out_specs=(VMEM, VMEM),
        scratch_shapes=folds + [sems] + packs + packs + [sems],
        compiler_params=params(1),
    )(update, inverse, ext)
    update = pl.pallas_call(
        gradient_kernel(False),
        name="gradient",
        out_shape=ext_shape,
        in_specs=[SMEM] + [VMEM] * 5,
        out_specs=VMEM,
        scratch_shapes=[tall],
        input_output_aliases={5: 0},
        compiler_params=params(),
    )(around, ext, probe, measured, tables, cleared)
    return pl.pallas_call(
        last_kernel(grid),
        name="last",
        out_shape=shape((2, 384, 384), f32),
        in_specs=[VMEM] * 3,
        out_specs=VMEM,
        scratch_shapes=folds + [sems],
        compiler_params=params(2),
    )(update, inverse, ext)


def solution(mesh):
    grid = (mesh.shape["row"], mesh.shape["col"])
    tables = dft_tables(128)
    placed = (
        P(None, "row", "col"),
        P(),
        P("row", "col", None, None, None),
        P("row", "col", None, None),
        P("row", "col"),
    )

    def body(*args):
        return shards(grid, jnp.asarray(tables), *args)

    return jax.shard_map(body, mesh=mesh, in_specs=placed, out_specs=P(None, "row", "col"), check_vma=False)
```

time: 601 us -> 80.9 us (0.13)
  the two profiles are of different devices: /device:TPU:141 before, /device:TPU:195 now
where the time goes in v2:
time: 80.9 us; the launch traced here: 80.5 us
  Pallas kernels  78.8 us (97%)
  local copies, waits for them, and re-layouts  1.02 us (1%)
    pallas_call x1, Pallas kernels, shards(): pl.pallas_call(between_kernel(grid), name='between', out_shape=(ext_shape...  32.3 us
    pallas_call x1, Pallas kernels, shards(): pl.pallas_call(spread_kernel(grid), name='spread', out_shape=(ext_shape,...  19.7 us
    pallas_call x1, Pallas kernels, shards(): pl.pallas_call(last_kernel(grid), name='last', out_shape=shape((2, 384, 3...  19.4 us
    pallas_call x1, Pallas kernels, shards(): pl.pallas_call(gradient_kernel(True), name='gradient_light', out_shape=(e...  4.58 us
    pallas_call x1, Pallas kernels, shards(): pl.pallas_call(gradient_kernel(False), name='gradient', out_shape=ext_sha...  2.84 us

profile of v2, /device:TPU:195, one launch (start us, length us, event | category | flops | bytes accessed | tf_op | source)
XLA Modules:
  0.0 80.5 jit_solution(3885157071005990550)
XLA Ops:
  0.7 19.7 %spread.1 = (f32[2,512,512]{2,1,0:T(8,128)S(1)}, s32[9,8,128]{2,1,0:T(8,128)S(1)}, f32[1,1,12,128,128]{4,3,2,1,0:T(8,128)S(1)}, bf16[4,256,256]{2,1,0:T(8,128)(2...) custom-call(f32[2,384,384]{2,1,0:T(8,128)} %field.1, ...), custom_call_target="tpu_custom_call" | custom-call | tf_op jit(solution)/shard_map/spread/pallas_call | solution.py:551
  20.4 4.6 %gradient_light.1 = (f32[2,512,512]{2,1,0:T(8,128)S(1)}, f32[384,384]{1,0:T(8,128)S(1)}, f32[648,640]{1,0:T(8,128)S(1)}) custom-call(s32[9,8,128]{2,1,0:T(8,128)S(1)} %get-tuple-element.16.refs_0_, f32[2,512,512]{2,1,0:T(8,128)S(1)} %get-tuple-element.17.refs_1_.field, ...), custom_call_target="tpu_custom_call", output_to_operand_aliasing={{0}: (5, {}), {2}: (6, {})} | custom-call | tf_op jit(solution)/shard_map/gradient_light/pallas_call | solution.py:572
  24.9 32.3 %between.1 = (f32[2,512,512]{2,1,0:T(8,128)S(1)}, f32[2,512,512]{2,1,0:T(8,128)S(1)}) custom-call(f32[2,512,512]{2,1,0:T(8,128)S(1)} %get-tuple-element.23.update, f32[384,384]{1,0:T(8,128)S(1)} %get-tuple-element.24.inverse, f32[2,512,512]{2,1,0:T(8,128)S(1)} %get-tuple-element.17.refs_1_.field), custom_call_target="tpu_custom_call" | custom-call | tf_op jit(solution)/shard_map/between/pallas_call | solution.py:582
  57.2 2.8 %gradient.1.update = f32[2,512,512]{2,1,0:T(8,128)S(1)} custom-call(s32[9,8,128]{2,1,0:T(8,128)S(1)} %get-tuple-element.16.refs_0_, f32[2,512,512]{2,1,0:T(8,128)S(1)} %get-tuple-element.25.refs_1_.ext, f32[2,128,128]{2,1,0:T(8,128)S(1)} %get-tuple-element.18.refs_2_, ...), custom_call_target="tpu_custom_call", output_to_operand_aliasing={{}: (5, {})} | custom-call | tf_op jit(solution)/shard_map/gradient/pallas_call | solution.py:591
  60.1 19.4 %last.1 = f32[2,384,384]{2,1,0:T(8,128)S(1)} custom-call(f32[2,512,512]{2,1,0:T(8,128)S(1)} %gradient.1.update, f32[384,384]{1,0:T(8,128)S(1)} %get-tuple-element.24.inverse, f32[2,512,512]{2,1,0:T(8,128)S(1)} %get-tuple-element.25.refs_1_.ext), custom_call_target="tpu_custom_call" | custom-call | tf_op jit(solution)/shard_map/last/pallas_call | solution.py:601
  79.5 1.0 %copy.15 = f32[2,384,384]{2,1,0:T(8,128)} copy(f32[2,384,384]{2,1,0:T(8,128)S(1)} %last.1) | data formatting | bytes 2359296

commit v3 on v2

--- a/solution.py
+++ b/solution.py
@@ -14,6 +14,7 @@
 SMEM = pl.BlockSpec(memory_space=pltpu.SMEM)
 HBM = pl.BlockSpec(memory_space=pltpu.MemorySpace.HBM)
 LIMIT = 24 << 20
+GROUP = 6
 NEAR, FAR, LEFT, RIGHT, FAR_LEFT, FAR_RIGHT, LEFT_NEXT, RIGHT_NEXT, RELAY = range(9)
 
 
@@ -287,9 +288,9 @@
 
 def spread_kernel(grid):
     def kernel(
-        field, offsets, counts, measured, tables, probe,
-        ext, around, measured_here, tables_here, probe_here, update, light,
-        mine, offsets_here, side, corner, side_in, corner_in, sems, notes, local,
+        field, offsets, counts, places, measured, tables, probe,
+        ext, around, measured_here, tables_here, beams, power, update, light,
+        mine, offsets_here, tall, side, corner, side_in, corner_in, sems, notes, local,
     ):
         place = Place(grid)
         peers = greet_all(place)
@@ -298,8 +299,8 @@
         later = [
             pltpu.make_async_copy(measured, measured_here, local.at[3]),
             pltpu.make_async_copy(tables, tables_here, local.at[4]),
-            pltpu.make_async_copy(probe, probe_here, local.at[5]),
         ]
+        pulls.append(pltpu.make_async_copy(probe, tall.at[:, 8:136], local.at[5]))
         for pull in pulls:
             pull.start()
         halo = Halo(place, ext, side, corner, side_in, corner_in, sems)
@@ -314,13 +315,6 @@
         mine[0:2, 0:12] = offsets_here[0, 0]
         mine[2:3, 0:1] = jnp.full((1, 1), counts[0, 0], jnp.int32)
         around[8] = mine[...]
-        pulls[1].wait()
-        halo.pack(0)
-        pl.semaphore_wait(pltpu.get_barrier_semaphore(), peers)
-        halo.start(0)
-        pulls[2].wait()
-        halo.pack(1)
-        halo.start(1)
         letters = []
         for i, d in enumerate(AROUND):
             letter = pltpu.make_async_remote_copy(
@@ -332,11 +326,32 @@
                 device_id_type=MESH,
             )
             letters.append(letter)
-            pl.when(beside(place, d))(letter.start)
+        pulls[1].wait()
+        halo.pack(0)
+        pl.semaphore_wait(pltpu.get_barrier_semaphore(), peers)
+        for i, d in enumerate(AROUND):
+            pl.when(beside(place, d))(letters[i].start)
+        halo.start(0)
+        pulls[2].wait()
+        halo.pack(1)
+        halo.start(1)
         for pull in later:
             pull.start()
         update[...] = jnp.zeros_like(update)
         light[...] = jnp.zeros_like(light)
+        pulls[3].wait()
+        for p in range(2):
+            tall[p, 0:8] = tall[p, 128:136]
+        power[...] = tall[0] * tall[0] + tall[1] * tall[1]
+
+        def turn(slot, carry):
+            live = (slot < counts[0, 0]).astype(jnp.float32)
+            low_row, low_col = places[0, 0, 0, slot] & 7, places[0, 0, 1, slot] & 127
+            for p in range(2):
+                beams[slot, p] = pltpu.roll(tall[p, pl.ds(8 - low_row, 128), :], low_col, 1) * live
+            return carry
+
+        lax.fori_loop(0, 12, turn, 0)
         halo.finish()
         for i, d in enumerate(AROUND):
             pl.when(beside(place, d))(letters[i].wait_send)
@@ -379,13 +394,10 @@
 def gradient_kernel(with_light):
     def kernel(*refs):
         if with_light:
-            around, ext, probe, measured, tables, _, _, update, inverse, light, tall, power = refs
+            around, ext, beams, measured, tables, _, power, _, update, light = refs
         else:
-            around, ext, probe, measured, tables, _, update, tall = refs
+            around, ext, beams, measured, tables, _, update = refs
         count = around[8, 2, 0]
-        for p in range(2):
-            tall[p, 0:8] = probe[p, 120:128]
-            tall[p, 8:136] = probe[p]
         lane = lax.broadcasted_iota(jnp.int32, (128, 128), 1)
         sub = lax.broadcasted_iota(jnp.int32, (8, 128), 0)
 
@@ -417,7 +429,7 @@
             low_row, low_col = jnp.bitwise_and(row, 7), jnp.bitwise_and(col, 127)
             first = pl.multiple_of(row - low_row + 64, 8)
             lanes = tiles_of(col, 0, 4)
-            beam = [turned(tall.at[p], low_row, low_col) for p in range(2)]
+            beam = [beams[slot, p] for p in range(2)]
             window = []
             for p in range(2):
                 main = jnp.where(
@@ -431,21 +443,20 @@
                 window.append(jnp.concatenate([jnp.where(sub >= low_row, main[:8], tail), main[8:]], axis=0))
             real = beam[0] * window[0] - beam[1] * window[1]
             imag = beam[0] * window[1] + beam[1] * window[0]
-            live = (slot < count).astype(jnp.float32)
-            return jnp.concatenate([real, imag], axis=1), (first, lanes, low_row, low_col, live, row, col)
+            return jnp.concatenate([real, imag], axis=1), (slot, first, lanes, low_row, low_col, row, col)
 
         def put(back, at):
-            first, lanes, low_row, low_col, live, row, col = at
-            beam = [turned(tall.at[p], low_row, low_col) * live for p in range(2)]
+            slot, first, lanes, low_row, low_col, row, col = at
+            beam = [beams[slot, p] for p in range(2)]
             real, imag = back[:, :128], back[:, 128:]
             scatter(update.at[0], first, lanes, low_row, low_col, beam[0] * real + beam[1] * imag)
             scatter(update.at[1], first, lanes, low_row, low_col, beam[0] * imag - beam[1] * real)
             if with_light:
                 brighten(row, col, beam[0] * beam[0] + beam[1] * beam[1])
 
-        def quad(step, carry):
-            slots = [step * 4 + k for k in range(4)]
-            pairs = ((0, 1), (2, 3))
+        def some(step, carry):
+            slots = [step * GROUP + k for k in range(GROUP)]
+            pairs = [(k, k + 1) for k in range(0, GROUP, 2)]
             gathered = [gather(slot) for slot in slots]
             waves = [jnp.concatenate([gathered[a][0], gathered[b][0]], axis=0) for a, b in pairs]
             half = [cross(right_mul(wave, tables[0], tables[1])) for wave in waves]
@@ -463,9 +474,8 @@
                 put(x[128:], gathered[b][1])
             return carry
 
-        lax.fori_loop(0, lax.shift_right_logical(count + 3, 2), quad, 0)
+        lax.fori_loop(0, (count + GROUP - 1) // GROUP, some, 0)
         if with_light:
-            power[...] = tall[0] * tall[0] + tall[1] * tall[1]
             for i, d in enumerate(AROUND):
 
                 def other(slot, carry):
@@ -481,15 +491,14 @@
                     return carry
 
                 lax.fori_loop(0, around[i, 2, 0], other, 0)
-            inverse[...] = 1.0 / (light[128:512, 128:512] + 1.0)
 
     return kernel
 
 
 def between_kernel(grid):
     def kernel(
-        update, inverse, field,
-        ext, cleared,
+        update, light, field,
+        ext, cleared, inverse,
         ends_in, near_in, side, corner, side_in, corner_in, sems,
         halo_side, halo_corner, halo_side_in, halo_corner_in, more,
     ):
@@ -501,6 +510,7 @@
         greeted(place)
         fold.start()
         halo.clear()
+        inverse[...] = 1.0 / (light[128:512, 128:512] + 1.0)
         for p in range(2):
             ext[p, 64:448, 0:384] = field[p, 64:448, 0:384] + update[p, 64:448, 0:384] * inverse[...]
         cleared[...] = jnp.zeros_like(cleared)
@@ -544,11 +554,12 @@
 def shards(grid, tables, object_field, probe, amplitudes, offsets, counts):
     f32, i32 = jnp.float32, jnp.int32
     shape = jax.ShapeDtypeStruct
-    ext_shape = shape((2, 512, 512), f32)
+    ext_shape, light_shape = shape((2, 512, 512), f32), shape((648, 640), f32)
+    offsets = jnp.swapaxes(offsets, 2, 3)
     packs = [pltpu.VMEM((2, 2, 192, 128), f32), pltpu.VMEM((2, 2, 32, 128), f32)]
     folds = [pltpu.VMEM((2, 2, 64, 384), f32), pltpu.VMEM((2, 64, 128), f32)] + packs + packs
     sems = pltpu.SemaphoreType.DMA((2, 2, 9))
-    ext, around, measured, tables, probe, update, light = pl.pallas_call(
+    ext, around, measured, tables, beams, power, update, light = pl.pallas_call(
         spread_kernel(grid),
         name="spread",
         out_shape=(
@@ -556,48 +567,46 @@
             shape((9, 8, 128), i32),
             shape(amplitudes.shape, f32),
             shape(tables.shape, tables.dtype),
-            shape(probe.shape, f32),
+            shape((12, 2, 128, 128), f32),
+            shape((136, 128), f32),
             ext_shape,
-            shape((648, 640), f32),
+            light_shape,
         ),
-        in_specs=[HBM, HBM, SMEM, HBM, HBM, HBM],
-        out_specs=(VMEM,) * 7,
-        scratch_shapes=[pltpu.VMEM((8, 128), i32), pltpu.VMEM((1, 1, 2, 12), i32)]
+        in_specs=[HBM, HBM, SMEM, SMEM, HBM, HBM, HBM],
+        out_specs=(VMEM,) * 8,
+        scratch_shapes=[pltpu.VMEM((8, 128), i32), pltpu.VMEM((1, 1, 2, 12), i32), pltpu.VMEM((2, 136, 128), f32)]
         + packs
         + packs
         + [sems, pltpu.SemaphoreType.DMA((2, 8)), pltpu.SemaphoreType.DMA((6,))],
         compiler_params=params(0),
-    )(*(hold(x) for x in (object_field, jnp.swapaxes(offsets, 2, 3))), counts, *(hold(x) for x in (amplitudes, tables, probe)))
-    tall = pltpu.VMEM((2, 136, 128), f32)
-    update, inverse, _ = pl.pallas_call(
+    )(hold(object_field), hold(offsets), counts, offsets, hold(amplitudes), hold(tables), hold(probe))
+    update, light = pl.pallas_call(
         gradient_kernel(True),
         name="gradient_light",
-        out_shape=(ext_shape, shape((384, 384), f32), shape((648, 640), f32)),
-        in_specs=[SMEM] + [VMEM] * 6,
-        out_specs=(VMEM,) * 3,
-        scratch_shapes=[tall, pltpu.VMEM((136, 128), f32)],
-        input_output_aliases={5: 0, 6: 2},
+        out_shape=(ext_shape, light_shape),
+        in_specs=[SMEM] + [VMEM] * 7,
+        out_specs=(VMEM,) * 2,
+        input_output_aliases={5: 0, 7: 1},
         compiler_params=params(),
-    )(around, ext, probe, measured, tables, update, light)
-    ext, cleared = pl.pallas_call(
+    )(around, ext, beams, measured, tables, update, power, light)
+    ext, cleared, inverse = pl.pallas_call(
         between_kernel(grid),
         name="between",
-        out_shape=(ext_shape, ext_shape),
+        out_shape=(ext_shape, ext_shape, shape((384, 384), f32)),
         in_specs=[VMEM] * 3,
-        out_specs=(VMEM, VMEM),
+        out_specs=(VMEM,) * 3,
         scratch_shapes=folds + [sems] + packs + packs + [sems],
         compiler_params=params(1),
-    )(update, inverse, ext)
+    )(update, light, ext)
     update = pl.pallas_call(
         gradient_kernel(False),
         name="gradient",
         out_shape=ext_shape,
         in_specs=[SMEM] + [VMEM] * 5,
         out_specs=VMEM,
-        scratch_shapes=[tall],
         input_output_aliases={5: 0},
         compiler_params=params(),
-    )(around, ext, probe, measured, tables, cleared)
+    )(around, ext, beams, measured, tables, cleared)
     return pl.pallas_call(
         last_kernel(grid),
         name="last",

time: 80.9 us -> 79.8 us (0.986)
  the two profiles are of different devices: /device:TPU:195 before, /device:TPU:107 now
where the time goes in v3:
time: 79.8 us; the launch traced here: 80.1 us
  Pallas kernels  78.4 us (98%)
  local copies, waits for them, and re-layouts  1.02 us (1%)
    pallas_call x1, Pallas kernels, shards(): pl.pallas_call(between_kernel(grid), name='between', out_shape=(ext_shape...  29 us
    pallas_call x1, Pallas kernels, shards(): pl.pallas_call(spread_kernel(grid), name='spread', out_shape=(ext_shape,...  19.6 us
    pallas_call x1, Pallas kernels, shards(): pl.pallas_call(last_kernel(grid), name='last', out_shape=shape((2, 384, 3...  17.7 us
    pallas_call x1, Pallas kernels, shards(): pl.pallas_call(gradient_kernel(True), name='gradient_light', out_shape=(e...  7.31 us
    pallas_call x1, Pallas kernels, shards(): pl.pallas_call(gradient_kernel(False), name='gradient', out_shape=ext_sha...  4.9 us

profile of v3, /device:TPU:107, one launch (start us, length us, event | category | flops | bytes accessed | tf_op | source)
XLA Modules:
  0.0 80.1 jit_solution(5837339694038456227)
XLA Ops:
  0.7 19.6 %spread.1 = (f32[2,512,512]{2,1,0:T(8,128)S(1)}, s32[9,8,128]{2,1,0:T(8,128)S(1)}, f32[1,1,12,128,128]{4,3,2,1,0:T(8,128)S(1)}, bf16[4,256,256]{2,1,0:T(8,128)(2...) custom-call(f32[2,384,384]{2,1,0:T(8,128)} %field.1, ...), custom_call_target="tpu_custom_call" | custom-call | tf_op jit(solution)/shard_map/spread/pallas_call | solution.py:562
  20.2 7.3 %gradient_light.1 = (f32[2,512,512]{2,1,0:T(8,128)S(1)}, f32[648,640]{1,0:T(8,128)S(1)}) custom-call(s32[9,8,128]{2,1,0:T(8,128)S(1)} %get-tuple-element.18.refs_0_, f32[2,512,512]{2,1,0:T(8,128)S(1)} %get-tuple-element.19.refs_1_.field, f32[12,2,128,128]{3,2,1,0:T(8,128)S(1)} %get-tuple-element.20.refs_2_, ...), custom_call_target="tpu_custom_call", output_to_operand_aliasing={{0}: (5, {}), {1}: (7, {})} | custom-call | tf_op jit(solution)/shard_map/gradient_light/pallas_call | solution.py:583
  27.5 29.0 %between.1 = (f32[2,512,512]{2,1,0:T(8,128)S(1)}, f32[2,512,512]{2,1,0:T(8,128)S(1)}, f32[384,384]{1,0:T(8,128)S(1)}) custom-call(f32[2,512,512]{2,1,0:T(8,128)S(1)} %get-tuple-element.26.update, f32[648,640]{1,0:T(8,128)S(1)} %get-tuple-element.27.light, f32[2,512,512]{2,1,0:T(8,128)S(1)} %get-tuple-element.19.refs_1_.field), custom_call_target="tpu_custom_call" | custom-call | tf_op jit(solution)/shard_map/between/pallas_call | solution.py:592
  56.5 4.9 %gradient.1.update = f32[2,512,512]{2,1,0:T(8,128)S(1)} custom-call(s32[9,8,128]{2,1,0:T(8,128)S(1)} %get-tuple-element.18.refs_0_, f32[2,512,512]{2,1,0:T(8,128)S(1)} %get-tuple-element.28.refs_1_.ext, f32[12,2,128,128]{3,2,1,0:T(8,128)S(1)} %get-tuple-element.20.refs_2_, ...), custom_call_target="tpu_custom_call", output_to_operand_aliasing={{}: (5, {})} | custom-call | tf_op jit(solution)/shard_map/gradient/pallas_call | solution.py:601
  61.4 17.7 %last.1 = f32[2,384,384]{2,1,0:T(8,128)S(1)} custom-call(f32[2,512,512]{2,1,0:T(8,128)S(1)} %gradient.1.update, f32[384,384]{1,0:T(8,128)S(1)} %get-tuple-element.30.inverse, f32[2,512,512]{2,1,0:T(8,128)S(1)} %get-tuple-element.28.refs_1_.ext), custom_call_target="tpu_custom_call" | custom-call | tf_op jit(solution)/shard_map/last/pallas_call | solution.py:610
  79.1 1.0 %copy.15 = f32[2,384,384]{2,1,0:T(8,128)} copy(f32[2,384,384]{2,1,0:T(8,128)S(1)} %last.1) | data formatting | bytes 2359296

commit v4 on v3

--- a/solution.py
+++ b/solution.py
@@ -15,7 +15,8 @@
 HBM = pl.BlockSpec(memory_space=pltpu.MemorySpace.HBM)
 LIMIT = 24 << 20
 GROUP = 6
-NEAR, FAR, LEFT, RIGHT, FAR_LEFT, FAR_RIGHT, LEFT_NEXT, RIGHT_NEXT, RELAY = range(9)
+NEAR, FAR, LEFT, RIGHT, FAR_LEFT, FAR_RIGHT, LEFT_NEXT, RIGHT_NEXT, RELAY, EDGE_LEFT, EDGE_RIGHT = range(11)
+DIAGONAL = (FAR_LEFT, FAR_RIGHT, EDGE_LEFT, EDGE_RIGHT)
 
 
 def dft_tables(length):
@@ -61,21 +62,24 @@
         far = (self.far_row >= 0) & (self.far_row < grid[0])
         left, right = self.col > 0, self.col < grid[1] - 1
         self.far, self.left, self.right = far, left, right
-        both = (None, far, left, right, far & left, far & right, left, right, None)
+        ends = (far & jnp.logical_not(left), far & jnp.logical_not(right))
+        both = (None, far, left, right, far & left, far & right, left, right, None) + ends
         self.sends = both
-        self.gets = tuple(both[i] for i in (NEAR, FAR, RIGHT, LEFT, FAR_RIGHT, FAR_LEFT, RIGHT_NEXT, LEFT_NEXT, RELAY))
+        order = (NEAR, FAR, RIGHT, LEFT, FAR_RIGHT, FAR_LEFT, RIGHT_NEXT, LEFT_NEXT, RELAY, EDGE_LEFT, EDGE_RIGHT)
+        self.gets = tuple(both[i] for i in order)
         self.near_border = self.pick(320, 0)
         self.far_border = self.pick(0, 320)
         self.near_halo = self.pick(448, 0)
         self.far_halo = self.pick(0, 448)
-        self.first = self.pick(256, 0)
-        self.rest = self.pick(0, 128)
+        self.near_part = self.pick(256, 0)
+        self.far_part = self.pick(0, 256)
 
     def pick(self, even, odd):
         return pl.multiple_of(even + self.odd * (odd - even), 64)
 
     def target(self, which):
-        row = {NEAR: self.near_row, RELAY: self.near_row, FAR: self.far_row, FAR_LEFT: self.far_row, FAR_RIGHT: self.far_row}
+        row = {NEAR: self.near_row, RELAY: self.near_row, FAR: self.far_row}
+        row.update({which: self.far_row for which in DIAGONAL})
         side = {LEFT: -1, FAR_LEFT: -1, LEFT_NEXT: -1, RIGHT: 1, FAR_RIGHT: 1, RIGHT_NEXT: 1}
         return {"row": row.get(which, self.row), "col": self.col + side.get(which, 0)}
 
@@ -144,38 +148,43 @@
         when(place.sends[i], copy.wait_send)
 
 
-def strips(side, side_in, corner, corner_in, p):
+def strips(far, far_in, side, side_in, corner, corner_in, p):
     return {
+        FAR: (far.at[p], far_in.at[p]),
         FAR_LEFT: (corner.at[0, p], corner_in.at[0, p]),
         FAR_RIGHT: (corner.at[1, p], corner_in.at[1, p]),
-        LEFT: (side.at[0, p, 0:64], side_in.at[0, p, 0:64]),
-        RIGHT: (side.at[1, p, 0:64], side_in.at[1, p, 0:64]),
-        LEFT_NEXT: (side.at[0, p, 64:192], side_in.at[0, p, 64:192]),
-        RIGHT_NEXT: (side.at[1, p, 64:192], side_in.at[1, p, 64:192]),
+        EDGE_LEFT: (corner.at[0, p], corner_in.at[1, p]),
+        EDGE_RIGHT: (corner.at[1, p], corner_in.at[0, p]),
+        LEFT: (side.at[0, p, 0:128], side_in.at[0, p, 0:128]),
+        RIGHT: (side.at[1, p, 0:128], side_in.at[1, p, 0:128]),
+        LEFT_NEXT: (side.at[0, p, 128:192], side_in.at[0, p, 128:192]),
+        RIGHT_NEXT: (side.at[1, p, 128:192], side_in.at[1, p, 128:192]),
     }
 
 
+def at_rows(first, rows):
+    return pl.ds(pl.multiple_of(first, 64), rows)
+
+
 class Halo:
-    def __init__(self, place, ext, side, corner, side_in, corner_in, sems):
-        self.place, self.ext = place, ext
+    def __init__(self, place, ext, far, side, corner, far_in, side_in, corner_in, sems):
+        self.place, self.ext, self.far, self.far_in = place, ext, far, far_in
         self.side, self.corner, self.side_in, self.corner_in = side, corner, side_in, corner_in
+        near, target = at_rows(place.near_border + 64, 64), at_rows(place.far_halo, 64)
         self.copies = []
         for p in range(2):
-            ends = strips(side, side_in, corner, corner_in, p)
-            rows = lambda first: pl.ds(first, 64)
-            inner = lambda first: pl.ds(pl.multiple_of(first + 64, 64), 64)
-            ends[NEAR] = (ext.at[p, inner(place.near_border), 0:384], ext.at[p, rows(place.far_halo), 0:384])
-            ends[FAR] = (ext.at[p, inner(place.far_border), 0:384], ext.at[p, rows(place.near_halo), 0:384])
-            ends[RELAY] = (ext.at[p, inner(place.near_border), 384:512], ext.at[p, rows(place.far_halo), 384:512])
-            self.copies.append([remote(place, i, *ends[i], sems, p) for i in range(9)])
+            ends = strips(far, far_in, side, side_in, corner, corner_in, p)
+            ends[NEAR] = (ext.at[p, near, 0:384], ext.at[p, target, 0:384])
+            ends[RELAY] = (ext.at[p, near, 384:512], ext.at[p, target, 384:512])
+            self.copies.append([remote(place, i, *ends[i], sems, p) for i in range(11)])
 
     def clear(self):
-        place, ext = self.place, self.ext
+        place = self.place
 
         @pl.when(jnp.logical_not(place.far))
         def _():
-            for p in range(2):
-                ext[p, pl.ds(place.far_halo, 64), 0:384] = jnp.zeros((64, 384), jnp.float32)
+            self.far_in[...] = jnp.zeros((2, 64, 256), jnp.float32)
+            self.corner_in[...] = jnp.zeros((2, 2, 64, 128), jnp.float32)
 
         for k, side in enumerate((place.right, place.left)):
 
@@ -183,103 +192,129 @@
             def _():
                 self.side_in[k] = jnp.zeros((2, 192, 128), jnp.float32)
 
-            @pl.when(jnp.logical_not(side & place.far))
-            def _():
-                self.corner_in[k] = jnp.zeros((2, 32, 128), jnp.float32)
-
     def pack(self, p):
         place, ext = self.place, self.ext
         for k, lane in enumerate((0, 256)):
-            take = lambda first, rows: ext[p, pl.ds(pl.multiple_of(first + 64, 64), rows), lane : lane + 128]
-            self.side[k, p, 0:64] = pack(take(place.first, 128), k == 0)
-            self.side[k, p, 64:192] = pack(take(place.rest, 256), k == 0)
-            self.corner[k, p] = pack(take(place.far_border, 64), k == 0)
+            for i, first in enumerate((place.near_part, place.far_part, 128)):
+                self.side[k, p, 64 * i : 64 * i + 64] = pack(ext[p, at_rows(first + 64, 128), lane : lane + 128], k == 0)
+        rows = at_rows(place.far_border + 64, 64)
+        self.far[p, :, 0:128] = ext[p, rows, 128:256]
+        self.far[p, :, 128:256] = jnp.where(lower(64), ext[p, rows, 256:384], ext[p, rows, 0:128])
 
     def start(self, p):
-        start(self.place, self.copies[p], LEFT, RIGHT, FAR, NEAR, FAR_LEFT, FAR_RIGHT, LEFT_NEXT, RIGHT_NEXT)
+        start(self.place, self.copies[p], LEFT, RIGHT, FAR, NEAR, LEFT_NEXT, RIGHT_NEXT)
 
     def finish(self):
-        place, ext = self.place, self.ext
+        place, ext, low = self.place, self.ext, lower(64)
         for p in range(2):
             wait_recv(place, self.copies[p], LEFT, RIGHT)
-            rows = pl.ds(pl.multiple_of(place.first + 64, 64), 128)
-            ext[p, rows, 384:512] = merge(self.side_in[0, p, 0:64], self.side_in[1, p, 0:64])
+            for i, first in enumerate((place.near_part, place.far_part)):
+                parts = [self.side_in[k, p, 64 * i : 64 * i + 64] for k in range(2)]
+                ext[p, at_rows(first + 64, 128), 384:512] = merge(*parts)
             start(place, self.copies[p], RELAY)
-            wait_recv(place, self.copies[p], FAR_LEFT, FAR_RIGHT, LEFT_NEXT, RIGHT_NEXT)
-            ext[p, pl.ds(place.far_halo, 64), 384:512] = merge(self.corner_in[0, p], self.corner_in[1, p])
-            rows = pl.ds(pl.multiple_of(place.rest + 64, 64), 256)
-            ext[p, rows, 384:512] = merge(self.side_in[0, p, 64:192], self.side_in[1, p, 64:192])
-        for p in range(2):
-            wait_recv(place, self.copies[p], FAR, NEAR, RELAY)
+            rows = at_rows(place.far_border + 64, 64)
+            self.corner[0, p] = jnp.where(low, ext[p, rows, 0:128], ext[p, rows, 384:512])
+            self.corner[1, p] = jnp.where(low, ext[p, rows, 384:512], ext[p, rows, 256:384])
+            start(place, self.copies[p], *DIAGONAL)
+        for p in range(2):
+            wait_recv(place, self.copies[p], LEFT_NEXT, RIGHT_NEXT)
+            ext[p, 192:320, 384:512] = merge(self.side_in[0, p, 128:192], self.side_in[1, p, 128:192])
+            wait_recv(place, self.copies[p], FAR, *DIAGONAL)
+            rows = at_rows(place.far_halo, 64)
+            right, left = self.corner_in[0, p], self.corner_in[1, p]
+            mixed = self.far_in[p, :, 128:256]
+            ext[p, rows, 0:128] = jnp.where(low, left, mixed)
+            ext[p, rows, 128:256] = self.far_in[p, :, 0:128]
+            ext[p, rows, 256:384] = jnp.where(low, mixed, right)
+            ext[p, rows, 384:512] = jnp.where(low, right, left)
+        for p in range(2):
+            wait_recv(place, self.copies[p], NEAR, RELAY)
             wait_send(place, self.copies[p])
 
 
 class Fold:
-    def __init__(self, place, update, ends_in, near_in, side, corner, side_in, corner_in, sems):
-        self.place, self.update, self.ends_in, self.near_in = place, update, ends_in, near_in
+    def __init__(self, place, update, near_in, relay_in, far, side, corner, far_in, side_in, corner_in, sems):
+        self.place, self.update, self.near_in, self.relay_in = place, update, near_in, relay_in
+        self.far, self.far_in = far, far_in
         self.side, self.corner, self.side_in, self.corner_in = side, corner, side_in, corner_in
+        near = at_rows(place.near_halo, 64)
         self.copies = []
         for p in range(2):
-            ends = strips(side, side_in, corner, corner_in, p)
-            ends[NEAR] = (update.at[p, pl.ds(place.near_halo, 64), 0:384], ends_in.at[0, p])
-            ends[FAR] = (update.at[p, pl.ds(place.far_halo, 64), 0:384], ends_in.at[1, p])
-            ends[RELAY] = (update.at[p, pl.ds(place.near_halo, 64), 384:512], near_in.at[p])
-            self.copies.append([remote(place, i, *ends[i], sems, p) for i in range(9)])
-
-    def take(self, p, first, rows):
-        return self.update[p, pl.ds(pl.multiple_of(first + 64, 64), rows), 384:512]
+            ends = strips(far, far_in, side, side_in, corner, corner_in, p)
+            ends[NEAR] = (update.at[p, near, 0:384], near_in.at[p])
+            ends[RELAY] = (update.at[p, near, 384:512], relay_in.at[p])
+            self.copies.append([remote(place, i, *ends[i], sems, p) for i in range(11)])
 
     def pack(self):
-        place = self.place
-        for p in range(2):
+        place, update, low = self.place, self.update, lower(64)
+
+        @pl.when(jnp.logical_not(place.far))
+        def _():
+            self.corner_in[...] = jnp.zeros((2, 2, 64, 128), jnp.float32)
+
+        rows = at_rows(place.far_halo, 64)
+        for p in range(2):
+            tiles = [update[p, rows, 128 * t : 128 * t + 128] for t in range(4)]
+            self.corner[0, p] = jnp.where(low, tiles[0], tiles[3])
+            self.corner[1, p] = jnp.where(low, tiles[3], tiles[2])
+            self.far[p, :, 0:128] = tiles[1]
+            self.far[p, :, 128:256] = jnp.where(low, tiles[2], tiles[0])
             for k in range(2):
-                self.side[k, p, 64:192] = pack(self.take(p, place.rest, 256), k == 1)
-                self.corner[k, p] = pack(self.update[p, pl.ds(place.far_halo, 64), 384:512], k == 1)
+                self.side[k, p, 128:192] = pack(update[p, 192:320, 384:512], k == 1)
 
     def start(self):
-        place = self.place
+        place, update = self.place, self.update
         odd = place.odd.astype(jnp.float32)
         for p in range(2):
-            start(place, self.copies[p], RELAY)
-        for p in range(2):
-            start(place, self.copies[p], FAR, NEAR, FAR_LEFT, FAR_RIGHT, LEFT_NEXT, RIGHT_NEXT)
-            wait_recv(place, self.copies[p], RELAY)
-            part = self.take(p, place.first, 128)
-            near = self.near_in[p]
-            part = jnp.concatenate([part[:64] + near * odd, part[64:] + near * (1.0 - odd)], axis=0)
-            for k in range(2):
-                self.side[k, p, 0:64] = pack(part, k == 1)
+            start(place, self.copies[p], *DIAGONAL, RELAY)
+        start(place, self.copies[0], FAR, LEFT_NEXT, RIGHT_NEXT, NEAR)
+        start(place, self.copies[1], FAR)
+        for p in range(2):
+            wait_recv(place, self.copies[p], RELAY, *DIAGONAL)
+            extra = (self.relay_in[p], jnp.where(lower(64), self.corner_in[0, p], self.corner_in[1, p]))
+            for i, first in enumerate((place.near_part, place.far_part)):
+                part = update[p, at_rows(first + 64, 128), 384:512]
+                here = odd if i == 0 else 1.0 - odd
+                part = jnp.concatenate([part[:64] + extra[i] * here, part[64:] + extra[i] * (1.0 - here)], axis=0)
+                for k in range(2):
+                    self.side[k, p, 64 * i : 64 * i + 64] = pack(part, k == 1)
             start(place, self.copies[p], LEFT, RIGHT)
+            if p == 0:
+                start(place, self.copies[1], LEFT_NEXT, RIGHT_NEXT, NEAR)
 
     def finish(self, p, dest, base, inverse):
         place = self.place
 
         def add(first, lane, value):
             lanes, rows = pl.ds(lane, value.shape[1]), value.shape[0]
-            at = pl.ds(pl.multiple_of(first + base, 64), rows)
-            dest[p, at, lanes] += value * inverse[pl.ds(pl.multiple_of(first, 64), rows), lanes]
-
-        def side(k, value):
-            keep = ~lower(value.shape[0]) if k == 0 else lower(value.shape[0])
-            return 256 if k == 0 else 0, jnp.where(keep, value, 0.0)
-
-        for i in (FAR, NEAR, FAR_LEFT, FAR_RIGHT, LEFT_NEXT, RIGHT_NEXT, LEFT, RIGHT):
-
-            def body():
-                self.copies[p][i].wait_recv()
-                k = i % 2
-                if i == NEAR:
-                    add(place.near_border, 0, self.ends_in[0, p])
-                elif i == FAR:
-                    add(place.far_border, 0, self.ends_in[1, p])
-                elif i in (FAR_LEFT, FAR_RIGHT):
-                    add(place.far_border, *side(k, unpack(self.corner_in[k, p])))
-                elif i in (LEFT, RIGHT):
-                    add(place.first, *side(k, unpack(self.side_in[k, p, 0:64])))
-                else:
-                    add(place.rest, *side(k, unpack(self.side_in[k, p, 64:192])))
-
-            when(place.gets[i], body)
+            dest[p, at_rows(first + base, rows), lanes] += value * inverse[at_rows(first, rows), lanes]
+
+        def lowest(value):
+            return jnp.where(lower(value.shape[0]), value, 0.0)
+
+        def highest(value):
+            return jnp.where(lower(value.shape[0]), 0.0, value)
+
+        wait_recv(place, self.copies[p], NEAR)
+        add(place.near_border, 0, self.near_in[p])
+
+        @pl.when(place.far)
+        def _():
+            self.copies[p][FAR].wait_recv()
+            mixed = self.far_in[p, :, 128:256]
+            add(place.far_border, 0, jnp.where(lower(64), self.corner_in[1, p], mixed))
+            add(place.far_border, 128, self.far_in[p, :, 0:128])
+            add(place.far_border, 256, jnp.where(lower(64), mixed, self.corner_in[0, p]))
+
+        for k, (here, lane, keep) in enumerate(((place.right, 256, highest), (place.left, 0, lowest))):
+
+            @pl.when(here)
+            def _():
+                self.copies[p][LEFT_NEXT + k].wait_recv()
+                add(128, lane, keep(unpack(self.side_in[k, p, 128:192])))
+                self.copies[p][LEFT + k].wait_recv()
+                add(place.near_part, lane, keep(unpack(self.side_in[k, p, 0:64])))
+                add(place.far_part, lane, keep(unpack(self.side_in[k, p, 64:128])))
 
     def close(self):
         for p in range(2):
@@ -290,7 +325,7 @@
     def kernel(
         field, offsets, counts, places, measured, tables, probe,
         ext, around, measured_here, tables_here, beams, power, update, light,
-        mine, offsets_here, tall, side, corner, side_in, corner_in, sems, notes, local,
+        mine, offsets_here, tall, far, side, corner, far_in, side_in, corner_in, sems, notes, local,
     ):
         place = Place(grid)
         peers = greet_all(place)
@@ -303,7 +338,7 @@
         pulls.append(pltpu.make_async_copy(probe, tall.at[:, 8:136], local.at[5]))
         for pull in pulls:
             pull.start()
-        halo = Halo(place, ext, side, corner, side_in, corner_in, sems)
+        halo = Halo(place, ext, far, side, corner, far_in, side_in, corner_in, sems)
         halo.clear()
         for i, d in enumerate(AROUND):
 
@@ -499,13 +534,13 @@
     def kernel(
         update, light, field,
         ext, cleared, inverse,
-        ends_in, near_in, side, corner, side_in, corner_in, sems,
-        halo_side, halo_corner, halo_side_in, halo_corner_in, more,
+        near_in, relay_in, far, side, corner, far_in, side_in, corner_in, sems,
+        halo_far, halo_side, halo_corner, halo_far_in, halo_side_in, halo_corner_in, more,
     ):
         place = Place(grid)
         greet(place)
-        fold = Fold(place, update, ends_in, near_in, side, corner, side_in, corner_in, sems)
-        halo = Halo(place, ext, halo_side, halo_corner, halo_side_in, halo_corner_in, more)
+        fold = Fold(place, update, near_in, relay_in, far, side, corner, far_in, side_in, corner_in, sems)
+        halo = Halo(place, ext, halo_far, halo_side, halo_corner, halo_far_in, halo_side_in, halo_corner_in, more)
         fold.pack()
         greeted(place)
         fold.start()
@@ -525,10 +560,10 @@
 
 
 def last_kernel(grid):
-    def kernel(update, inverse, ext, out, ends_in, near_in, side, corner, side_in, corner_in, sems):
+    def kernel(update, inverse, ext, out, near_in, relay_in, far, side, corner, far_in, side_in, corner_in, sems):
         place = Place(grid)
         greet(place)
-        fold = Fold(place, update, ends_in, near_in, side, corner, side_in, corner_in, sems)
+        fold = Fold(place, update, near_in, relay_in, far, side, corner, far_in, side_in, corner_in, sems)
         fold.pack()
         greeted(place)
         fold.start()
@@ -556,9 +591,9 @@
     shape = jax.ShapeDtypeStruct
     ext_shape, light_shape = shape((2, 512, 512), f32), shape((648, 640), f32)
     offsets = jnp.swapaxes(offsets, 2, 3)
-    packs = [pltpu.VMEM((2, 2, 192, 128), f32), pltpu.VMEM((2, 2, 32, 128), f32)]
-    folds = [pltpu.VMEM((2, 2, 64, 384), f32), pltpu.VMEM((2, 64, 128), f32)] + packs + packs
-    sems = pltpu.SemaphoreType.DMA((2, 2, 9))
+    packs = [pltpu.VMEM((2, 64, 256), f32), pltpu.VMEM((2, 2, 192, 128), f32), pltpu.VMEM((2, 2, 64, 128), f32)]
+    folds = [pltpu.VMEM((2, 64, 384), f32), pltpu.VMEM((2, 64, 128), f32)] + packs + packs
+    sems = pltpu.SemaphoreType.DMA((2, 2, 11))
     ext, around, measured, tables, beams, power, update, light = pl.pallas_call(
         spread_kernel(grid),
         name="spread",

time: 79.8 us -> 83.5 us (1.046)
  the two profiles are of different devices: /device:TPU:107 before, /device:TPU:109 now
where the time goes in v4:
time: 83.5 us; the launch traced here: 84.3 us
  Pallas kernels  82.6 us (99%)
  local copies, waits for them, and re-layouts  1.02 us (1%)
    pallas_call x1, Pallas kernels, shards(): pl.pallas_call(between_kernel(grid), name='between', out_shape=(ext_shape...  29.9 us
    pallas_call x1, Pallas kernels, shards(): pl.pallas_call(spread_kernel(grid), name='spread', out_shape=(ext_shape,...  22.4 us
    pallas_call x1, Pallas kernels, shards(): pl.pallas_call(last_kernel(grid), name='last', out_shape=shape((2, 384, 3...  19.7 us
    pallas_call x1, Pallas kernels, shards(): pl.pallas_call(gradient_kernel(True), name='gradient_light', out_shape=(e...  5.71 us
    pallas_call x1, Pallas kernels, shards(): pl.pallas_call(gradient_kernel(False), name='gradient', out_shape=ext_sha...  4.91 us

profile of v4, /device:TPU:109, one launch (start us, length us, event | category | flops | bytes accessed | tf_op | source)
XLA Modules:
  0.0 84.3 jit_solution(12503605551235340833)
XLA Ops:
  0.7 22.4 %spread.1 = (f32[2,512,512]{2,1,0:T(8,128)S(1)}, s32[9,8,128]{2,1,0:T(8,128)S(1)}, f32[1,1,12,128,128]{4,3,2,1,0:T(8,128)S(1)}, bf16[4,256,256]{2,1,0:T(8,128)(2...) custom-call(f32[2,384,384]{2,1,0:T(8,128)} %field.1, ...), custom_call_target="tpu_custom_call" | custom-call | tf_op jit(solution)/shard_map/spread/pallas_call | solution.py:597
  23.0 5.7 %gradient_light.1 = (f32[2,512,512]{2,1,0:T(8,128)S(1)}, f32[648,640]{1,0:T(8,128)S(1)}) custom-call(s32[9,8,128]{2,1,0:T(8,128)S(1)} %get-tuple-element.18.refs_0_, f32[2,512,512]{2,1,0:T(8,128)S(1)} %get-tuple-element.19.refs_1_.field, f32[12,2,128,128]{3,2,1,0:T(8,128)S(1)} %get-tuple-element.20.refs_2_, ...), custom_call_target="tpu_custom_call", output_to_operand_aliasing={{0}: (5, {}), {1}: (7, {})} | custom-call | tf_op jit(solution)/shard_map/gradient_light/pallas_call | solution.py:618
  28.8 29.9 %between.1 = (f32[2,512,512]{2,1,0:T(8,128)S(1)}, f32[2,512,512]{2,1,0:T(8,128)S(1)}, f32[384,384]{1,0:T(8,128)S(1)}) custom-call(f32[2,512,512]{2,1,0:T(8,128)S(1)} %get-tuple-element.26.update, f32[648,640]{1,0:T(8,128)S(1)} %get-tuple-element.27.light, f32[2,512,512]{2,1,0:T(8,128)S(1)} %get-tuple-element.19.refs_1_.field), custom_call_target="tpu_custom_call" | custom-call | tf_op jit(solution)/shard_map/between/pallas_call | solution.py:627
  58.7 4.9 %gradient.1.update = f32[2,512,512]{2,1,0:T(8,128)S(1)} custom-call(s32[9,8,128]{2,1,0:T(8,128)S(1)} %get-tuple-element.18.refs_0_, f32[2,512,512]{2,1,0:T(8,128)S(1)} %get-tuple-element.28.refs_1_.ext, f32[12,2,128,128]{3,2,1,0:T(8,128)S(1)} %get-tuple-element.20.refs_2_, ...), custom_call_target="tpu_custom_call", output_to_operand_aliasing={{}: (5, {})} | custom-call | tf_op jit(solution)/shard_map/gradient/pallas_call | solution.py:636
  63.6 19.7 %last.1 = f32[2,384,384]{2,1,0:T(8,128)S(1)} custom-call(f32[2,512,512]{2,1,0:T(8,128)S(1)} %gradient.1.update, f32[384,384]{1,0:T(8,128)S(1)} %get-tuple-element.30.inverse, f32[2,512,512]{2,1,0:T(8,128)S(1)} %get-tuple-element.28.refs_1_.ext), custom_call_target="tpu_custom_call" | custom-call | tf_op jit(solution)/shard_map/last/pallas_call | solution.py:645
  83.3 1.0 %copy.15 = f32[2,384,384]{2,1,0:T(8,128)} copy(f32[2,384,384]{2,1,0:T(8,128)S(1)} %last.1) | data formatting | bytes 2359296

commit v5 on v4

--- a/solution.py
+++ b/solution.py
@@ -202,7 +202,11 @@
         self.far[p, :, 128:256] = jnp.where(lower(64), ext[p, rows, 256:384], ext[p, rows, 0:128])
 
     def start(self, p):
-        start(self.place, self.copies[p], LEFT, RIGHT, FAR, NEAR, LEFT_NEXT, RIGHT_NEXT)
+        start(self.place, self.copies[p], LEFT, RIGHT, FAR)
+
+    def start_rest(self):
+        for p in range(2):
+            start(self.place, self.copies[p], LEFT_NEXT, RIGHT_NEXT, NEAR)
 
     def finish(self):
         place, ext, low = self.place, self.ext, lower(64)
@@ -266,9 +270,9 @@
         place, update = self.place, self.update
         odd = place.odd.astype(jnp.float32)
         for p in range(2):
-            start(place, self.copies[p], *DIAGONAL, RELAY)
-        start(place, self.copies[0], FAR, LEFT_NEXT, RIGHT_NEXT, NEAR)
-        start(place, self.copies[1], FAR)
+            start(place, self.copies[p], *DIAGONAL, RELAY, FAR, LEFT_NEXT, RIGHT_NEXT)
+        for p in range(2):
+            start(place, self.copies[p], NEAR)
         for p in range(2):
             wait_recv(place, self.copies[p], RELAY, *DIAGONAL)
             extra = (self.relay_in[p], jnp.where(lower(64), self.corner_in[0, p], self.corner_in[1, p]))
@@ -279,8 +283,6 @@
                 for k in range(2):
                     self.side[k, p, 64 * i : 64 * i + 64] = pack(part, k == 1)
             start(place, self.copies[p], LEFT, RIGHT)
-            if p == 0:
-                start(place, self.copies[1], LEFT_NEXT, RIGHT_NEXT, NEAR)
 
     def finish(self, p, dest, base, inverse):
         place = self.place
@@ -370,6 +372,7 @@
         pulls[2].wait()
         halo.pack(1)
         halo.start(1)
+        halo.start_rest()
         for pull in later:
             pull.start()
         update[...] = jnp.zeros_like(update)
@@ -553,6 +556,7 @@
             fold.finish(p, ext, 64, inverse)
             halo.pack(p)
             halo.start(p)
+        halo.start_rest()
         halo.finish()
         fold.close()
 

time: 83.5 us -> 80.8 us (0.968)
  the two profiles are of different devices: /device:TPU:109 before, /device:TPU:11 now
where the time goes in v5:
time: 80.8 us; the launch traced here: 80.7 us
  Pallas kernels  79 us (98%)
  local copies, waits for them, and re-layouts  1.02 us (1%)
    pallas_call x1, Pallas kernels, shards(): pl.pallas_call(between_kernel(grid), name='between', out_shape=(ext_shape...  31.6 us
    pallas_call x1, Pallas kernels, shards(): pl.pallas_call(spread_kernel(grid), name='spread', out_shape=(ext_shape,...  21.1 us
    pallas_call x1, Pallas kernels, shards(): pl.pallas_call(last_kernel(grid), name='last', out_shape=shape((2, 384, 3...  15.4 us
    pallas_call x1, Pallas kernels, shards(): pl.pallas_call(gradient_kernel(True), name='gradient_light', out_shape=(e...  5.85 us
    pallas_call x1, Pallas kernels, shards(): pl.pallas_call(gradient_kernel(False), name='gradient', out_shape=ext_sha...  4.92 us

profile of v5, /device:TPU:11, one launch (start us, length us, event | category | flops | bytes accessed | tf_op | source)
XLA Modules:
  0.0 80.7 jit_solution(3173001267359497547)
XLA Ops:
  0.7 21.1 %spread.1 = (f32[2,512,512]{2,1,0:T(8,128)S(1)}, s32[9,8,128]{2,1,0:T(8,128)S(1)}, f32[1,1,12,128,128]{4,3,2,1,0:T(8,128)S(1)}, bf16[4,256,256]{2,1,0:T(8,128)(2...) custom-call(f32[2,384,384]{2,1,0:T(8,128)} %field.1, ...), custom_call_target="tpu_custom_call" | custom-call | tf_op jit(solution)/shard_map/spread/pallas_call | solution.py:601
  21.8 5.9 %gradient_light.1 = (f32[2,512,512]{2,1,0:T(8,128)S(1)}, f32[648,640]{1,0:T(8,128)S(1)}) custom-call(s32[9,8,128]{2,1,0:T(8,128)S(1)} %get-tuple-element.18.refs_0_, f32[2,512,512]{2,1,0:T(8,128)S(1)} %get-tuple-element.19.refs_1_.field, f32[12,2,128,128]{3,2,1,0:T(8,128)S(1)} %get-tuple-element.20.refs_2_, ...), custom_call_target="tpu_custom_call", output_to_operand_aliasing={{0}: (5, {}), {1}: (7, {})} | custom-call | tf_op jit(solution)/shard_map/gradient_light/pallas_call | solution.py:622
  27.7 31.6 %between.1 = (f32[2,512,512]{2,1,0:T(8,128)S(1)}, f32[2,512,512]{2,1,0:T(8,128)S(1)}, f32[384,384]{1,0:T(8,128)S(1)}) custom-call(f32[2,512,512]{2,1,0:T(8,128)S(1)} %get-tuple-element.26.update, f32[648,640]{1,0:T(8,128)S(1)} %get-tuple-element.27.light, f32[2,512,512]{2,1,0:T(8,128)S(1)} %get-tuple-element.19.refs_1_.field), custom_call_target="tpu_custom_call" | custom-call | tf_op jit(solution)/shard_map/between/pallas_call | solution.py:631
  59.3 4.9 %gradient.1.update = f32[2,512,512]{2,1,0:T(8,128)S(1)} custom-call(s32[9,8,128]{2,1,0:T(8,128)S(1)} %get-tuple-element.18.refs_0_, f32[2,512,512]{2,1,0:T(8,128)S(1)} %get-tuple-element.28.refs_1_.ext, f32[12,2,128,128]{3,2,1,0:T(8,128)S(1)} %get-tuple-element.20.refs_2_, ...), custom_call_target="tpu_custom_call", output_to_operand_aliasing={{}: (5, {})} | custom-call | tf_op jit(solution)/shard_map/gradient/pallas_call | solution.py:640
  64.2 15.4 %last.1 = f32[2,384,384]{2,1,0:T(8,128)S(1)} custom-call(f32[2,512,512]{2,1,0:T(8,128)S(1)} %gradient.1.update, f32[384,384]{1,0:T(8,128)S(1)} %get-tuple-element.30.inverse, f32[2,512,512]{2,1,0:T(8,128)S(1)} %get-tuple-element.28.refs_1_.ext), custom_call_target="tpu_custom_call" | custom-call | tf_op jit(solution)/shard_map/last/pallas_call | solution.py:649
  79.7 1.0 %copy.15 = f32[2,384,384]{2,1,0:T(8,128)} copy(f32[2,384,384]{2,1,0:T(8,128)S(1)} %last.1) | data formatting | bytes 2359296

commit v6 on v5

--- a/solution.py
+++ b/solution.py
@@ -71,8 +71,6 @@
         self.far_border = self.pick(0, 320)
         self.near_halo = self.pick(448, 0)
         self.far_halo = self.pick(0, 448)
-        self.near_part = self.pick(256, 0)
-        self.far_part = self.pick(0, 256)
 
     def pick(self, even, odd):
         return pl.multiple_of(even + self.odd * (odd - even), 64)
@@ -155,10 +153,10 @@
         FAR_RIGHT: (corner.at[1, p], corner_in.at[1, p]),
         EDGE_LEFT: (corner.at[0, p], corner_in.at[1, p]),
         EDGE_RIGHT: (corner.at[1, p], corner_in.at[0, p]),
-        LEFT: (side.at[0, p, 0:128], side_in.at[0, p, 0:128]),
-        RIGHT: (side.at[1, p, 0:128], side_in.at[1, p, 0:128]),
-        LEFT_NEXT: (side.at[0, p, 128:192], side_in.at[0, p, 128:192]),
-        RIGHT_NEXT: (side.at[1, p, 128:192], side_in.at[1, p, 128:192]),
+        LEFT: (side.at[0, p, 0:64], side_in.at[0, p, 0:64]),
+        RIGHT: (side.at[1, p, 0:64], side_in.at[1, p, 0:64]),
+        LEFT_NEXT: (side.at[0, p, 64:192], side_in.at[0, p, 64:192]),
+        RIGHT_NEXT: (side.at[1, p, 64:192], side_in.at[1, p, 64:192]),
     }
 
 
@@ -195,8 +193,9 @@
     def pack(self, p):
         place, ext = self.place, self.ext
         for k, lane in enumerate((0, 256)):
-            for i, first in enumerate((place.near_part, place.far_part, 128)):
-                self.side[k, p, 64 * i : 64 * i + 64] = pack(ext[p, at_rows(first + 64, 128), lane : lane + 128], k == 0)
+            for i, first in enumerate((place.near_border, place.far_border)):
+                self.side[k, p, 32 * i : 32 * i + 32] = pack(ext[p, at_rows(first + 64, 64), lane : lane + 128], k == 0)
+            self.side[k, p, 64:192] = pack(ext[p, 128:384, lane : lane + 128], k == 0)
         rows = at_rows(place.far_border + 64, 64)
         self.far[p, :, 0:128] = ext[p, rows, 128:256]
         self.far[p, :, 128:256] = jnp.where(lower(64), ext[p, rows, 256:384], ext[p, rows, 0:128])
@@ -212,9 +211,9 @@
         place, ext, low = self.place, self.ext, lower(64)
         for p in range(2):
             wait_recv(place, self.copies[p], LEFT, RIGHT)
-            for i, first in enumerate((place.near_part, place.far_part)):
-                parts = [self.side_in[k, p, 64 * i : 64 * i + 64] for k in range(2)]
-                ext[p, at_rows(first + 64, 128), 384:512] = merge(*parts)
+            for i, first in enumerate((place.near_border, place.far_border)):
+                parts = [self.side_in[k, p, 32 * i : 32 * i + 32] for k in range(2)]
+                ext[p, at_rows(first + 64, 64), 384:512] = merge(*parts)
             start(place, self.copies[p], RELAY)
             rows = at_rows(place.far_border + 64, 64)
             self.corner[0, p] = jnp.where(low, ext[p, rows, 0:128], ext[p, rows, 384:512])
@@ -222,7 +221,7 @@
             start(place, self.copies[p], *DIAGONAL)
         for p in range(2):
             wait_recv(place, self.copies[p], LEFT_NEXT, RIGHT_NEXT)
-            ext[p, 192:320, 384:512] = merge(self.side_in[0, p, 128:192], self.side_in[1, p, 128:192])
+            ext[p, 128:384, 384:512] = merge(self.side_in[0, p, 64:192], self.side_in[1, p, 64:192])
             wait_recv(place, self.copies[p], FAR, *DIAGONAL)
             rows = at_rows(place.far_halo, 64)
             right, left = self.corner_in[0, p], self.corner_in[1, p]
@@ -264,25 +263,27 @@
             self.far[p, :, 0:128] = tiles[1]
             self.far[p, :, 128:256] = jnp.where(low, tiles[2], tiles[0])
             for k in range(2):
-                self.side[k, p, 128:192] = pack(update[p, 192:320, 384:512], k == 1)
+                self.side[k, p, 64:192] = pack(update[p, 128:384, 384:512], k == 1)
 
     def start(self):
         place, update = self.place, self.update
-        odd = place.odd.astype(jnp.float32)
-        for p in range(2):
-            start(place, self.copies[p], *DIAGONAL, RELAY, FAR, LEFT_NEXT, RIGHT_NEXT)
-        for p in range(2):
-            start(place, self.copies[p], NEAR)
+        for p in range(2):
+            start(place, self.copies[p], *DIAGONAL, RELAY)
+            if p == 0:
+                start(place, self.copies[p], FAR, LEFT_NEXT, RIGHT_NEXT)
+        start(place, self.copies[1], FAR)
         for p in range(2):
             wait_recv(place, self.copies[p], RELAY, *DIAGONAL)
             extra = (self.relay_in[p], jnp.where(lower(64), self.corner_in[0, p], self.corner_in[1, p]))
-            for i, first in enumerate((place.near_part, place.far_part)):
-                part = update[p, at_rows(first + 64, 128), 384:512]
-                here = odd if i == 0 else 1.0 - odd
-                part = jnp.concatenate([part[:64] + extra[i] * here, part[64:] + extra[i] * (1.0 - here)], axis=0)
+            for i, first in enumerate((place.near_border, place.far_border)):
+                part = update[p, at_rows(first + 64, 64), 384:512] + extra[i]
                 for k in range(2):
-                    self.side[k, p, 64 * i : 64 * i + 64] = pack(part, k == 1)
+                    self.side[k, p, 32 * i : 32 * i + 32] = pack(part, k == 1)
             start(place, self.copies[p], LEFT, RIGHT)
+            if p == 0:
+                start(place, self.copies[1], LEFT_NEXT, RIGHT_NEXT)
+        for p in range(2):
+            start(place, self.copies[p], NEAR)
 
     def finish(self, p, dest, base, inverse):
         place = self.place
@@ -313,10 +314,10 @@
             @pl.when(here)
             def _():
                 self.copies[p][LEFT_NEXT + k].wait_recv()
-                add(128, lane, keep(unpack(self.side_in[k, p, 128:192])))
+                add(64, lane, keep(unpack(self.side_in[k, p, 64:192])))
                 self.copies[p][LEFT + k].wait_recv()
-                add(place.near_part, lane, keep(unpack(self.side_in[k, p, 0:64])))
-                add(place.far_part, lane, keep(unpack(self.side_in[k, p, 64:128])))
+                add(place.near_border, lane, keep(unpack(self.side_in[k, p, 0:32])))
+                add(place.far_border, lane, keep(unpack(self.side_in[k, p, 32:64])))
 
     def close(self):
         for p in range(2):

time: 80.8 us -> 78.6 us (0.973)
  Pallas kernels: 79 us -> 76 us
    pallas_call x1, Pallas kernels: 31.6 us -> 28.7 us  [shards(): pl.pallas_call(between_kernel(grid), name='between', out_shape=(ext_shape...]
    pallas_call x1, Pallas kernels: 21.1 us -> 19.8 us  [shards(): pl.pallas_call(spread_kernel(grid), name='spread', out_shape=(ext_shape,...]
    pallas_call x1, Pallas kernels: 15.4 us -> 16.6 us  [shards(): pl.pallas_call(last_kernel(grid), name='last', out_shape=shape((2, 384, 3...]
where the time goes in v6:
time: 78.6 us; the launch traced here: 77.7 us
  Pallas kernels  76 us (97%)
  local copies, waits for them, and re-layouts  1.02 us (1%)
    pallas_call x1, Pallas kernels, shards(): pl.pallas_call(between_kernel(grid), name='between', out_shape=(ext_shape...  28.7 us
    pallas_call x1, Pallas kernels, shards(): pl.pallas_call(spread_kernel(grid), name='spread', out_shape=(ext_shape,...  19.8 us
    pallas_call x1, Pallas kernels, shards(): pl.pallas_call(last_kernel(grid), name='last', out_shape=shape((2, 384, 3...  16.6 us
    pallas_call x1, Pallas kernels, shards(): pl.pallas_call(gradient_kernel(True), name='gradient_light', out_shape=(e...  6.11 us
    pallas_call x1, Pallas kernels, shards(): pl.pallas_call(gradient_kernel(False), name='gradient', out_shape=ext_sha...  4.93 us

profile of v6, /device:TPU:11, one launch (start us, length us, event | category | flops | bytes accessed | tf_op | source)
XLA Modules:
  0.0 77.7 jit_solution(14670065555990746794)
XLA Ops:
  0.7 19.8 %spread.1 = (f32[2,512,512]{2,1,0:T(8,128)S(1)}, s32[9,8,128]{2,1,0:T(8,128)S(1)}, f32[1,1,12,128,128]{4,3,2,1,0:T(8,128)S(1)}, bf16[4,256,256]{2,1,0:T(8,128)(2...) custom-call(f32[2,384,384]{2,1,0:T(8,128)} %field.1, ...), custom_call_target="tpu_custom_call" | custom-call | tf_op jit(solution)/shard_map/spread/pallas_call | solution.py:602
  20.4 6.1 %gradient_light.1 = (f32[2,512,512]{2,1,0:T(8,128)S(1)}, f32[648,640]{1,0:T(8,128)S(1)}) custom-call(s32[9,8,128]{2,1,0:T(8,128)S(1)} %get-tuple-element.18.refs_0_, f32[2,512,512]{2,1,0:T(8,128)S(1)} %get-tuple-element.19.refs_1_.field, f32[12,2,128,128]{3,2,1,0:T(8,128)S(1)} %get-tuple-element.20.refs_2_, ...), custom_call_target="tpu_custom_call", output_to_operand_aliasing={{0}: (5, {}), {1}: (7, {})} | custom-call | tf_op jit(solution)/shard_map/gradient_light/pallas_call | solution.py:623
  26.5 28.7 %between.1 = (f32[2,512,512]{2,1,0:T(8,128)S(1)}, f32[2,512,512]{2,1,0:T(8,128)S(1)}, f32[384,384]{1,0:T(8,128)S(1)}) custom-call(f32[2,512,512]{2,1,0:T(8,128)S(1)} %get-tuple-element.26.update, f32[648,640]{1,0:T(8,128)S(1)} %get-tuple-element.27.light, f32[2,512,512]{2,1,0:T(8,128)S(1)} %get-tuple-element.19.refs_1_.field), custom_call_target="tpu_custom_call" | custom-call | tf_op jit(solution)/shard_map/between/pallas_call | solution.py:632
  55.2 4.9 %gradient.1.update = f32[2,512,512]{2,1,0:T(8,128)S(1)} custom-call(s32[9,8,128]{2,1,0:T(8,128)S(1)} %get-tuple-element.18.refs_0_, f32[2,512,512]{2,1,0:T(8,128)S(1)} %get-tuple-element.28.refs_1_.ext, f32[12,2,128,128]{3,2,1,0:T(8,128)S(1)} %get-tuple-element.20.refs_2_, ...), custom_call_target="tpu_custom_call", output_to_operand_aliasing={{}: (5, {})} | custom-call | tf_op jit(solution)/shard_map/gradient/pallas_call | solution.py:641
  60.1 16.6 %last.1 = f32[2,384,384]{2,1,0:T(8,128)S(1)} custom-call(f32[2,512,512]{2,1,0:T(8,128)S(1)} %gradient.1.update, f32[384,384]{1,0:T(8,128)S(1)} %get-tuple-element.30.inverse, f32[2,512,512]{2,1,0:T(8,128)S(1)} %get-tuple-element.28.refs_1_.ext), custom_call_target="tpu_custom_call" | custom-call | tf_op jit(solution)/shard_map/last/pallas_call | solution.py:650
  76.7 1.0 %copy.15 = f32[2,384,384]{2,1,0:T(8,128)} copy(f32[2,384,384]{2,1,0:T(8,128)S(1)} %last.1) | data formatting | bytes 2359296

commit v7 on v6

--- a/solution.py
+++ b/solution.py
@@ -207,7 +207,7 @@
         for p in range(2):
             start(self.place, self.copies[p], LEFT_NEXT, RIGHT_NEXT, NEAR)
 
-    def finish(self):
+    def forward(self):
         place, ext, low = self.place, self.ext, lower(64)
         for p in range(2):
             wait_recv(place, self.copies[p], LEFT, RIGHT)
@@ -219,6 +219,9 @@
             self.corner[0, p] = jnp.where(low, ext[p, rows, 0:128], ext[p, rows, 384:512])
             self.corner[1, p] = jnp.where(low, ext[p, rows, 384:512], ext[p, rows, 256:384])
             start(place, self.copies[p], *DIAGONAL)
+
+    def finish(self):
+        place, ext, low = self.place, self.ext, lower(64)
         for p in range(2):
             wait_recv(place, self.copies[p], LEFT_NEXT, RIGHT_NEXT)
             ext[p, 128:384, 384:512] = merge(self.side_in[0, p, 64:192], self.side_in[1, p, 64:192])
@@ -377,6 +380,7 @@
         for pull in later:
             pull.start()
         update[...] = jnp.zeros_like(update)
+        halo.forward()
         light[...] = jnp.zeros_like(light)
         pulls[3].wait()
         for p in range(2):
@@ -558,6 +562,7 @@
             halo.pack(p)
             halo.start(p)
         halo.start_rest()
+        halo.forward()
         halo.finish()
         fold.close()
 

time: 78.6 us -> 77.9 us (level)
  no operation moved by 1% of the time
where the time goes in v7:
time: 77.9 us; the launch traced here: 77.5 us
  Pallas kernels  75.8 us (97%)
  local copies, waits for them, and re-layouts  1.02 us (1%)
    pallas_call x1, Pallas kernels, shards(): pl.pallas_call(between_kernel(grid), name='between', out_shape=(ext_shape...  28.8 us
    pallas_call x1, Pallas kernels, shards(): pl.pallas_call(spread_kernel(grid), name='spread', out_shape=(ext_shape,...  19.8 us
    pallas_call x1, Pallas kernels, shards(): pl.pallas_call(last_kernel(grid), name='last', out_shape=shape((2, 384, 3...  16.3 us
    pallas_call x1, Pallas kernels, shards(): pl.pallas_call(gradient_kernel(True), name='gradient_light', out_shape=(e...  6.01 us
    pallas_call x1, Pallas kernels, shards(): pl.pallas_call(gradient_kernel(False), name='gradient', out_shape=ext_sha...  4.91 us

profile of v7, /device:TPU:11, one launch (start us, length us, event | category | flops | bytes accessed | tf_op | source)
XLA Modules:
  0.0 77.5 jit_solution(17959082008649637059)
XLA Ops:
  0.7 19.8 %spread.1 = (f32[2,512,512]{2,1,0:T(8,128)S(1)}, s32[9,8,128]{2,1,0:T(8,128)S(1)}, f32[1,1,12,128,128]{4,3,2,1,0:T(8,128)S(1)}, bf16[4,256,256]{2,1,0:T(8,128)(2...) custom-call(f32[2,384,384]{2,1,0:T(8,128)} %field.1, ...), custom_call_target="tpu_custom_call" | custom-call | tf_op jit(solution)/shard_map/spread/pallas_call | solution.py:607
  20.4 6.0 %gradient_light.1 = (f32[2,512,512]{2,1,0:T(8,128)S(1)}, f32[648,640]{1,0:T(8,128)S(1)}) custom-call(s32[9,8,128]{2,1,0:T(8,128)S(1)} %get-tuple-element.18.refs_0_, f32[2,512,512]{2,1,0:T(8,128)S(1)} %get-tuple-element.19.refs_1_.field, f32[12,2,128,128]{3,2,1,0:T(8,128)S(1)} %get-tuple-element.20.refs_2_, ...), custom_call_target="tpu_custom_call", output_to_operand_aliasing={{0}: (5, {}), {1}: (7, {})} | custom-call | tf_op jit(solution)/shard_map/gradient_light/pallas_call | solution.py:628
  26.4 28.8 %between.1 = (f32[2,512,512]{2,1,0:T(8,128)S(1)}, f32[2,512,512]{2,1,0:T(8,128)S(1)}, f32[384,384]{1,0:T(8,128)S(1)}) custom-call(f32[2,512,512]{2,1,0:T(8,128)S(1)} %get-tuple-element.26.update, f32[648,640]{1,0:T(8,128)S(1)} %get-tuple-element.27.light, f32[2,512,512]{2,1,0:T(8,128)S(1)} %get-tuple-element.19.refs_1_.field), custom_call_target="tpu_custom_call" | custom-call | tf_op jit(solution)/shard_map/between/pallas_call | solution.py:637
  55.2 4.9 %gradient.1.update = f32[2,512,512]{2,1,0:T(8,128)S(1)} custom-call(s32[9,8,128]{2,1,0:T(8,128)S(1)} %get-tuple-element.18.refs_0_, f32[2,512,512]{2,1,0:T(8,128)S(1)} %get-tuple-element.28.refs_1_.ext, f32[12,2,128,128]{3,2,1,0:T(8,128)S(1)} %get-tuple-element.20.refs_2_, ...), custom_call_target="tpu_custom_call", output_to_operand_aliasing={{}: (5, {})} | custom-call | tf_op jit(solution)/shard_map/gradient/pallas_call | solution.py:646
  60.1 16.3 %last.1 = f32[2,384,384]{2,1,0:T(8,128)S(1)} custom-call(f32[2,512,512]{2,1,0:T(8,128)S(1)} %gradient.1.update, f32[384,384]{1,0:T(8,128)S(1)} %get-tuple-element.30.inverse, f32[2,512,512]{2,1,0:T(8,128)S(1)} %get-tuple-element.28.refs_1_.ext), custom_call_target="tpu_custom_call" | custom-call | tf_op jit(solution)/shard_map/last/pallas_call | solution.py:655
  76.4 1.0 %copy.15 = f32[2,384,384]{2,1,0:T(8,128)} copy(f32[2,384,384]{2,1,0:T(8,128)S(1)} %last.1) | data formatting | bytes 2359296

commit v8 on v7

--- a/solution.py
+++ b/solution.py
@@ -141,9 +141,11 @@
         when(place.gets[i], copies[i].wait_recv)
 
 
-def wait_send(place, copies):
-    for i, copy in enumerate(copies):
-        when(place.sends[i], copy.wait_send)
+def wait_send(place, copies, gone, *which):
+    for i in which or range(len(copies)):
+        if i not in gone:
+            when(place.sends[i], copies[i].wait_send)
+    gone.update(which or range(len(copies)))
 
 
 def strips(far, far_in, side, side_in, corner, corner_in, p):
@@ -167,6 +169,7 @@
 class Halo:
     def __init__(self, place, ext, far, side, corner, far_in, side_in, corner_in, sems):
         self.place, self.ext, self.far, self.far_in = place, ext, far, far_in
+        self.gone = (set(), set())
         self.side, self.corner, self.side_in, self.corner_in = side, corner, side_in, corner_in
         near, target = at_rows(place.near_border + 64, 64), at_rows(place.far_halo, 64)
         self.copies = []
@@ -203,9 +206,9 @@
     def start(self, p):
         start(self.place, self.copies[p], LEFT, RIGHT, FAR)
 
-    def start_rest(self):
-        for p in range(2):
-            start(self.place, self.copies[p], LEFT_NEXT, RIGHT_NEXT, NEAR)
+    def start_rest(self, p):
+        wait_send(self.place, self.copies[p], self.gone[p], LEFT, RIGHT)
+        start(self.place, self.copies[p], LEFT_NEXT, RIGHT_NEXT, NEAR)
 
     def forward(self):
         place, ext, low = self.place, self.ext, lower(64)
@@ -235,13 +238,14 @@
             ext[p, rows, 384:512] = jnp.where(low, right, left)
         for p in range(2):
             wait_recv(place, self.copies[p], NEAR, RELAY)
-            wait_send(place, self.copies[p])
+            wait_send(place, self.copies[p], self.gone[p])
 
 
 class Fold:
     def __init__(self, place, update, near_in, relay_in, far, side, corner, far_in, side_in, corner_in, sems):
         self.place, self.update, self.near_in, self.relay_in = place, update, near_in, relay_in
         self.far, self.far_in = far, far_in
+        self.gone = (set(), set())
         self.side, self.corner, self.side_in, self.corner_in = side, corner, side_in, corner_in
         near = at_rows(place.near_halo, 64)
         self.copies = []
@@ -268,13 +272,13 @@
             for k in range(2):
                 self.side[k, p, 64:192] = pack(update[p, 128:384, 384:512], k == 1)
 
-    def start(self):
+    def start(self, paced):
         place, update = self.place, self.update
         for p in range(2):
             start(place, self.copies[p], *DIAGONAL, RELAY)
-            if p == 0:
-                start(place, self.copies[p], FAR, LEFT_NEXT, RIGHT_NEXT)
-        start(place, self.copies[1], FAR)
+        start(place, self.copies[0], FAR, LEFT_NEXT, RIGHT_NEXT)
+        if not paced:
+            start(place, self.copies[1], FAR)
         for p in range(2):
             wait_recv(place, self.copies[p], RELAY, *DIAGONAL)
             extra = (self.relay_in[p], jnp.where(lower(64), self.corner_in[0, p], self.corner_in[1, p]))
@@ -283,23 +287,23 @@
                 for k in range(2):
                     self.side[k, p, 32 * i : 32 * i + 32] = pack(part, k == 1)
             start(place, self.copies[p], LEFT, RIGHT)
+            if p == 0 and paced:
+                start(place, self.copies[0], NEAR)
+                wait_send(place, self.copies[0], self.gone[0], FAR, LEFT_NEXT, RIGHT_NEXT)
+                start(place, self.copies[1], FAR)
             if p == 0:
                 start(place, self.copies[1], LEFT_NEXT, RIGHT_NEXT)
-        for p in range(2):
-            start(place, self.copies[p], NEAR)
-
-    def finish(self, p, dest, base, inverse):
+        if not paced:
+            start(place, self.copies[0], NEAR)
+        start(place, self.copies[1], NEAR)
+
+    def finish(self, p, dest, base, inverse, between=None):
         place = self.place
+        sides = ((place.right, 256, lambda x: jnp.where(lower(x.shape[0]), 0.0, x)), (place.left, 0, lambda x: jnp.where(lower(x.shape[0]), x, 0.0)))
 
         def add(first, lane, value):
             lanes, rows = pl.ds(lane, value.shape[1]), value.shape[0]
             dest[p, at_rows(first + base, rows), lanes] += value * inverse[at_rows(first, rows), lanes]
-
-        def lowest(value):
-            return jnp.where(lower(value.shape[0]), value, 0.0)
-
-        def highest(value):
-            return jnp.where(lower(value.shape[0]), 0.0, value)
 
         wait_recv(place, self.copies[p], NEAR)
         add(place.near_border, 0, self.near_in[p])
@@ -312,19 +316,26 @@
             add(place.far_border, 128, self.far_in[p, :, 0:128])
             add(place.far_border, 256, jnp.where(lower(64), mixed, self.corner_in[0, p]))
 
-        for k, (here, lane, keep) in enumerate(((place.right, 256, highest), (place.left, 0, lowest))):
+        for k, (here, lane, keep) in enumerate(sides):
 
             @pl.when(here)
             def _():
                 self.copies[p][LEFT_NEXT + k].wait_recv()
                 add(64, lane, keep(unpack(self.side_in[k, p, 64:192])))
+
+        if between is not None:
+            between()
+        for k, (here, lane, keep) in enumerate(sides):
+
+            @pl.when(here)
+            def _():
                 self.copies[p][LEFT + k].wait_recv()
                 add(place.near_border, lane, keep(unpack(self.side_in[k, p, 0:32])))
                 add(place.far_border, lane, keep(unpack(self.side_in[k, p, 32:64])))
 
     def close(self):
         for p in range(2):
-            wait_send(self.place, self.copies[p])
+            wait_send(self.place, self.copies[p], self.gone[p])
 
 
 def spread_kernel(grid):
@@ -376,7 +387,8 @@
         pulls[2].wait()
         halo.pack(1)
         halo.start(1)
-        halo.start_rest()
+        halo.start_rest(0)
+        halo.start_rest(1)
         for pull in later:
             pull.start()
         update[...] = jnp.zeros_like(update)
@@ -551,17 +563,19 @@
         halo = Halo(place, ext, halo_far, halo_side, halo_corner, halo_far_in, halo_side_in, halo_corner_in, more)
         fold.pack()
         greeted(place)
-        fold.start()
+        fold.start(True)
         halo.clear()
         inverse[...] = 1.0 / (light[128:512, 128:512] + 1.0)
         for p in range(2):
             ext[p, 64:448, 0:384] = field[p, 64:448, 0:384] + update[p, 64:448, 0:384] * inverse[...]
         cleared[...] = jnp.zeros_like(cleared)
-        for p in range(2):
-            fold.finish(p, ext, 64, inverse)
-            halo.pack(p)
-            halo.start(p)
-        halo.start_rest()
+        fold.finish(0, ext, 64, inverse)
+        halo.pack(0)
+        halo.start(0)
+        fold.finish(1, ext, 64, inverse, lambda: halo.start_rest(0))
+        halo.pack(1)
+        halo.start(1)
+        halo.start_rest(1)
         halo.forward()
         halo.finish()
         fold.close()
@@ -576,7 +590,7 @@
         fold = Fold(place, update, near_in, relay_in, far, side, corner, far_in, side_in, corner_in, sems)
         fold.pack()
         greeted(place)
-        fold.start()
+        fold.start(False)
         for p in range(2):
             out[p] = ext[p, 64:448, 0:384] + update[p, 64:448, 0:384] * inverse[...]
         for p in range(2):

time: 77.9 us -> 78.5 us (level)
    pallas_call x1, Pallas kernels: 28.8 us -> 29.8 us  [shards(): pl.pallas_call(between_kernel(grid), name='between', out_shape=(ext_shape...]
where the time goes in v8:
time: 78.5 us; the launch traced here: 77.9 us
  Pallas kernels  76.2 us (97%)
  local copies, waits for them, and re-layouts  1.02 us (1%)
    pallas_call x1, Pallas kernels, shards(): pl.pallas_call(between_kernel(grid), name='between', out_shape=(ext_shape...  29.8 us
    pallas_call x1, Pallas kernels, shards(): pl.pallas_call(spread_kernel(grid), name='spread', out_shape=(ext_shape,...  19.8 us
    pallas_call x1, Pallas kernels, shards(): pl.pallas_call(last_kernel(grid), name='last', out_shape=shape((2, 384, 3...  15.6 us
    pallas_call x1, Pallas kernels, shards(): pl.pallas_call(gradient_kernel(True), name='gradient_light', out_shape=(e...  6.12 us
    pallas_call x1, Pallas kernels, shards(): pl.pallas_call(gradient_kernel(False), name='gradient', out_shape=ext_sha...  4.91 us

profile of v8, /device:TPU:11, one launch (start us, length us, event | category | flops | bytes accessed | tf_op | source)
XLA Modules:
  0.0 77.9 jit_solution(7823439907095335655)
XLA Ops:
  0.7 19.8 %spread.1 = (f32[2,512,512]{2,1,0:T(8,128)S(1)}, s32[9,8,128]{2,1,0:T(8,128)S(1)}, f32[1,1,12,128,128]{4,3,2,1,0:T(8,128)S(1)}, bf16[4,256,256]{2,1,0:T(8,128)(2...) custom-call(f32[2,384,384]{2,1,0:T(8,128)} %field.1, ...), custom_call_target="tpu_custom_call" | custom-call | tf_op jit(solution)/shard_map/spread/pallas_call | solution.py:621
  20.4 6.1 %gradient_light.1 = (f32[2,512,512]{2,1,0:T(8,128)S(1)}, f32[648,640]{1,0:T(8,128)S(1)}) custom-call(s32[9,8,128]{2,1,0:T(8,128)S(1)} %get-tuple-element.18.refs_0_, f32[2,512,512]{2,1,0:T(8,128)S(1)} %get-tuple-element.19.refs_1_.field, f32[12,2,128,128]{3,2,1,0:T(8,128)S(1)} %get-tuple-element.20.refs_2_, ...), custom_call_target="tpu_custom_call", output_to_operand_aliasing={{0}: (5, {}), {1}: (7, {})} | custom-call | tf_op jit(solution)/shard_map/gradient_light/pallas_call | solution.py:642
  26.5 29.8 %between.1 = (f32[2,512,512]{2,1,0:T(8,128)S(1)}, f32[2,512,512]{2,1,0:T(8,128)S(1)}, f32[384,384]{1,0:T(8,128)S(1)}) custom-call(f32[2,512,512]{2,1,0:T(8,128)S(1)} %get-tuple-element.26.update, f32[648,640]{1,0:T(8,128)S(1)} %get-tuple-element.27.light, f32[2,512,512]{2,1,0:T(8,128)S(1)} %get-tuple-element.19.refs_1_.field), custom_call_target="tpu_custom_call" | custom-call | tf_op jit(solution)/shard_map/between/pallas_call | solution.py:651
  56.4 4.9 %gradient.1.update = f32[2,512,512]{2,1,0:T(8,128)S(1)} custom-call(s32[9,8,128]{2,1,0:T(8,128)S(1)} %get-tuple-element.18.refs_0_, f32[2,512,512]{2,1,0:T(8,128)S(1)} %get-tuple-element.28.refs_1_.ext, f32[12,2,128,128]{3,2,1,0:T(8,128)S(1)} %get-tuple-element.20.refs_2_, ...), custom_call_target="tpu_custom_call", output_to_operand_aliasing={{}: (5, {})} | custom-call | tf_op jit(solution)/shard_map/gradient/pallas_call | solution.py:660
  61.3 15.6 %last.1 = f32[2,384,384]{2,1,0:T(8,128)S(1)} custom-call(f32[2,512,512]{2,1,0:T(8,128)S(1)} %gradient.1.update, f32[384,384]{1,0:T(8,128)S(1)} %get-tuple-element.30.inverse, f32[2,512,512]{2,1,0:T(8,128)S(1)} %get-tuple-element.28.refs_1_.ext), custom_call_target="tpu_custom_call" | custom-call | tf_op jit(solution)/shard_map/last/pallas_call | solution.py:669
  76.9 1.0 %copy.15 = f32[2,384,384]{2,1,0:T(8,128)} copy(f32[2,384,384]{2,1,0:T(8,128)S(1)} %last.1) | data formatting | bytes 2359296

commit v9 on v8

--- a/solution.py
+++ b/solution.py
@@ -366,7 +366,6 @@
         pulls[0].wait()
         mine[0:2, 0:12] = offsets_here[0, 0]
         mine[2:3, 0:1] = jnp.full((1, 1), counts[0, 0], jnp.int32)
-        around[8] = mine[...]
         letters = []
         for i, d in enumerate(AROUND):
             letter = pltpu.make_async_remote_copy(
@@ -449,10 +448,13 @@
 def gradient_kernel(with_light):
     def kernel(*refs):
         if with_light:
-            around, ext, beams, measured, tables, _, power, _, update, light = refs
+            offsets, counts, around, ext, beams, measured, tables, _, power, _, update, light, notes, arrived = refs
         else:
-            around, ext, beams, measured, tables, _, update = refs
-        count = around[8, 2, 0]
+            offsets, counts, ext, beams, measured, tables, _, update = refs
+        count = counts[0, 0]
+        if with_light:
+            bring = pltpu.make_async_copy(around, notes, arrived.at[0])
+            bring.start()
         lane = lax.broadcasted_iota(jnp.int32, (128, 128), 1)
         sub = lax.broadcasted_iota(jnp.int32, (8, 128), 0)
 
@@ -480,7 +482,7 @@
             scatter(light, first, tiles_of(col, 1, 5), low_row, low_col, value)
 
         def gather(slot):
-            row, col = around[8, 0, slot], around[8, 1, slot]
+            row, col = offsets[0, 0, 0, slot], offsets[0, 0, 1, slot]
             low_row, low_col = jnp.bitwise_and(row, 7), jnp.bitwise_and(col, 127)
             first = pl.multiple_of(row - low_row + 64, 8)
             lanes = tiles_of(col, 0, 4)
@@ -531,11 +533,12 @@
 
         lax.fori_loop(0, (count + GROUP - 1) // GROUP, some, 0)
         if with_light:
+            bring.wait()
             for i, d in enumerate(AROUND):
 
                 def other(slot, carry):
-                    row = around[i, 0, slot] + d[0] * 384
-                    col = around[i, 1, slot] + d[1] * 384
+                    row = notes[i, 0, slot] + d[0] * 384
+                    col = notes[i, 1, slot] + d[1] * 384
                     touches = (row > -128) & (row < 384) & (col > -128) & (col < 384)
 
                     @pl.when(touches)
@@ -545,7 +548,7 @@
 
                     return carry
 
-                lax.fori_loop(0, around[i, 2, 0], other, 0)
+                lax.fori_loop(0, notes[i, 2, 0], other, 0)
 
     return kernel
 
@@ -623,7 +626,7 @@
         name="spread",
         out_shape=(
             ext_shape,
-            shape((9, 8, 128), i32),
+            shape((8, 8, 128), i32),
             shape(amplitudes.shape, f32),
             shape(tables.shape, tables.dtype),
             shape((12, 2, 128, 128), f32),
@@ -643,11 +646,12 @@
         gradient_kernel(True),
         name="gradient_light",
         out_shape=(ext_shape, light_shape),
-        in_specs=[SMEM] + [VMEM] * 7,
+        in_specs=[SMEM] * 2 + [VMEM] * 8,
         out_specs=(VMEM,) * 2,
-        input_output_aliases={5: 0, 7: 1},
+        scratch_shapes=[pltpu.SMEM((8, 8, 128), i32), pltpu.SemaphoreType.DMA((1,))],
+        input_output_aliases={7: 0, 9: 1},
         compiler_params=params(),
-    )(around, ext, beams, measured, tables, update, power, light)
+    )(offsets, counts, around, ext, beams, measured, tables, update, power, light)
     ext, cleared, inverse = pl.pallas_call(
         between_kernel(grid),
         name="between",
@@ -661,11 +665,11 @@
         gradient_kernel(False),
         name="gradient",
         out_shape=ext_shape,
-        in_specs=[SMEM] + [VMEM] * 5,
+        in_specs=[SMEM] * 2 + [VMEM] * 5,
         out_specs=VMEM,
-        input_output_aliases={5: 0},
+        input_output_aliases={6: 0},
         compiler_params=params(),
-    )(around, ext, beams, measured, tables, cleared)
+    )(offsets, counts, ext, beams, measured, tables, cleared)
     return pl.pallas_call(
         last_kernel(grid),
         name="last",

time: 78.5 us -> 77.1 us (0.982)
  the two profiles are of different devices: /device:TPU:11 before, /device:TPU:13 now
where the time goes in v9:
time: 77.1 us; the launch traced here: 76.1 us
  Pallas kernels  74.4 us (96%)
  local copies, waits for them, and re-layouts  1.02 us (1%)
    pallas_call x1, Pallas kernels, shards(): pl.pallas_call(between_kernel(grid), name='between', out_shape=(ext_shape...  27.4 us
    pallas_call x1, Pallas kernels, shards(): pl.pallas_call(spread_kernel(grid), name='spread', out_shape=(ext_shape,...  19.5 us
    pallas_call x1, Pallas kernels, shards(): pl.pallas_call(last_kernel(grid), name='last', out_shape=shape((2, 384, 3...  16.7 us
    pallas_call x1, Pallas kernels, shards(): pl.pallas_call(gradient_kernel(True), name='gradient_light', out_shape=(e...  6.42 us
    pallas_call x1, Pallas kernels, shards(): pl.pallas_call(gradient_kernel(False), name='gradient', out_shape=ext_sha...  4.32 us

profile of v9, /device:TPU:13, one launch (start us, length us, event | category | flops | bytes accessed | tf_op | source)
XLA Modules:
  0.0 76.1 jit_solution(16996804864275995773)
XLA Ops:
  0.0 0.0 copy-start
  0.7 19.5 %spread.1 = (f32[2,512,512]{2,1,0:T(8,128)S(1)}, s32[8,8,128]{2,1,0:T(8,128)S(1)}, f32[1,1,12,128,128]{4,3,2,1,0:T(8,128)S(1)}, bf16[4,256,256]{2,1,0:T(8,128)(2...) custom-call(f32[2,384,384]{2,1,0:T(8,128)} %field.1, ...), custom_call_target="tpu_custom_call" | custom-call | tf_op jit(solution)/shard_map/spread/pallas_call | solution.py:624
  20.2 0.0 copy-done
  20.2 6.4 %gradient_light.1 = (f32[2,512,512]{2,1,0:T(8,128)S(1)}, f32[648,640]{1,0:T(8,128)S(1)}) custom-call(s32[1,1,2,12]{3,2,1,0:T(2,128)S(1)} %bitcast.3, s32[1,1]{1,0:T(1,128)S(6)} %copy.14.counts.refs_1_, s32[8,8,128]{2,1,0:T(8,128)S(1)} %get-tuple-element.18.refs_2_, ...), custom_call_target="tpu_custom_call", output_to_operand_aliasing={{0}: (7, {}), {1}: (9, {})} | custom-call | tf_op jit(solution)/shard_map/gradient_light/pallas_call | solution.py:645
  26.6 27.4 %between.1 = (f32[2,512,512]{2,1,0:T(8,128)S(1)}, f32[2,512,512]{2,1,0:T(8,128)S(1)}, f32[384,384]{1,0:T(8,128)S(1)}) custom-call(f32[2,512,512]{2,1,0:T(8,128)S(1)} %get-tuple-element.26.update, f32[648,640]{1,0:T(8,128)S(1)} %get-tuple-element.27.light, f32[2,512,512]{2,1,0:T(8,128)S(1)} %get-tuple-element.19.refs_3_.field), custom_call_target="tpu_custom_call" | custom-call | tf_op jit(solution)/shard_map/between/pallas_call | solution.py:655
  54.0 4.3 %gradient.1.update = f32[2,512,512]{2,1,0:T(8,128)S(1)} custom-call(s32[1,1,2,12]{3,2,1,0:T(2,128)S(1)} %bitcast.4, s32[1,1]{1,0:T(1,128)S(6)} %copy.14.counts.refs_1_, f32[2,512,512]{2,1,0:T(8,128)S(1)} %get-tuple-element.28.refs_2_.ext, f32[12,2,128,128]{3,2,1,0:T(8,128)S(1)} %get-tuple-element.20.refs_4_.refs_3_, ...), custom_call_target="tpu_custom_call", output_to_operand_aliasing={{}: (6, {})} | custom-call | tf_op jit(solution)/shard_map/gradient/pallas_call | solution.py:664
  58.4 16.7 %last.1 = f32[2,384,384]{2,1,0:T(8,128)S(1)} custom-call(f32[2,512,512]{2,1,0:T(8,128)S(1)} %gradient.1.update, f32[384,384]{1,0:T(8,128)S(1)} %get-tuple-element.30.inverse, f32[2,512,512]{2,1,0:T(8,128)S(1)} %get-tuple-element.28.refs_2_.ext), custom_call_target="tpu_custom_call" | custom-call | tf_op jit(solution)/shard_map/last/pallas_call | solution.py:673
  75.1 1.0 %copy.15 = f32[2,384,384]{2,1,0:T(8,128)} copy(f32[2,384,384]{2,1,0:T(8,128)S(1)} %last.1) | data formatting | bytes 2359296
Async XLA Ops:
  0.0 20.2 %copy-start = (s32[1,1,12,2]{2,3,1,0:T(2,128)S(1)}, s32[1,1,12,2]{2,3,1,0:T(2,128)}, u32[]{:S(2)}) copy-start(s32[1,1,12,2]{2,3,1,0:T(2,128)} %param.9) | copy-start | bytes 292

commit v10 on v9

--- a/solution.py
+++ b/solution.py
@@ -14,7 +14,6 @@
 SMEM = pl.BlockSpec(memory_space=pltpu.SMEM)
 HBM = pl.BlockSpec(memory_space=pltpu.MemorySpace.HBM)
 LIMIT = 24 << 20
-GROUP = 6
 NEAR, FAR, LEFT, RIGHT, FAR_LEFT, FAR_RIGHT, LEFT_NEXT, RIGHT_NEXT, RELAY, EDGE_LEFT, EDGE_RIGHT = range(11)
 DIAGONAL = (FAR_LEFT, FAR_RIGHT, EDGE_LEFT, EDGE_RIGHT)
 
@@ -198,10 +197,13 @@
         for k, lane in enumerate((0, 256)):
             for i, first in enumerate((place.near_border, place.far_border)):
                 self.side[k, p, 32 * i : 32 * i + 32] = pack(ext[p, at_rows(first + 64, 64), lane : lane + 128], k == 0)
-            self.side[k, p, 64:192] = pack(ext[p, 128:384, lane : lane + 128], k == 0)
         rows = at_rows(place.far_border + 64, 64)
         self.far[p, :, 0:128] = ext[p, rows, 128:256]
         self.far[p, :, 128:256] = jnp.where(lower(64), ext[p, rows, 256:384], ext[p, rows, 0:128])
+
+    def pack_rest(self, p):
+        for k, lane in enumerate((0, 256)):
+            self.side[k, p, 64:192] = pack(self.ext[p, 128:384, lane : lane + 128], k == 0)
 
     def start(self, p):
         start(self.place, self.copies[p], LEFT, RIGHT, FAR)
@@ -386,8 +388,9 @@
         pulls[2].wait()
         halo.pack(1)
         halo.start(1)
-        halo.start_rest(0)
-        halo.start_rest(1)
+        for p in range(2):
+            halo.pack_rest(p)
+            halo.start_rest(p)
         for pull in later:
             pull.start()
         update[...] = jnp.zeros_like(update)
@@ -511,27 +514,53 @@
             if with_light:
                 brighten(row, col, beam[0] * beam[0] + beam[1] * beam[1])
 
-        def some(step, carry):
-            slots = [step * GROUP + k for k in range(GROUP)]
-            pairs = [(k, k + 1) for k in range(0, GROUP, 2)]
-            gathered = [gather(slot) for slot in slots]
-            waves = [jnp.concatenate([gathered[a][0], gathered[b][0]], axis=0) for a, b in pairs]
-            half = [cross(right_mul(wave, tables[0], tables[1])) for wave in waves]
-            far = [left_mul(tables[2], tables[3], x) for x in half]
-            change = []
-            for x, (a, b) in zip(far, pairs):
-                real, imag = x[:128], x[128:]
-                known = jnp.concatenate([measured[0, 0, slots[a]], measured[0, 0, slots[b]]], axis=1)
-                ratio = known * lax.rsqrt(real * real + imag * imag + 0.25) - 1.0
-                change.append(jnp.concatenate([real * ratio, imag * ratio], axis=0))
-            half = [cross(left_mul(tables[0], tables[1], x)) for x in change]
-            back = [right_mul(x, tables[2], tables[3]) for x in half]
-            for x, (a, b) in zip(back, pairs):
-                put(x[:128], gathered[a][1])
-                put(x[128:], gathered[b][1])
-            return carry
-
-        lax.fori_loop(0, (count + GROUP - 1) // GROUP, some, 0)
+        def block(size):
+            slots = list(range(size))
+            pairs = [(k, k + 1) for k in range(0, size, 2)]
+            got, given, raw = {}, {}, {}
+
+            def fetch(k):
+                a, b = pairs[k]
+                got[k] = gather(slots[a]), gather(slots[b])
+                given[k] = split(jnp.concatenate([got[k][0][0], got[k][1][0]], axis=0))
+
+            def multiply(n, k):
+                high, low = given[k]
+                if n in (0, 3):
+                    t, u = (tables[0], tables[1]) if n == 0 else (tables[2], tables[3])
+                    raw[k] = dot(high, t) + dot(low, t) + dot(high, u)
+                else:
+                    t, u = (tables[2], tables[3]) if n == 1 else (tables[0], tables[1])
+                    raw[k] = dot(t, high) + dot(t, low) + dot(u, high)
+
+            def after(n, k):
+                a, b = pairs[k]
+                x = raw[k]
+                if n == 3:
+                    put(x[:128], got[k][0][1])
+                    put(x[128:], got[k][1][1])
+                    return
+                if n == 1:
+                    real, imag = x[:128], x[128:]
+                    known = jnp.concatenate([measured[0, 0, slots[a]], measured[0, 0, slots[b]]], axis=1)
+                    ratio = known * lax.rsqrt(real * real + imag * imag + 0.25) - 1.0
+                    x = jnp.concatenate([real * ratio, imag * ratio], axis=0)
+                else:
+                    x = cross(x)
+                given[k] = split(x)
+
+            todo = [(n, k) for n in range(4) for k in range(len(pairs))]
+            fetch(0)
+            for i, (n, k) in enumerate(todo):
+                multiply(n, k)
+                if n == 0 and k + 1 < len(pairs):
+                    fetch(k + 1)
+                if i:
+                    after(*todo[i - 1])
+            after(*todo[-1])
+
+        pl.when(count > 6)(lambda: block(12))
+        pl.when(count <= 6)(lambda: block(6))
         if with_light:
             bring.wait()
             for i, d in enumerate(AROUND):
@@ -572,10 +601,15 @@
         for p in range(2):
             ext[p, 64:448, 0:384] = field[p, 64:448, 0:384] + update[p, 64:448, 0:384] * inverse[...]
         cleared[...] = jnp.zeros_like(cleared)
-        fold.finish(0, ext, 64, inverse)
+        fold.finish(0, ext, 64, inverse, lambda: halo.pack_rest(0))
         halo.pack(0)
         halo.start(0)
-        fold.finish(1, ext, 64, inverse, lambda: halo.start_rest(0))
+
+        def meanwhile():
+            halo.start_rest(0)
+            halo.pack_rest(1)
+
+        fold.finish(1, ext, 64, inverse, meanwhile)
         halo.pack(1)
         halo.start(1)
         halo.start_rest(1)

time: 77.1 us -> 76.7 us (level)
  the two profiles are of different devices: /device:TPU:13 before, /device:TPU:11 now
where the time goes in v10:
time: 76.7 us
  Pallas kernels  74.9 us (98%)
  local copies, waits for them, and re-layouts  1.02 us (1%)
    pallas_call x1, Pallas kernels, shards(): pl.pallas_call(between_kernel(grid), name='between', out_shape=(ext_shape...  31.3 us
    pallas_call x1, Pallas kernels, shards(): pl.pallas_call(spread_kernel(grid), name='spread', out_shape=(ext_shape,...  19.8 us
    pallas_call x1, Pallas kernels, shards(): pl.pallas_call(last_kernel(grid), name='last', out_shape=shape((2, 384, 3...  17.7 us
    pallas_call x1, Pallas kernels, shards(): pl.pallas_call(gradient_kernel(True), name='gradient_light', out_shape=(e...  3.58 us
    pallas_call x1, Pallas kernels, shards(): pl.pallas_call(gradient_kernel(False), name='gradient', out_shape=ext_sha...  2.63 us

profile of v10, /device:TPU:11, one launch (start us, length us, event | category | flops | bytes accessed | tf_op | source)
XLA Modules:
  0.0 76.7 jit_solution(7673950216659027452)
XLA Ops:
  0.0 0.0 copy-start
  0.7 19.8 %spread.1 = (f32[2,512,512]{2,1,0:T(8,128)S(1)}, s32[8,8,128]{2,1,0:T(8,128)S(1)}, f32[1,1,12,128,128]{4,3,2,1,0:T(8,128)S(1)}, bf16[4,256,256]{2,1,0:T(8,128)(2...) custom-call(f32[2,384,384]{2,1,0:T(8,128)} %field.1, ...), custom_call_target="tpu_custom_call" | custom-call | tf_op jit(solution)/shard_map/spread/pallas_call | solution.py:658
  20.4 0.0 copy-done
  20.4 3.6 %gradient_light.1 = (f32[2,512,512]{2,1,0:T(8,128)S(1)}, f32[648,640]{1,0:T(8,128)S(1)}) custom-call(s32[1,1,2,12]{3,2,1,0:T(2,128)S(1)} %bitcast.3, s32[1,1]{1,0:T(1,128)S(6)} %copy.14.counts.refs_1_, s32[8,8,128]{2,1,0:T(8,128)S(1)} %get-tuple-element.18.refs_2_, ...), custom_call_target="tpu_custom_call", output_to_operand_aliasing={{0}: (7, {}), {1}: (9, {})} | custom-call | tf_op jit(solution)/shard_map/gradient_light/pallas_call | solution.py:679
  24.0 31.3 %between.1 = (f32[2,512,512]{2,1,0:T(8,128)S(1)}, f32[2,512,512]{2,1,0:T(8,128)S(1)}, f32[384,384]{1,0:T(8,128)S(1)}) custom-call(f32[2,512,512]{2,1,0:T(8,128)S(1)} %get-tuple-element.26.update, f32[648,640]{1,0:T(8,128)S(1)} %get-tuple-element.27.light, f32[2,512,512]{2,1,0:T(8,128)S(1)} %get-tuple-element.19.refs_3_.field), custom_call_target="tpu_custom_call" | custom-call | tf_op jit(solution)/shard_map/between/pallas_call | solution.py:689
  55.3 2.6 %gradient.1.update = f32[2,512,512]{2,1,0:T(8,128)S(1)} custom-call(s32[1,1,2,12]{3,2,1,0:T(2,128)S(1)} %bitcast.4, s32[1,1]{1,0:T(1,128)S(6)} %copy.14.counts.refs_1_, f32[2,512,512]{2,1,0:T(8,128)S(1)} %get-tuple-element.28.refs_2_.ext, f32[12,2,128,128]{3,2,1,0:T(8,128)S(1)} %get-tuple-element.20.refs_4_.refs_3_, ...), custom_call_target="tpu_custom_call", output_to_operand_aliasing={{}: (6, {})} | custom-call | tf_op jit(solution)/shard_map/gradient/pallas_call | solution.py:698
  57.9 17.7 %last.1 = f32[2,384,384]{2,1,0:T(8,128)S(1)} custom-call(f32[2,512,512]{2,1,0:T(8,128)S(1)} %gradient.1.update, f32[384,384]{1,0:T(8,128)S(1)} %get-tuple-element.30.inverse, f32[2,512,512]{2,1,0:T(8,128)S(1)} %get-tuple-element.28.refs_2_.ext), custom_call_target="tpu_custom_call" | custom-call | tf_op jit(solution)/shard_map/last/pallas_call | solution.py:707
  75.7 1.0 %copy.15 = f32[2,384,384]{2,1,0:T(8,128)} copy(f32[2,384,384]{2,1,0:T(8,128)S(1)} %last.1) | data formatting | bytes 2359296
Async XLA Ops:
  0.0 20.4 %copy-start = (s32[1,1,12,2]{2,3,1,0:T(2,128)S(1)}, s32[1,1,12,2]{2,3,1,0:T(2,128)}, u32[]{:S(2)}) copy-start(s32[1,1,12,2]{2,3,1,0:T(2,128)} %param.9) | copy-start | bytes 292

commit v11 on v10

--- a/solution.py
+++ b/solution.py
@@ -342,8 +342,8 @@
 
 def spread_kernel(grid):
     def kernel(
-        field, offsets, counts, places, measured, tables, probe,
-        ext, around, measured_here, tables_here, beams, power, update, light,
+        field, offsets, counts, measured, tables, probe,
+        ext, around, measured_here, tables_here, beams, power, update, light, places,
         mine, offsets_here, tall, far, side, corner, far_in, side_in, corner_in, sems, notes, local,
     ):
         place = Place(grid)
@@ -355,6 +355,7 @@
             pltpu.make_async_copy(tables, tables_here, local.at[4]),
         ]
         pulls.append(pltpu.make_async_copy(probe, tall.at[:, 8:136], local.at[5]))
+        pulls.append(pltpu.make_async_copy(offsets, places, local.at[6]))
         for pull in pulls:
             pull.start()
         halo = Halo(place, ext, far, side, corner, far_in, side_in, corner_in, sems)
@@ -397,6 +398,7 @@
         halo.forward()
         light[...] = jnp.zeros_like(light)
         pulls[3].wait()
+        pulls[4].wait()
         for p in range(2):
             tall[p, 0:8] = tall[p, 128:136]
         power[...] = tall[0] * tall[0] + tall[1] * tall[1]
@@ -655,7 +657,7 @@
     packs = [pltpu.VMEM((2, 64, 256), f32), pltpu.VMEM((2, 2, 192, 128), f32), pltpu.VMEM((2, 2, 64, 128), f32)]
     folds = [pltpu.VMEM((2, 64, 384), f32), pltpu.VMEM((2, 64, 128), f32)] + packs + packs
     sems = pltpu.SemaphoreType.DMA((2, 2, 11))
-    ext, around, measured, tables, beams, power, update, light = pl.pallas_call(
+    ext, around, measured, tables, beams, power, update, light, places = pl.pallas_call(
         spread_kernel(grid),
         name="spread",
         out_shape=(
@@ -667,15 +669,16 @@
             shape((136, 128), f32),
             ext_shape,
             light_shape,
+            shape((1, 1, 2, 12), i32),
         ),
-        in_specs=[HBM, HBM, SMEM, SMEM, HBM, HBM, HBM],
-        out_specs=(VMEM,) * 8,
+        in_specs=[HBM, HBM, SMEM, HBM, HBM, HBM],
+        out_specs=(VMEM,) * 8 + (SMEM,),
         scratch_shapes=[pltpu.VMEM((8, 128), i32), pltpu.VMEM((1, 1, 2, 12), i32), pltpu.VMEM((2, 136, 128), f32)]
         + packs
         + packs
-        + [sems, pltpu.SemaphoreType.DMA((2, 8)), pltpu.SemaphoreType.DMA((6,))],
+        + [sems, pltpu.SemaphoreType.DMA((2, 8)), pltpu.SemaphoreType.DMA((7,))],
         compiler_params=params(0),
-    )(hold(object_field), hold(offsets), counts, offsets, hold(amplitudes), hold(tables), hold(probe))
+    )(hold(object_field), hold(offsets), counts, hold(amplitudes), hold(tables), hold(probe))
     update, light = pl.pallas_call(
         gradient_kernel(True),
         name="gradient_light",
@@ -685,7 +688,7 @@
         scratch_shapes=[pltpu.SMEM((8, 8, 128), i32), pltpu.SemaphoreType.DMA((1,))],
         input_output_aliases={7: 0, 9: 1},
         compiler_params=params(),
-    )(offsets, counts, around, ext, beams, measured, tables, update, power, light)
+    )(places, counts, around, ext, beams, measured, tables, update, power, light)
     ext, cleared, inverse = pl.pallas_call(
         between_kernel(grid),
         name="between",
@@ -703,7 +706,7 @@
         out_specs=VMEM,
         input_output_aliases={6: 0},
         compiler_params=params(),
-    )(offsets, counts, ext, beams, measured, tables, cleared)
+    )(places, counts, ext, beams, measured, tables, cleared)
     return pl.pallas_call(
         last_kernel(grid),
         name="last",

time: 76.7 us -> 76.5 us (level); the launches traced: 76.7 us -> 75.5 us
  Pallas kernels: 74.9 us -> 73.8 us
    pallas_call x1, Pallas kernels: 31.3 us -> 30.3 us  [shards(): pl.pallas_call(between_kernel(grid), name='between', out_shape=(ext_shape...]
where the time goes in v11:
time: 76.5 us; the launch traced here: 75.5 us
  Pallas kernels  73.8 us (96%)
  local copies, waits for them, and re-layouts  1.02 us (1%)
    pallas_call x1, Pallas kernels, shards(): pl.pallas_call(between_kernel(grid), name='between', out_shape=(ext_shape...  30.3 us
    pallas_call x1, Pallas kernels, shards(): pl.pallas_call(spread_kernel(grid), name='spread', out_shape=(ext_shape,...  19.7 us
    pallas_call x1, Pallas kernels, shards(): pl.pallas_call(last_kernel(grid), name='last', out_shape=shape((2, 384, 3...  17.9 us
    pallas_call x1, Pallas kernels, shards(): pl.pallas_call(gradient_kernel(True), name='gradient_light', out_shape=(e...  3.26 us
    pallas_call x1, Pallas kernels, shards(): pl.pallas_call(gradient_kernel(False), name='gradient', out_shape=ext_sha...  2.63 us

profile of v11, /device:TPU:11, one launch (start us, length us, event | category | flops | bytes accessed | tf_op | source)
XLA Modules:
  0.0 75.5 jit_solution(14261038052994858216)
XLA Ops:
  0.7 19.7 %spread.1 = (f32[2,512,512]{2,1,0:T(8,128)S(1)}, s32[8,8,128]{2,1,0:T(8,128)S(1)}, f32[1,1,12,128,128]{4,3,2,1,0:T(8,128)S(1)}, bf16[4,256,256]{2,1,0:T(8,128)(2...) custom-call(f32[2,384,384]{2,1,0:T(8,128)} %field.1, ...), custom_call_target="tpu_custom_call" | custom-call | tf_op jit(solution)/shard_map/spread/pallas_call | solution.py:660
  20.3 3.3 %gradient_light.1 = (f32[2,512,512]{2,1,0:T(8,128)S(1)}, f32[648,640]{1,0:T(8,128)S(1)}) custom-call(s32[1,1,2,12]{3,2,1,0:T(2,128)S(1)} %get-tuple-element.19.refs_0_, s32[1,1]{1,0:T(1,128)S(6)} %copy.14.counts.refs_1_, s32[8,8,128]{2,1,0:T(8,128)S(1)} %get-tuple-element.20.refs_2_, ...), custom_call_target="tpu_custom_call", output_to_operand_aliasing={{0}: (7, {}), {1}: (9, {})} | custom-call | tf_op jit(solution)/shard_map/gradient_light/pallas_call | solution.py:682
  23.6 30.3 %between.1 = (f32[2,512,512]{2,1,0:T(8,128)S(1)}, f32[2,512,512]{2,1,0:T(8,128)S(1)}, f32[384,384]{1,0:T(8,128)S(1)}) custom-call(f32[2,512,512]{2,1,0:T(8,128)S(1)} %get-tuple-element.28.update, f32[648,640]{1,0:T(8,128)S(1)} %get-tuple-element.29.light, f32[2,512,512]{2,1,0:T(8,128)S(1)} %get-tuple-element.21.refs_3_.field), custom_call_target="tpu_custom_call" | custom-call | tf_op jit(solution)/shard_map/between/pallas_call | solution.py:692
  54.0 2.6 %gradient.1.update = f32[2,512,512]{2,1,0:T(8,128)S(1)} custom-call(s32[1,1,2,12]{3,2,1,0:T(2,128)S(1)} %get-tuple-element.19.refs_0_, s32[1,1]{1,0:T(1,128)S(6)} %copy.14.counts.refs_1_, f32[2,512,512]{2,1,0:T(8,128)S(1)} %get-tuple-element.30.refs_2_.ext, ...), custom_call_target="tpu_custom_call", output_to_operand_aliasing={{}: (6, {})} | custom-call | tf_op jit(solution)/shard_map/gradient/pallas_call | solution.py:701
  56.6 17.9 %last.1 = f32[2,384,384]{2,1,0:T(8,128)S(1)} custom-call(f32[2,512,512]{2,1,0:T(8,128)S(1)} %gradient.1.update, f32[384,384]{1,0:T(8,128)S(1)} %get-tuple-element.32.inverse, f32[2,512,512]{2,1,0:T(8,128)S(1)} %get-tuple-element.30.refs_2_.ext), custom_call_target="tpu_custom_call" | custom-call | tf_op jit(solution)/shard_map/last/pallas_call | solution.py:710
  74.5 1.0 %copy.15 = f32[2,384,384]{2,1,0:T(8,128)} copy(f32[2,384,384]{2,1,0:T(8,128)S(1)} %last.1) | data formatting | bytes 2359296

commit v12 on v11

--- a/solution.py
+++ b/solution.py
@@ -562,7 +562,8 @@
             after(*todo[-1])
 
         pl.when(count > 6)(lambda: block(12))
-        pl.when(count <= 6)(lambda: block(6))
+        pl.when((count > 4) & (count <= 6))(lambda: block(6))
+        pl.when(count <= 4)(lambda: block(4))
         if with_light:
             bring.wait()
             for i, d in enumerate(AROUND):

time: 76.5 us -> 76.7 us (level)
  Pallas kernels: 73.8 us -> 74.6 us
    pallas_call x1, Pallas kernels: 3.26 us -> 5.81 us  [shards(): pl.pallas_call(gradient_kernel(True), name='gradient_light', out_shape=(e...]
    pallas_call x1, Pallas kernels: 17.9 us -> 15.9 us  [shards(): pl.pallas_call(last_kernel(grid), name='last', out_shape=shape((2, 384, 3...]
    pallas_call x1, Pallas kernels: 2.63 us -> 4.28 us  [shards(): pl.pallas_call(gradient_kernel(False), name='gradient', out_shape=ext_sha...]
    pallas_call x1, Pallas kernels: 30.3 us -> 29 us  [shards(): pl.pallas_call(between_kernel(grid), name='between', out_shape=(ext_shape...]
where the time goes in v12:
time: 76.7 us; the launch traced here: 76.3 us
  Pallas kernels  74.6 us (97%)
  local copies, waits for them, and re-layouts  1.02 us (1%)
    pallas_call x1, Pallas kernels, shards(): pl.pallas_call(between_kernel(grid), name='between', out_shape=(ext_shape...  29 us
    pallas_call x1, Pallas kernels, shards(): pl.pallas_call(spread_kernel(grid), name='spread', out_shape=(ext_shape,...  19.7 us
    pallas_call x1, Pallas kernels, shards(): pl.pallas_call(last_kernel(grid), name='last', out_shape=shape((2, 384, 3...  15.9 us
    pallas_call x1, Pallas kernels, shards(): pl.pallas_call(gradient_kernel(True), name='gradient_light', out_shape=(e...  5.81 us
    pallas_call x1, Pallas kernels, shards(): pl.pallas_call(gradient_kernel(False), name='gradient', out_shape=ext_sha...  4.28 us

profile of v12, /device:TPU:11, one launch (start us, length us, event | category | flops | bytes accessed | tf_op | source)
XLA Modules:
  0.0 76.3 jit_solution(4415255021715754316)
XLA Ops:
  0.7 19.7 %spread.1 = (f32[2,512,512]{2,1,0:T(8,128)S(1)}, s32[8,8,128]{2,1,0:T(8,128)S(1)}, f32[1,1,12,128,128]{4,3,2,1,0:T(8,128)S(1)}, bf16[4,256,256]{2,1,0:T(8,128)(2...) custom-call(f32[2,384,384]{2,1,0:T(8,128)} %field.1, ...), custom_call_target="tpu_custom_call" | custom-call | tf_op jit(solution)/shard_map/spread/pallas_call | solution.py:661
  20.3 5.8 %gradient_light.1 = (f32[2,512,512]{2,1,0:T(8,128)S(1)}, f32[648,640]{1,0:T(8,128)S(1)}) custom-call(s32[1,1,2,12]{3,2,1,0:T(2,128)S(1)} %get-tuple-element.19.refs_0_, s32[1,1]{1,0:T(1,128)S(6)} %copy.14.counts.refs_1_, s32[8,8,128]{2,1,0:T(8,128)S(1)} %get-tuple-element.20.refs_2_, ...), custom_call_target="tpu_custom_call", output_to_operand_aliasing={{0}: (7, {}), {1}: (9, {})} | custom-call | tf_op jit(solution)/shard_map/gradient_light/pallas_call | solution.py:683
  26.2 29.0 %between.1 = (f32[2,512,512]{2,1,0:T(8,128)S(1)}, f32[2,512,512]{2,1,0:T(8,128)S(1)}, f32[384,384]{1,0:T(8,128)S(1)}) custom-call(f32[2,512,512]{2,1,0:T(8,128)S(1)} %get-tuple-element.28.update, f32[648,640]{1,0:T(8,128)S(1)} %get-tuple-element.29.light, f32[2,512,512]{2,1,0:T(8,128)S(1)} %get-tuple-element.21.refs_3_.field), custom_call_target="tpu_custom_call" | custom-call | tf_op jit(solution)/shard_map/between/pallas_call | solution.py:693
  55.2 4.3 %gradient.1.update = f32[2,512,512]{2,1,0:T(8,128)S(1)} custom-call(s32[1,1,2,12]{3,2,1,0:T(2,128)S(1)} %get-tuple-element.19.refs_0_, s32[1,1]{1,0:T(1,128)S(6)} %copy.14.counts.refs_1_, f32[2,512,512]{2,1,0:T(8,128)S(1)} %get-tuple-element.30.refs_2_.ext, ...), custom_call_target="tpu_custom_call", output_to_operand_aliasing={{}: (6, {})} | custom-call | tf_op jit(solution)/shard_map/gradient/pallas_call | solution.py:702
  59.5 15.9 %last.1 = f32[2,384,384]{2,1,0:T(8,128)S(1)} custom-call(f32[2,512,512]{2,1,0:T(8,128)S(1)} %gradient.1.update, f32[384,384]{1,0:T(8,128)S(1)} %get-tuple-element.32.inverse, f32[2,512,512]{2,1,0:T(8,128)S(1)} %get-tuple-element.30.refs_2_.ext), custom_call_target="tpu_custom_call" | custom-call | tf_op jit(solution)/shard_map/last/pallas_call | solution.py:711
  75.3 1.0 %copy.15 = f32[2,384,384]{2,1,0:T(8,128)} copy(f32[2,384,384]{2,1,0:T(8,128)S(1)} %last.1) | data formatting | bytes 2359296

commit v13 on v11

--- a/solution.py
+++ b/solution.py
@@ -597,7 +597,7 @@
         halo = Halo(place, ext, halo_far, halo_side, halo_corner, halo_far_in, halo_side_in, halo_corner_in, more)
         fold.pack()
         greeted(place)
-        fold.start(True)
+        fold.start(False)
         halo.clear()
         inverse[...] = 1.0 / (light[128:512, 128:512] + 1.0)
         for p in range(2):

time: 76.5 us -> 76.2 us (level)
  no operation moved by 1% of the time
where the time goes in v13:
time: 76.2 us; the launch traced here: 74.9 us
  Pallas kernels  73.2 us (96%)
  local copies, waits for them, and re-layouts  1.02 us (1%)
    pallas_call x1, Pallas kernels, shards(): pl.pallas_call(between_kernel(grid), name='between', out_shape=(ext_shape...  29.7 us
    pallas_call x1, Pallas kernels, shards(): pl.pallas_call(spread_kernel(grid), name='spread', out_shape=(ext_shape,...  19.7 us
    pallas_call x1, Pallas kernels, shards(): pl.pallas_call(last_kernel(grid), name='last', out_shape=shape((2, 384, 3...  18 us
    pallas_call x1, Pallas kernels, shards(): pl.pallas_call(gradient_kernel(True), name='gradient_light', out_shape=(e...  3.24 us
    pallas_call x1, Pallas kernels, shards(): pl.pallas_call(gradient_kernel(False), name='gradient', out_shape=ext_sha...  2.61 us

profile of v13, /device:TPU:11, one launch (start us, length us, event | category | flops | bytes accessed | tf_op | source)
XLA Modules:
  0.0 74.9 jit_solution(2465245973437673760)
XLA Ops:
  0.7 19.7 %spread.1 = (f32[2,512,512]{2,1,0:T(8,128)S(1)}, s32[8,8,128]{2,1,0:T(8,128)S(1)}, f32[1,1,12,128,128]{4,3,2,1,0:T(8,128)S(1)}, bf16[4,256,256]{2,1,0:T(8,128)(2...) custom-call(f32[2,384,384]{2,1,0:T(8,128)} %field.1, ...), custom_call_target="tpu_custom_call" | custom-call | tf_op jit(solution)/shard_map/spread/pallas_call | solution.py:660
  20.3 3.2 %gradient_light.1 = (f32[2,512,512]{2,1,0:T(8,128)S(1)}, f32[648,640]{1,0:T(8,128)S(1)}) custom-call(s32[1,1,2,12]{3,2,1,0:T(2,128)S(1)} %get-tuple-element.19.refs_0_, s32[1,1]{1,0:T(1,128)S(6)} %copy.14.counts.refs_1_, s32[8,8,128]{2,1,0:T(8,128)S(1)} %get-tuple-element.20.refs_2_, ...), custom_call_target="tpu_custom_call", output_to_operand_aliasing={{0}: (7, {}), {1}: (9, {})} | custom-call | tf_op jit(solution)/shard_map/gradient_light/pallas_call | solution.py:682
  23.6 29.7 %between.1 = (f32[2,512,512]{2,1,0:T(8,128)S(1)}, f32[2,512,512]{2,1,0:T(8,128)S(1)}, f32[384,384]{1,0:T(8,128)S(1)}) custom-call(f32[2,512,512]{2,1,0:T(8,128)S(1)} %get-tuple-element.28.update, f32[648,640]{1,0:T(8,128)S(1)} %get-tuple-element.29.light, f32[2,512,512]{2,1,0:T(8,128)S(1)} %get-tuple-element.21.refs_3_.field), custom_call_target="tpu_custom_call" | custom-call | tf_op jit(solution)/shard_map/between/pallas_call | solution.py:692
  53.3 2.6 %gradient.1.update = f32[2,512,512]{2,1,0:T(8,128)S(1)} custom-call(s32[1,1,2,12]{3,2,1,0:T(2,128)S(1)} %get-tuple-element.19.refs_0_, s32[1,1]{1,0:T(1,128)S(6)} %copy.14.counts.refs_1_, f32[2,512,512]{2,1,0:T(8,128)S(1)} %get-tuple-element.30.refs_2_.ext, ...), custom_call_target="tpu_custom_call", output_to_operand_aliasing={{}: (6, {})} | custom-call | tf_op jit(solution)/shard_map/gradient/pallas_call | solution.py:701
  55.9 18.0 %last.1 = f32[2,384,384]{2,1,0:T(8,128)S(1)} custom-call(f32[2,512,512]{2,1,0:T(8,128)S(1)} %gradient.1.update, f32[384,384]{1,0:T(8,128)S(1)} %get-tuple-element.32.inverse, f32[2,512,512]{2,1,0:T(8,128)S(1)} %get-tuple-element.30.refs_2_.ext), custom_call_target="tpu_custom_call" | custom-call | tf_op jit(solution)/shard_map/last/pallas_call | solution.py:710
  73.9 1.0 %copy.15 = f32[2,384,384]{2,1,0:T(8,128)} copy(f32[2,384,384]{2,1,0:T(8,128)S(1)} %last.1) | data formatting | bytes 2359296
